TPU v7x, 256 devices: a whole 4x4x8 slice. The times are simulated.
256 devices in a mesh: gx: 8 (over y, core), gy: 16 (over x, z_hi), gz: 2 (over z_lo).
Axes of the slice: x: 4, y: 4, z: 8 (z_hi: 4, z_lo: 2; z = z_hi * 2 + z_lo), core: 2. Of those that a mesh axis runs over, the one named last changes fastest.
Arguments:
- force_u: float32 [16, 64, 32, 1024], P('gz', None, 'gy', 'gx'), may hold values from -6 to 6
- force_p: float32 [16, 16, 32, 1024], P('gz', None, 'gy', 'gx'), may hold values from -6 to 6
- cellmask: int32 [16, 32, 1024], P('gz', 'gy', 'gx'), may hold values 0 or 1
- layer_mats: int32 [16], P('gz'), may hold values from 0 to 3
- kblocks: bfloat16 [4, 7, 64, 64], replicated
- bcoup: float32 [4, 16, 64], replicated, may hold values from -0.75 to 0.75
- sinv: float32 [8, 16, 16, 16], replicated, may hold values from -0.75 to 0.75
- band_offsets: int32 [8], replicated, may hold values from -15 to 15, as said below
- spectrum: float32 [2], replicated, may hold values from 0.25 to 1.9, as said below
Outputs:
- displacement: float32 [16, 64, 32, 1024], P('gz', None, 'gy', 'gx')
- pressure: float32 [16, 16, 32, 1024], P('gz', None, 'gy', 'gx')
Inputs may be any that keep to these rules, and one draw needn't show every extreme that they name: `band_offsets`: the offsets are distinct; 0, 15 and -(15) are among them. `spectrum`: the lower bound is positive and below the upper bound.
All inputs are finite; a program needn't handle non-finite values. No bound on the sum of `cellmask` on one device may be relied on, other than what follows from the above.
Results may differ from a plain program's by a relative error of at most 0.0028.
The roundings to bfloat16 on the way count: a program that leaves them out, or rounds other values in their place, can miss the bound.
Values may be sent and summed in bfloat16 or wider, within the bound.
No kernel may reach another device: no remote copies, remote signals or barrier semaphores. Data moves between devices by JAX's collectives and lax.ppermute only.
A program may use at most 64 MiB of HBM per device.

v0:
```python
import jax
import jax.numpy as jnp
from jax import lax
from jax.sharding import PartitionSpec as P

SWEEPS = 4
OUTER = 2


HIGHEST = lax.Precision.HIGHEST


def padded_2(block, sides, width):
    for axis, dim in sides:
        count = lax.axis_size(axis)
        forward = [(i, i + 1) for i in range(count - 1)]
        backward = [(target, source) for source, target in forward]
        low = lax.ppermute(
            lax.slice_in_dim(block, block.shape[dim] - width, None, axis=dim), axis, forward
        )
        high = lax.ppermute(lax.slice_in_dim(block, 0, width, axis=dim), axis, backward)
        block = jnp.concatenate([low, block, high], axis=dim)
    return block


def select(layer_mats, table):
    count = table.shape[0]
    onehot = (layer_mats[:, None] == jnp.arange(count, dtype=jnp.int32)[None, :]).astype(
        jnp.float32
    )
    flat = table.astype(jnp.float32).reshape(count, -1)
    picked = jnp.dot(onehot, flat, precision=HIGHEST)
    return picked.reshape((layer_mats.shape[0],) + table.shape[1:])


def extend(rounded):
    return padded_2(rounded, (("gx", 3), ("gy", 2), ("gz", 0)), 1)


def stacked_apply(padded, tables):
    parts = jnp.stack(
        [
            padded[1:-1, :, 1:-1, 1:-1],
            padded[:-2, :, 1:-1, 1:-1],
            padded[2:, :, 1:-1, 1:-1],
            padded[1:-1, :, :-2, 1:-1],
            padded[1:-1, :, 2:, 1:-1],
            padded[1:-1, :, 1:-1, :-2],
            padded[1:-1, :, 1:-1, 2:],
        ],
        axis=1,
    )
    return jnp.einsum("zdij,zdjyx->ziyx", tables, parts, preferred_element_type=jnp.float32)


def stencil(field, tables, weight):
    rounded = field.astype(jnp.bfloat16)
    result = stacked_apply(extend(rounded), tables)
    return result * weight[:, None]


def couple(field, coupling, weight):
    return jnp.einsum("zpj,zjyx->zpyx", coupling, field, precision=HIGHEST) * weight[:, None]


def couple_back(field, coupling, weight):
    return jnp.einsum("zpj,zpyx->zjyx", coupling, field, precision=HIGHEST) * weight[:, None]


def band_rows(pencil, sinv, band_offsets):
    depth = pencil.shape[0]
    padded = jnp.pad(pencil, ((depth, depth), (0, 0), (0, 0), (0, 0)))
    total = jnp.zeros(pencil.shape, jnp.float32)
    for band in range(band_offsets.shape[0]):
        begin = band_offsets[band] + depth
        shifted = lax.dynamic_slice_in_dim(padded, begin, depth, 0)
        total = total + jnp.einsum("zab,zbyx->zayx", sinv[band], shifted, precision=HIGHEST)
    return total


def schur(field, sinv, band_offsets, weight):
    columns = band_rows(
        lax.all_to_all(field, "gz", split_axis=2, concat_axis=0, tiled=True), sinv, band_offsets
    )
    result = lax.all_to_all(columns, "gz", split_axis=0, concat_axis=2, tiled=True)
    return result * weight[:, None]


def chebyshev(residue, apply_op, spectrum):
    lower, upper = (spectrum[0], spectrum[1])
    theta = (upper + lower) / 2.0
    delta = (upper - lower) / 2.0
    sigma = theta / delta
    rho = 1.0 / sigma
    direction = residue / theta
    solution = jnp.zeros_like(residue)
    for sweep in range(SWEEPS):
        solution = solution + direction
        if sweep + 1 < SWEEPS:
            residue = residue - apply_op(direction)
            rho_next = 1.0 / (2.0 * sigma - rho)
            direction = rho_next * rho * direction + 2.0 * rho_next / delta * residue
            rho = rho_next
    return solution


def body(force_u, force_p, cellmask, layer_mats, kblocks, bcoup, sinv, band_offsets, spectrum):
    weight = cellmask.astype(jnp.float32)
    tables = select(layer_mats, kblocks).astype(jnp.bfloat16)
    coupling = select(layer_mats, bcoup)
    force_disp = force_u * weight[:, None]
    force_pres = force_p * weight[:, None]

    def apply_op(field):
        return stencil(field, tables, weight)

    displacement = jnp.zeros_like(force_disp)
    pressure = jnp.zeros_like(force_pres)
    for outer in range(OUTER):
        if outer == 0:
            res_disp = force_disp
            res_pres = force_pres
        else:
            res_disp = force_disp - apply_op(displacement) - couple_back(pressure, coupling, weight)
            res_pres = force_pres - couple(displacement, coupling, weight)
        step_disp = chebyshev(res_disp, apply_op, spectrum)
        step_pres = schur(
            couple(step_disp, coupling, weight) - res_pres, sinv, band_offsets, weight
        )
        displacement = displacement + step_disp
        pressure = pressure + step_pres
    return (displacement, pressure)


def solution(mesh):
    in_specs = (
        P("gz", None, "gy", "gx"),
        P("gz", None, "gy", "gx"),
        P("gz", "gy", "gx"),
        P("gz"),
        P(),
        P(),
        P(),
        P(),
        P(),
    )
    out_specs = (P("gz", None, "gy", "gx"), P("gz", None, "gy", "gx"))
    return jax.shard_map(body, mesh=mesh, in_specs=in_specs, out_specs=out_specs, check_vma=False)
```

profile of v0, /device:TPU:16, one launch (start us, length us, event | category | flops | bytes accessed | tf_op | source)
XLA Modules:
  0.0 344.9 jit_solution(15322508219982196883)
XLA Ops:
  7.9 3.6 %collective-permute-start.1 = (bf16[8,64,2,1]{3,1,2,0:T(8,128)(2,1)S(1)}, bf16[8,64,2,1]{3,1,2,0:T(8,128)(2,1)S(1)}, u32[]{:S(2)}, u32[]{:S(2)}) collective-permute-start(bf16[8,64,2,1]{3,1,2,0:T(8,128)(2,1)S(1)} %get-tuple-element.63), channel_id=1, source_target_pairs={{32,0},{64,32},{96,64},{128,96},{160,128},{192,160},{224,192},{33,... | collective-permute-start | bytes 6152 | tf_op jit(solution)/shard_map/ppermute | solution.py:21
  15.8 5.2 %collective-permute-start.2 = (bf16[8,64,1,130]{3,1,2,0:T(8,128)(2,1)S(1)}, bf16[8,64,1,130]{3,1,2,0:T(8,128)(2,1)S(1)}, u32[]{:S(2)}, u32[]{:S(2)}) collective-permute-start(bf16[8,64,1,130]{3,1,2,0:T(8,128)(2,1)S(1)} %get-tuple-element.48), channel_id=1, source_target_pairs={{0,2},{2,4},{4,6},{6,8},{8,10},{10,12},{12,14},{14,16},{16,18},{18... | collective-permute-start | bytes 399368 | tf_op jit(solution)/shard_map/ppermute | solution.py:18
  23.0 5.1 %collective-permute-done.2 = bf16[8,64,1,130]{3,1,2,0:T(8,128)(2,1)S(1)} collective-permute-done((bf16[8,64,1,130]{3,1,2,0:T(8,128)(2,1)S(1)}, bf16[8,64,1,130]{3,1,2,0:T(8,128)(2,1)S(1)}, u32[]{:S(2)}, u32[]{:S(2)}) %collective-permute-start.2) | collective-permute-done | bytes 133152 | tf_op jit(solution)/shard_map/ppermute | solution.py:18
  28.1 11.4 %collective-permute-done.3 = bf16[8,64,1,130]{3,1,2,0:T(8,128)(2,1)S(1)} collective-permute-done((bf16[8,64,1,130]{3,1,2,0:T(8,128)(2,1)S(1)}, bf16[8,64,1,130]{3,1,2,0:T(8,128)(2,1)S(1)}, u32[]{:S(2)}, u32[]{:S(2)}) %collective-permute-start.3) | collective-permute-done | bytes 133152 | tf_op jit(solution)/shard_map/ppermute | solution.py:21
  45.4 5.3 %collective-permute-done.5 = bf16[1,64,4,130]{3,1,2,0:T(8,128)(2,1)S(1)} collective-permute-done((bf16[1,64,4,130]{3,1,2,0:T(8,128)(2,1)S(1)}, bf16[1,64,4,130]{3,1,2,0:T(8,128)(2,1)S(1)}, u32[]{:S(2)}, u32[]{:S(2)}) %collective-permute-start.5) | collective-permute-done | bytes 66592 | tf_op jit(solution)/shard_map/ppermute | solution.py:21
  60.0 3.6 %collective-permute-start.7 = (bf16[8,64,2,1]{3,1,2,0:T(8,128)(2,1)S(1)}, bf16[8,64,2,1]{3,1,2,0:T(8,128)(2,1)S(1)}, u32[]{:S(2)}, u32[]{:S(2)}) collective-permute-start(bf16[8,64,2,1]{3,1,2,0:T(8,128)(2,1)S(1)} %get-tuple-element.61), channel_id=1, source_target_pairs={{32,0},{64,32},{96,64},{128,96},{160,128},{192,160},{224,192},{33,... | collective-permute-start | bytes 6152 | tf_op jit(solution)/shard_map/ppermute | solution.py:21
  67.9 6.5 %collective-permute-start.8 = (bf16[8,64,1,130]{3,1,2,0:T(8,128)(2,1)S(1)}, bf16[8,64,1,130]{3,1,2,0:T(8,128)(2,1)S(1)}, u32[]{:S(2)}, u32[]{:S(2)}) collective-permute-start(bf16[8,64,1,130]{3,1,2,0:T(8,128)(2,1)S(1)} %get-tuple-element.46), channel_id=1, source_target_pairs={{0,2},{2,4},{4,6},{6,8},{8,10},{10,12},{12,14},{14,16},{16,18},{18... | collective-permute-start | bytes 399368 | tf_op jit(solution)/shard_map/ppermute | solution.py:18
  75.7 7.8 %collective-permute-done.8 = bf16[8,64,1,130]{3,1,2,0:T(8,128)(2,1)S(1)} collective-permute-done((bf16[8,64,1,130]{3,1,2,0:T(8,128)(2,1)S(1)}, bf16[8,64,1,130]{3,1,2,0:T(8,128)(2,1)S(1)}, u32[]{:S(2)}, u32[]{:S(2)}) %collective-permute-start.8) | collective-permute-done | bytes 133152 | tf_op jit(solution)/shard_map/ppermute | solution.py:18
  83.5 6.7 %collective-permute-done.9 = bf16[8,64,1,130]{3,1,2,0:T(8,128)(2,1)S(1)} collective-permute-done((bf16[8,64,1,130]{3,1,2,0:T(8,128)(2,1)S(1)}, bf16[8,64,1,130]{3,1,2,0:T(8,128)(2,1)S(1)}, u32[]{:S(2)}, u32[]{:S(2)}) %collective-permute-start.9) | collective-permute-done | bytes 133152 | tf_op jit(solution)/shard_map/ppermute | solution.py:21
  108.5 3.6 %collective-permute-start.13 = (bf16[8,64,2,1]{3,1,2,0:T(8,128)(2,1)S(1)}, bf16[8,64,2,1]{3,1,2,0:T(8,128)(2,1)S(1)}, u32[]{:S(2)}, u32[]{:S(2)}) collective-permute-start(bf16[8,64,2,1]{3,1,2,0:T(8,128)(2,1)S(1)} %get-tuple-element.59), channel_id=1, source_target_pairs={{32,0},{64,32},{96,64},{128,96},{160,128},{192,160},{224,192},{33,... | collective-permute-start | bytes 6152 | tf_op jit(solution)/shard_map/ppermute | solution.py:21
  116.4 4.2 %collective-permute-start.14 = (bf16[8,64,1,130]{3,1,2,0:T(8,128)(2,1)S(1)}, bf16[8,64,1,130]{3,1,2,0:T(8,128)(2,1)S(1)}, u32[]{:S(2)}, u32[]{:S(2)}) collective-permute-start(bf16[8,64,1,130]{3,1,2,0:T(8,128)(2,1)S(1)} %get-tuple-element.44), channel_id=1, source_target_pairs={{0,2},{2,4},{4,6},{6,8},{8,10},{10,12},{12,14},{14,16},{16,18},{18... | collective-permute-start | bytes 399368 | tf_op jit(solution)/shard_map/ppermute | solution.py:18
  140.1 3.5 %collective-permute-done.17 = bf16[1,64,4,130]{3,1,2,0:T(8,128)(2,1)S(1)} collective-permute-done((bf16[1,64,4,130]{3,1,2,0:T(8,128)(2,1)S(1)}, bf16[1,64,4,130]{3,1,2,0:T(8,128)(2,1)S(1)}, u32[]{:S(2)}, u32[]{:S(2)}) %collective-permute-start.17) | collective-permute-done | bytes 66592 | tf_op jit(solution)/shard_map/ppermute | solution.py:21
  152.9 3.6 %collective-permute-start.19 = (bf16[8,64,2,1]{3,1,2,0:T(8,128)(2,1)S(1)}, bf16[8,64,2,1]{3,1,2,0:T(8,128)(2,1)S(1)}, u32[]{:S(2)}, u32[]{:S(2)}) collective-permute-start(bf16[8,64,2,1]{3,1,2,0:T(8,128)(2,1)S(1)} %get-tuple-element.57), channel_id=1, source_target_pairs={{32,0},{64,32},{96,64},{128,96},{160,128},{192,160},{224,192},{33,... | collective-permute-start | bytes 6152 | tf_op jit(solution)/shard_map/ppermute | solution.py:21
  162.9 3.7 %collective-permute-start.20 = (bf16[8,64,1,130]{3,1,2,0:T(8,128)(2,1)}, bf16[8,64,1,130]{3,1,2,0:T(8,128)(2,1)S(1)}, u32[]{:S(2)}, u32[]{:S(2)}) collective-permute-start(bf16[8,64,1,130]{3,1,2,0:T(8,128)(2,1)} %get-tuple-element.42), channel_id=1, source_target_pairs={{0,2},{2,4},{4,6},{6,8},{8,10},{10,12},{12,14},{14,16},{16,18},{18... | collective-permute-start | bytes 399368 | tf_op jit(solution)/shard_map/ppermute | solution.py:18
  171.3 10.4 %collective-permute-done.21 = bf16[8,64,1,130]{3,1,2,0:T(8,128)(2,1)S(1)} collective-permute-done((bf16[8,64,1,130]{3,1,2,0:T(8,128)(2,1)}, bf16[8,64,1,130]{3,1,2,0:T(8,128)(2,1)S(1)}, u32[]{:S(2)}, u32[]{:S(2)}) %collective-permute-start.21) | collective-permute-done | bytes 133152 | tf_op jit(solution)/shard_map/ppermute | solution.py:21
  191.7 4.1 %collective-permute-done.23 = bf16[1,64,4,130]{3,1,2,0:T(8,128)(2,1)S(1)} collective-permute-done((bf16[1,64,4,130]{3,1,2,0:T(8,128)(2,1)}, bf16[1,64,4,130]{3,1,2,0:T(8,128)(2,1)S(1)}, u32[]{:S(2)}, u32[]{:S(2)}) %collective-permute-start.23) | collective-permute-done | bytes 66592 | tf_op jit(solution)/shard_map/ppermute | solution.py:21
  205.0 3.6 %collective-permute-start.25 = (bf16[8,64,2,1]{3,1,2,0:T(8,128)(2,1)S(1)}, bf16[8,64,2,1]{3,1,2,0:T(8,128)(2,1)S(1)}, u32[]{:S(2)}, u32[]{:S(2)}) collective-permute-start(bf16[8,64,2,1]{3,1,2,0:T(8,128)(2,1)S(1)} %get-tuple-element.55), channel_id=1, source_target_pairs={{32,0},{64,32},{96,64},{128,96},{160,128},{192,160},{224,192},{33,... | collective-permute-start | bytes 6152 | tf_op jit(solution)/shard_map/ppermute | solution.py:21
  212.9 7.1 %collective-permute-start.26 = (bf16[8,64,1,130]{3,1,2,0:T(8,128)(2,1)S(1)}, bf16[8,64,1,130]{3,1,2,0:T(8,128)(2,1)S(1)}, u32[]{:S(2)}, u32[]{:S(2)}) collective-permute-start(bf16[8,64,1,130]{3,1,2,0:T(8,128)(2,1)S(1)} %get-tuple-element.40), channel_id=1, source_target_pairs={{0,2},{2,4},{4,6},{6,8},{8,10},{10,12},{12,14},{14,16},{16,18},{18... | collective-permute-start | bytes 399368 | tf_op jit(solution)/shard_map/ppermute | solution.py:18
  221.3 8.6 %collective-permute-done.26 = bf16[8,64,1,130]{3,1,2,0:T(8,128)(2,1)S(1)} collective-permute-done((bf16[8,64,1,130]{3,1,2,0:T(8,128)(2,1)S(1)}, bf16[8,64,1,130]{3,1,2,0:T(8,128)(2,1)S(1)}, u32[]{:S(2)}, u32[]{:S(2)}) %collective-permute-start.26) | collective-permute-done | bytes 133152 | tf_op jit(solution)/shard_map/ppermute | solution.py:18
  229.9 4.4 %collective-permute-done.27 = bf16[8,64,1,130]{3,1,2,0:T(8,128)(2,1)S(1)} collective-permute-done((bf16[8,64,1,130]{3,1,2,0:T(8,128)(2,1)S(1)}, bf16[8,64,1,130]{3,1,2,0:T(8,128)(2,1)S(1)}, u32[]{:S(2)}, u32[]{:S(2)}) %collective-permute-start.27) | collective-permute-done | bytes 133152 | tf_op jit(solution)/shard_map/ppermute | solution.py:21
  239.2 3.9 %collective-permute-done.29 = bf16[1,64,4,130]{3,1,2,0:T(8,128)(2,1)S(1)} collective-permute-done((bf16[1,64,4,130]{3,1,2,0:T(8,128)(2,1)S(1)}, bf16[1,64,4,130]{3,1,2,0:T(8,128)(2,1)S(1)}, u32[]{:S(2)}, u32[]{:S(2)}) %collective-permute-start.29) | collective-permute-done | bytes 66592 | tf_op jit(solution)/shard_map/ppermute | solution.py:21
  246.7 4.1 %collective-permute-start.31 = (bf16[8,64,2,1]{3,1,2,0:T(8,128)(2,1)S(1)}, bf16[8,64,2,1]{3,1,2,0:T(8,128)(2,1)S(1)}, u32[]{:S(2)}, u32[]{:S(2)}) collective-permute-start(bf16[8,64,2,1]{3,1,2,0:T(8,128)(2,1)S(1)} %get-tuple-element.53), channel_id=1, source_target_pairs={{32,0},{64,32},{96,64},{128,96},{160,128},{192,160},{224,192},{33,... | collective-permute-start | bytes 6152 | tf_op jit(solution)/shard_map/ppermute | solution.py:21
  255.1 5.8 %collective-permute-start.32 = (bf16[8,64,1,130]{3,1,2,0:T(8,128)(2,1)S(1)}, bf16[8,64,1,130]{3,1,2,0:T(8,128)(2,1)S(1)}, u32[]{:S(2)}, u32[]{:S(2)}) collective-permute-start(bf16[8,64,1,130]{3,1,2,0:T(8,128)(2,1)S(1)} %get-tuple-element.38), channel_id=1, source_target_pairs={{0,2},{2,4},{4,6},{6,8},{8,10},{10,12},{12,14},{14,16},{16,18},{18... | collective-permute-start | bytes 399368 | tf_op jit(solution)/shard_map/ppermute | solution.py:18
  262.2 8.9 %collective-permute-done.32 = bf16[8,64,1,130]{3,1,2,0:T(8,128)(2,1)S(1)} collective-permute-done((bf16[8,64,1,130]{3,1,2,0:T(8,128)(2,1)S(1)}, bf16[8,64,1,130]{3,1,2,0:T(8,128)(2,1)S(1)}, u32[]{:S(2)}, u32[]{:S(2)}) %collective-permute-start.32) | collective-permute-done | bytes 133152 | tf_op jit(solution)/shard_map/ppermute | solution.py:18
  271.1 4.0 %collective-permute-done.33 = bf16[8,64,1,130]{3,1,2,0:T(8,128)(2,1)S(1)} collective-permute-done((bf16[8,64,1,130]{3,1,2,0:T(8,128)(2,1)S(1)}, bf16[8,64,1,130]{3,1,2,0:T(8,128)(2,1)S(1)}, u32[]{:S(2)}, u32[]{:S(2)}) %collective-permute-start.33) | collective-permute-done | bytes 133152 | tf_op jit(solution)/shard_map/ppermute | solution.py:21
  279.9 3.9 %collective-permute-done.35 = bf16[1,64,4,130]{3,1,2,0:T(8,128)(2,1)S(1)} collective-permute-done((bf16[1,64,4,130]{3,1,2,0:T(8,128)(2,1)S(1)}, bf16[1,64,4,130]{3,1,2,0:T(8,128)(2,1)S(1)}, u32[]{:S(2)}, u32[]{:S(2)}) %collective-permute-start.35) | collective-permute-done | bytes 66592 | tf_op jit(solution)/shard_map/ppermute | solution.py:21
  287.5 4.1 %collective-permute-start.37 = (bf16[8,64,2,1]{3,1,2,0:T(8,128)(2,1)S(1)}, bf16[8,64,2,1]{3,1,2,0:T(8,128)(2,1)S(1)}, u32[]{:S(2)}, u32[]{:S(2)}) collective-permute-start(bf16[8,64,2,1]{3,1,2,0:T(8,128)(2,1)S(1)} %get-tuple-element.51), channel_id=1, source_target_pairs={{32,0},{64,32},{96,64},{128,96},{160,128},{192,160},{224,192},{33,... | collective-permute-start | bytes 6152 | tf_op jit(solution)/shard_map/ppermute | solution.py:21
  295.9 5.3 %collective-permute-start.38 = (bf16[8,64,1,130]{3,1,2,0:T(8,128)(2,1)S(1)}, bf16[8,64,1,130]{3,1,2,0:T(8,128)(2,1)S(1)}, u32[]{:S(2)}, u32[]{:S(2)}) collective-permute-start(bf16[8,64,1,130]{3,1,2,0:T(8,128)(2,1)S(1)} %get-tuple-element.36), channel_id=1, source_target_pairs={{0,2},{2,4},{4,6},{6,8},{8,10},{10,12},{12,14},{14,16},{16,18},{18... | collective-permute-start | bytes 399368 | tf_op jit(solution)/shard_map/ppermute | solution.py:18
  302.5 8.7 %collective-permute-done.38 = bf16[8,64,1,130]{3,1,2,0:T(8,128)(2,1)S(1)} collective-permute-done((bf16[8,64,1,130]{3,1,2,0:T(8,128)(2,1)S(1)}, bf16[8,64,1,130]{3,1,2,0:T(8,128)(2,1)S(1)}, u32[]{:S(2)}, u32[]{:S(2)}) %collective-permute-start.38) | collective-permute-done | bytes 133152 | tf_op jit(solution)/shard_map/ppermute | solution.py:18
  311.3 4.0 %collective-permute-done.39 = bf16[8,64,1,130]{3,1,2,0:T(8,128)(2,1)S(1)} collective-permute-done((bf16[8,64,1,130]{3,1,2,0:T(8,128)(2,1)S(1)}, bf16[8,64,1,130]{3,1,2,0:T(8,128)(2,1)S(1)}, u32[]{:S(2)}, u32[]{:S(2)}) %collective-permute-start.39) | collective-permute-done | bytes 133152 | tf_op jit(solution)/shard_map/ppermute | solution.py:21
  320.1 3.9 %collective-permute-done.41 = bf16[1,64,4,130]{3,1,2,0:T(8,128)(2,1)S(1)} collective-permute-done((bf16[1,64,4,130]{3,1,2,0:T(8,128)(2,1)S(1)}, bf16[1,64,4,130]{3,1,2,0:T(8,128)(2,1)S(1)}, u32[]{:S(2)}, u32[]{:S(2)}) %collective-permute-start.41) | collective-permute-done | bytes 66592 | tf_op jit(solution)/shard_map/ppermute | solution.py:21
  326.6 6.8 %all_to_all.72 = f32[8,16,2,128]{3,1,0,2:T(8,128)S(1)} all-to-all(f32[8,16,2,128]{3,1,0,2:T(8,128)S(1)} %copy.98), channel_id=1, replica_groups=mesh['gx'=8,'gy'=16,'gz'=2] {'gz'}, dimensions={2} | all-to-all | bytes 262144 | tf_op jit(solution)/shard_map/all_to_all | solution.py:83
  (200 shorter events, 154.6 us)
Async XLA Ops:
  5.9 7.7 %collective-permute-start = (bf16[8,64,2,1]{3,1,2,0:T(8,128)(2,1)S(1)}, bf16[8,64,2,1]{3,1,2,0:T(8,128)(2,1)S(1)}, u32[]{:S(2)}, u32[]{:S(2)}) collective-permute-start(bf16[8,64,2,1]{3,1,2,0:T(8,128)(2,1)S(1)} %get-tuple-element.62), channel_id=1, source_target_pairs={{0,32},{32,64},{64,96},{96,128},{128,160},{160,192},{192,224},{1,3... | collective-permute-start | bytes 6152 | tf_op jit(solution)/shard_map/ppermute | solution.py:18
  7.9 7.5 %collective-permute-start.1 = (bf16[8,64,2,1]{3,1,2,0:T(8,128)(2,1)S(1)}, bf16[8,64,2,1]{3,1,2,0:T(8,128)(2,1)S(1)}, u32[]{:S(2)}, u32[]{:S(2)}) collective-permute-start(bf16[8,64,2,1]{3,1,2,0:T(8,128)(2,1)S(1)} %get-tuple-element.63), channel_id=1, source_target_pairs={{32,0},{64,32},{96,64},{128,96},{160,128},{192,160},{224,192},{33,... | collective-permute-start | bytes 6152 | tf_op jit(solution)/shard_map/ppermute | solution.py:21
  15.8 12.4 %collective-permute-start.2 = (bf16[8,64,1,130]{3,1,2,0:T(8,128)(2,1)S(1)}, bf16[8,64,1,130]{3,1,2,0:T(8,128)(2,1)S(1)}, u32[]{:S(2)}, u32[]{:S(2)}) collective-permute-start(bf16[8,64,1,130]{3,1,2,0:T(8,128)(2,1)S(1)} %get-tuple-element.48), channel_id=1, source_target_pairs={{0,2},{2,4},{4,6},{6,8},{8,10},{10,12},{12,14},{14,16},{16,18},{18... | collective-permute-start | bytes 399368 | tf_op jit(solution)/shard_map/ppermute | solution.py:18
  21.0 18.6 %collective-permute-start.3 = (bf16[8,64,1,130]{3,1,2,0:T(8,128)(2,1)S(1)}, bf16[8,64,1,130]{3,1,2,0:T(8,128)(2,1)S(1)}, u32[]{:S(2)}, u32[]{:S(2)}) collective-permute-start(bf16[8,64,1,130]{3,1,2,0:T(8,128)(2,1)S(1)} %get-tuple-element.49), channel_id=1, source_target_pairs={{2,0},{4,2},{6,4},{8,6},{10,8},{12,10},{14,12},{16,14},{18,16},{20... | collective-permute-start | bytes 399368 | tf_op jit(solution)/shard_map/ppermute | solution.py:21
  43.0 7.7 %collective-permute-start.5 = (bf16[1,64,4,130]{3,1,2,0:T(8,128)(2,1)S(1)}, bf16[1,64,4,130]{3,1,2,0:T(8,128)(2,1)S(1)}, u32[]{:S(2)}, u32[]{:S(2)}) collective-permute-start(bf16[1,64,4,130]{3,1,2,0:T(8,128)(2,1)S(1)} %get-tuple-element.34), channel_id=1, source_target_pairs={{1,0},{3,2},{5,4},{7,6},{9,8},{11,10},{13,12},{15,14},{17,16},{19,... | collective-permute-start | bytes 199688 | tf_op jit(solution)/shard_map/ppermute | solution.py:21
  58.1 7.7 %collective-permute-start.6 = (bf16[8,64,2,1]{3,1,2,0:T(8,128)(2,1)S(1)}, bf16[8,64,2,1]{3,1,2,0:T(8,128)(2,1)S(1)}, u32[]{:S(2)}, u32[]{:S(2)}) collective-permute-start(bf16[8,64,2,1]{3,1,2,0:T(8,128)(2,1)S(1)} %get-tuple-element.60), channel_id=1, source_target_pairs={{0,32},{32,64},{64,96},{96,128},{128,160},{160,192},{192,224},{1,3... | collective-permute-start | bytes 6152 | tf_op jit(solution)/shard_map/ppermute | solution.py:18
  60.0 7.5 %collective-permute-start.7 = (bf16[8,64,2,1]{3,1,2,0:T(8,128)(2,1)S(1)}, bf16[8,64,2,1]{3,1,2,0:T(8,128)(2,1)S(1)}, u32[]{:S(2)}, u32[]{:S(2)}) collective-permute-start(bf16[8,64,2,1]{3,1,2,0:T(8,128)(2,1)S(1)} %get-tuple-element.61), channel_id=1, source_target_pairs={{32,0},{64,32},{96,64},{128,96},{160,128},{192,160},{224,192},{33,... | collective-permute-start | bytes 6152 | tf_op jit(solution)/shard_map/ppermute | solution.py:21
  67.9 15.6 %collective-permute-start.8 = (bf16[8,64,1,130]{3,1,2,0:T(8,128)(2,1)S(1)}, bf16[8,64,1,130]{3,1,2,0:T(8,128)(2,1)S(1)}, u32[]{:S(2)}, u32[]{:S(2)}) collective-permute-start(bf16[8,64,1,130]{3,1,2,0:T(8,128)(2,1)S(1)} %get-tuple-element.46), channel_id=1, source_target_pairs={{0,2},{2,4},{4,6},{6,8},{8,10},{10,12},{12,14},{14,16},{16,18},{18... | collective-permute-start | bytes 399368 | tf_op jit(solution)/shard_map/ppermute | solution.py:18
  74.4 15.8 %collective-permute-start.9 = (bf16[8,64,1,130]{3,1,2,0:T(8,128)(2,1)S(1)}, bf16[8,64,1,130]{3,1,2,0:T(8,128)(2,1)S(1)}, u32[]{:S(2)}, u32[]{:S(2)}) collective-permute-start(bf16[8,64,1,130]{3,1,2,0:T(8,128)(2,1)S(1)} %get-tuple-element.47), channel_id=1, source_target_pairs={{2,0},{4,2},{6,4},{8,6},{10,8},{12,10},{14,12},{16,14},{18,16},{20... | collective-permute-start | bytes 399368 | tf_op jit(solution)/shard_map/ppermute | solution.py:21
  106.6 7.7 %collective-permute-start.12 = (bf16[8,64,2,1]{3,1,2,0:T(8,128)(2,1)S(1)}, bf16[8,64,2,1]{3,1,2,0:T(8,128)(2,1)S(1)}, u32[]{:S(2)}, u32[]{:S(2)}) collective-permute-start(bf16[8,64,2,1]{3,1,2,0:T(8,128)(2,1)S(1)} %get-tuple-element.58), channel_id=1, source_target_pairs={{0,32},{32,64},{64,96},{96,128},{128,160},{160,192},{192,224},{1,3... | collective-permute-start | bytes 6152 | tf_op jit(solution)/shard_map/ppermute | solution.py:18
  108.5 7.5 %collective-permute-start.13 = (bf16[8,64,2,1]{3,1,2,0:T(8,128)(2,1)S(1)}, bf16[8,64,2,1]{3,1,2,0:T(8,128)(2,1)S(1)}, u32[]{:S(2)}, u32[]{:S(2)}) collective-permute-start(bf16[8,64,2,1]{3,1,2,0:T(8,128)(2,1)S(1)} %get-tuple-element.59), channel_id=1, source_target_pairs={{32,0},{64,32},{96,64},{128,96},{160,128},{192,160},{224,192},{33,... | collective-permute-start | bytes 6152 | tf_op jit(solution)/shard_map/ppermute | solution.py:21
  116.4 16.4 %collective-permute-start.14 = (bf16[8,64,1,130]{3,1,2,0:T(8,128)(2,1)S(1)}, bf16[8,64,1,130]{3,1,2,0:T(8,128)(2,1)S(1)}, u32[]{:S(2)}, u32[]{:S(2)}) collective-permute-start(bf16[8,64,1,130]{3,1,2,0:T(8,128)(2,1)S(1)} %get-tuple-element.44), channel_id=1, source_target_pairs={{0,2},{2,4},{4,6},{6,8},{8,10},{10,12},{12,14},{14,16},{16,18},{18... | collective-permute-start | bytes 399368 | tf_op jit(solution)/shard_map/ppermute | solution.py:18
  120.6 14.0 %collective-permute-start.15 = (bf16[8,64,1,130]{3,1,2,0:T(8,128)(2,1)S(1)}, bf16[8,64,1,130]{3,1,2,0:T(8,128)(2,1)S(1)}, u32[]{:S(2)}, u32[]{:S(2)}) collective-permute-start(bf16[8,64,1,130]{3,1,2,0:T(8,128)(2,1)S(1)} %get-tuple-element.45), channel_id=1, source_target_pairs={{2,0},{4,2},{6,4},{8,6},{10,8},{12,10},{14,12},{16,14},{18,16},{20... | collective-permute-start | bytes 399368 | tf_op jit(solution)/shard_map/ppermute | solution.py:21
  151.0 10.7 %collective-permute-start.18 = (bf16[8,64,2,1]{3,1,2,0:T(8,128)(2,1)S(1)}, bf16[8,64,2,1]{3,1,2,0:T(8,128)(2,1)S(1)}, u32[]{:S(2)}, u32[]{:S(2)}) collective-permute-start(bf16[8,64,2,1]{3,1,2,0:T(8,128)(2,1)S(1)} %get-tuple-element.56), channel_id=1, source_target_pairs={{0,32},{32,64},{64,96},{96,128},{128,160},{160,192},{192,224},{1,3... | collective-permute-start | bytes 6152 | tf_op jit(solution)/shard_map/ppermute | solution.py:18
  152.9 8.8 %collective-permute-start.19 = (bf16[8,64,2,1]{3,1,2,0:T(8,128)(2,1)S(1)}, bf16[8,64,2,1]{3,1,2,0:T(8,128)(2,1)S(1)}, u32[]{:S(2)}, u32[]{:S(2)}) collective-permute-start(bf16[8,64,2,1]{3,1,2,0:T(8,128)(2,1)S(1)} %get-tuple-element.57), channel_id=1, source_target_pairs={{32,0},{64,32},{96,64},{128,96},{160,128},{192,160},{224,192},{33,... | collective-permute-start | bytes 6152 | tf_op jit(solution)/shard_map/ppermute | solution.py:21
  158.3 9.8 %all-to-all-start = ((f32[8,16,2,128]{3,1,0,2:T(8,128)}), f32[8,16,2,128]{3,1,0,2:T(8,128)S(1)}, u32[]{:S(2)}, u32[]{:S(2)}) async-start(f32[8,16,2,128]{3,1,0,2:T(8,128)} %copy.87), calls=%async_computation | async-start | bytes 262144 | tf_op jit(solution)/shard_map/all_to_all | solution.py:83
  162.9 8.3 %collective-permute-start.20 = (bf16[8,64,1,130]{3,1,2,0:T(8,128)(2,1)}, bf16[8,64,1,130]{3,1,2,0:T(8,128)(2,1)S(1)}, u32[]{:S(2)}, u32[]{:S(2)}) collective-permute-start(bf16[8,64,1,130]{3,1,2,0:T(8,128)(2,1)} %get-tuple-element.42), channel_id=1, source_target_pairs={{0,2},{2,4},{4,6},{6,8},{8,10},{10,12},{12,14},{14,16},{16,18},{18... | collective-permute-start | bytes 399368 | tf_op jit(solution)/shard_map/ppermute | solution.py:18
  166.6 15.1 %collective-permute-start.21 = (bf16[8,64,1,130]{3,1,2,0:T(8,128)(2,1)}, bf16[8,64,1,130]{3,1,2,0:T(8,128)(2,1)S(1)}, u32[]{:S(2)}, u32[]{:S(2)}) collective-permute-start(bf16[8,64,1,130]{3,1,2,0:T(8,128)(2,1)} %get-tuple-element.43), channel_id=1, source_target_pairs={{2,0},{4,2},{6,4},{8,6},{10,8},{12,10},{14,12},{16,14},{18,16},{20... | collective-permute-start | bytes 399368 | tf_op jit(solution)/shard_map/ppermute | solution.py:21
  182.5 7.5 %collective-permute-start.22 = (bf16[1,64,4,130]{3,1,2,0:T(8,128)(2,1)}, bf16[1,64,4,130]{3,1,2,0:T(8,128)(2,1)}, u32[]{:S(2)}, u32[]{:S(2)}) collective-permute-start(bf16[1,64,4,130]{3,1,2,0:T(8,128)(2,1)} %get-tuple-element.29), channel_id=1, source_target_pairs={{0,1},{2,3},{4,5},{6,7},{8,9},{10,11},{12,13},{14,15},{16,17},{18,... | collective-permute-start | bytes 199688 | tf_op jit(solution)/shard_map/ppermute | solution.py:18
  185.3 16.8 %all-to-all-start.1 = ((f32[16,16,1,128]{3,1,2,0:T(8,128)}), f32[16,16,1,128]{3,1,2,0:T(8,128)S(1)}, u32[]{:S(2)}, u32[]{:S(2)}) async-start(f32[16,16,1,128]{3,1,2,0:T(8,128)} %fusion.90), calls=%async_computation.1 | async-start | bytes 262144 | tf_op jit(solution)/shard_map/all_to_all | solution.py:85
  203.0 7.7 %collective-permute-start.24 = (bf16[8,64,2,1]{3,1,2,0:T(8,128)(2,1)S(1)}, bf16[8,64,2,1]{3,1,2,0:T(8,128)(2,1)S(1)}, u32[]{:S(2)}, u32[]{:S(2)}) collective-permute-start(bf16[8,64,2,1]{3,1,2,0:T(8,128)(2,1)S(1)} %get-tuple-element.54), channel_id=1, source_target_pairs={{0,32},{32,64},{64,96},{96,128},{128,160},{160,192},{192,224},{1,3... | collective-permute-start | bytes 6152 | tf_op jit(solution)/shard_map/ppermute | solution.py:18
  212.9 17.0 %collective-permute-start.26 = (bf16[8,64,1,130]{3,1,2,0:T(8,128)(2,1)S(1)}, bf16[8,64,1,130]{3,1,2,0:T(8,128)(2,1)S(1)}, u32[]{:S(2)}, u32[]{:S(2)}) collective-permute-start(bf16[8,64,1,130]{3,1,2,0:T(8,128)(2,1)S(1)} %get-tuple-element.40), channel_id=1, source_target_pairs={{0,2},{2,4},{4,6},{6,8},{8,10},{10,12},{12,14},{14,16},{16,18},{18... | collective-permute-start | bytes 399368 | tf_op jit(solution)/shard_map/ppermute | solution.py:18
  220.0 14.4 %collective-permute-start.27 = (bf16[8,64,1,130]{3,1,2,0:T(8,128)(2,1)S(1)}, bf16[8,64,1,130]{3,1,2,0:T(8,128)(2,1)S(1)}, u32[]{:S(2)}, u32[]{:S(2)}) collective-permute-start(bf16[8,64,1,130]{3,1,2,0:T(8,128)(2,1)S(1)} %get-tuple-element.41), channel_id=1, source_target_pairs={{2,0},{4,2},{6,4},{8,6},{10,8},{12,10},{14,12},{16,14},{18,16},{20... | collective-permute-start | bytes 399368 | tf_op jit(solution)/shard_map/ppermute | solution.py:21
  244.8 8.1 %collective-permute-start.30 = (bf16[8,64,2,1]{3,1,2,0:T(8,128)(2,1)S(1)}, bf16[8,64,2,1]{3,1,2,0:T(8,128)(2,1)S(1)}, u32[]{:S(2)}, u32[]{:S(2)}) collective-permute-start(bf16[8,64,2,1]{3,1,2,0:T(8,128)(2,1)S(1)} %get-tuple-element.52), channel_id=1, source_target_pairs={{0,32},{32,64},{64,96},{96,128},{128,160},{160,192},{192,224},{1,3... | collective-permute-start | bytes 6152 | tf_op jit(solution)/shard_map/ppermute | solution.py:18
  246.7 8.0 %collective-permute-start.31 = (bf16[8,64,2,1]{3,1,2,0:T(8,128)(2,1)S(1)}, bf16[8,64,2,1]{3,1,2,0:T(8,128)(2,1)S(1)}, u32[]{:S(2)}, u32[]{:S(2)}) collective-permute-start(bf16[8,64,2,1]{3,1,2,0:T(8,128)(2,1)S(1)} %get-tuple-element.53), channel_id=1, source_target_pairs={{32,0},{64,32},{96,64},{128,96},{160,128},{192,160},{224,192},{33,... | collective-permute-start | bytes 6152 | tf_op jit(solution)/shard_map/ppermute | solution.py:21
  255.1 16.0 %collective-permute-start.32 = (bf16[8,64,1,130]{3,1,2,0:T(8,128)(2,1)S(1)}, bf16[8,64,1,130]{3,1,2,0:T(8,128)(2,1)S(1)}, u32[]{:S(2)}, u32[]{:S(2)}) collective-permute-start(bf16[8,64,1,130]{3,1,2,0:T(8,128)(2,1)S(1)} %get-tuple-element.38), channel_id=1, source_target_pairs={{0,2},{2,4},{4,6},{6,8},{8,10},{10,12},{12,14},{14,16},{16,18},{18... | collective-permute-start | bytes 399368 | tf_op jit(solution)/shard_map/ppermute | solution.py:18
  260.9 14.2 %collective-permute-start.33 = (bf16[8,64,1,130]{3,1,2,0:T(8,128)(2,1)S(1)}, bf16[8,64,1,130]{3,1,2,0:T(8,128)(2,1)S(1)}, u32[]{:S(2)}, u32[]{:S(2)}) collective-permute-start(bf16[8,64,1,130]{3,1,2,0:T(8,128)(2,1)S(1)} %get-tuple-element.39), channel_id=1, source_target_pairs={{2,0},{4,2},{6,4},{8,6},{10,8},{12,10},{14,12},{16,14},{18,16},{20... | collective-permute-start | bytes 399368 | tf_op jit(solution)/shard_map/ppermute | solution.py:21
  285.6 8.1 %collective-permute-start.36 = (bf16[8,64,2,1]{3,1,2,0:T(8,128)(2,1)S(1)}, bf16[8,64,2,1]{3,1,2,0:T(8,128)(2,1)S(1)}, u32[]{:S(2)}, u32[]{:S(2)}) collective-permute-start(bf16[8,64,2,1]{3,1,2,0:T(8,128)(2,1)S(1)} %get-tuple-element.50), channel_id=1, source_target_pairs={{0,32},{32,64},{64,96},{96,128},{128,160},{160,192},{192,224},{1,3... | collective-permute-start | bytes 6152 | tf_op jit(solution)/shard_map/ppermute | solution.py:18
  287.5 8.0 %collective-permute-start.37 = (bf16[8,64,2,1]{3,1,2,0:T(8,128)(2,1)S(1)}, bf16[8,64,2,1]{3,1,2,0:T(8,128)(2,1)S(1)}, u32[]{:S(2)}, u32[]{:S(2)}) collective-permute-start(bf16[8,64,2,1]{3,1,2,0:T(8,128)(2,1)S(1)} %get-tuple-element.51), channel_id=1, source_target_pairs={{32,0},{64,32},{96,64},{128,96},{160,128},{192,160},{224,192},{33,... | collective-permute-start | bytes 6152 | tf_op jit(solution)/shard_map/ppermute | solution.py:21
  295.9 15.4 %collective-permute-start.38 = (bf16[8,64,1,130]{3,1,2,0:T(8,128)(2,1)S(1)}, bf16[8,64,1,130]{3,1,2,0:T(8,128)(2,1)S(1)}, u32[]{:S(2)}, u32[]{:S(2)}) collective-permute-start(bf16[8,64,1,130]{3,1,2,0:T(8,128)(2,1)S(1)} %get-tuple-element.36), channel_id=1, source_target_pairs={{0,2},{2,4},{4,6},{6,8},{8,10},{10,12},{12,14},{14,16},{16,18},{18... | collective-permute-start | bytes 399368 | tf_op jit(solution)/shard_map/ppermute | solution.py:18
  301.2 14.1 %collective-permute-start.39 = (bf16[8,64,1,130]{3,1,2,0:T(8,128)(2,1)S(1)}, bf16[8,64,1,130]{3,1,2,0:T(8,128)(2,1)S(1)}, u32[]{:S(2)}, u32[]{:S(2)}) collective-permute-start(bf16[8,64,1,130]{3,1,2,0:T(8,128)(2,1)S(1)} %get-tuple-element.37), channel_id=1, source_target_pairs={{2,0},{4,2},{6,4},{8,6},{10,8},{12,10},{14,12},{16,14},{18,16},{20... | collective-permute-start | bytes 399368 | tf_op jit(solution)/shard_map/ppermute | solution.py:21
  336.3 7.8 %all-to-all-start.3 = ((f32[16,16,1,128]{3,1,2,0:T(8,128)}), f32[16,16,1,128]{3,1,2,0:T(8,128)S(1)}, u32[]{:S(2)}, u32[]{:S(2)}) async-start(f32[16,16,1,128]{3,1,2,0:T(8,128)} %fusion.89), calls=%async_computation.3 | async-start | bytes 262144 | tf_op jit(solution)/shard_map/all_to_all | solution.py:85
  (28 other events, 209.3 us)
where the time goes:
time: 351 us; the launch traced here: 345 us
  waiting for transfers between devices  147 us (42%)
  starting transfers between devices  116 us (33%)
  other arithmetic  31.9 us (9%)
  matrix products  20.6 us (6%)
  between operations  14.4 us (4%)
  local copies, waits for them, and re-layouts  8.13 us (2%)
  blocking collectives  6.85 us (2%)
    ppermute x21, waiting for transfers between devices, padded_2(): lax.ppermute(lax.slice_in_dim(block, 0, width, axis=dim), axis, backward)  81.4 us
    ppermute x21, waiting for transfers between devices, padded_2(): lax.ppermute(lax.slice_in_dim(block, block.shape[dim] - width, None, axis...  62.3 us
    ppermute x21, starting transfers between devices, padded_2(): lax.ppermute(lax.slice_in_dim(block, block.shape[dim] - width, None, axis...  61 us
    ppermute x21, starting transfers between devices, padded_2(): lax.ppermute(lax.slice_in_dim(block, 0, width, axis=dim), axis, backward)  44.9 us
    unnamed x36, other arithmetic  22.8 us
    dot_general x7, matrix products, stacked_apply(): jnp.einsum('zdij,zdjyx->ziyx', tables, parts, preferred_element_type=jnp....  12.3 us
  transfers between devices with their start and end apart: 45, of which 39 were waited for; matrix products, arithmetic and copies ran while one was open for 6% of the time, Pallas kernels for 0%

commit v1 on v0

v1 whole, which is shorter than its diff:
```python
import jax
import jax.numpy as jnp
from jax import lax
from jax.experimental import pallas as pl
from jax.experimental.pallas import tpu as pltpu
from jax.sharding import PartitionSpec as P

SWEEPS = 4
ALL = ("gx", "gy", "gz")
PLANE = ("gy", "gz")
HIGHEST = lax.Precision.HIGHEST
NZ, BU, PB, NY = 16, 64, 16, 32
ZL, YL, XL, CH = 8, 2, 4, 32
RU, RP = NZ * BU, NZ * PB
HU, HP = ZL * BU, ZL * PB
WIDE = HU + HP
LANES = 128
BLOCKS = WIDE // LANES
STEP = 2 * BLOCKS * 8
f32, bf16 = jnp.float32, jnp.bfloat16


def place(variant, k):
    if variant == 0:
        cx, r = k // 8, k % 8
        cz = r if cx % 2 == 0 else 7 - r
    elif variant == 1:
        cz, r = k // 4, k % 4
        cx = 3 - r if cz % 2 == 0 else r
    elif variant == 2:
        q, r = k // 8, k % 8
        cx = 3 - q
        cz = 7 - r if q % 2 == 0 else r
    else:
        q, r = k // 4, k % 4
        cz = 7 - q
        cx = r if q % 2 == 0 else 3 - r
    return cx * 8 + cz


def slot_of(variant, k):
    a, b, c, d = (place(v, k) for v in range(4))
    return jnp.where(
        variant < 2, jnp.where(variant == 0, a, b), jnp.where(variant == 2, c, d)
    )


def chain():
    order = [g * CH + place(g % 4, k) for g in range(8) for k in range(CH)]
    up = [(order[i], order[i + 1]) for i in range(len(order) - 1)]
    return up, [(b, a) for a, b in up]


def pack_kernel(var_ref, fu_ref, fp_ref, mask_ref, out_ref, flip_ref):
    for yl in range(YL):
        pressure = []
        for z in range(ZL):
            live = mask_ref[pl.ds(z * YL + yl, 1), :] != 0
            weight = live.astype(f32)
            fp = fp_ref[pl.ds(z * PB * YL + yl, PB, stride=YL), :] * weight
            last = lax.broadcasted_iota(jnp.int32, (PB, LANES), 0) == PB - 1
            dead = jnp.broadcast_to(weight, (PB, LANES)) == 0.0
            pressure.append(jnp.where(jnp.logical_and(last, dead), jnp.inf, fp))
        for b in range(BLOCKS - 1):
            pair = []
            for z in (2 * b, 2 * b + 1):
                weight = (mask_ref[pl.ds(z * YL + yl, 1), :] != 0).astype(f32)
                pair.append(fu_ref[pl.ds(z * BU * YL + yl, BU, stride=YL), :] * weight)
            flip_ref[yl, b] = jnp.concatenate(pair, axis=0).T
        flip_ref[yl, BLOCKS - 1] = jnp.concatenate(pressure, axis=0).T
    variant = var_ref[0]
    for k in range(CH):
        dest = slot_of(variant, k) * BLOCKS
        for b in range(BLOCKS):
            out_ref[dest + b] = jnp.concatenate(
                [flip_ref[yl, b, pl.ds(XL * k, XL), :] for yl in range(YL)], axis=0
            )


def spread_kernel(coef_ref, got_ref, fu_ref, fp_ref, mask_ref, send_ref, rows_ref):
    theta_inv = coef_ref[0]
    for half in range(2):
        for b in range(BLOCKS):
            for x in range(XL):
                for yl in range(YL):
                    rows_ref[b, pl.ds(x * NY + yl, CH // 2, stride=YL), :] = got_ref[
                        pl.ds((half * BLOCKS + b) * 8 + yl * XL + x, CH // 2, stride=STEP), :
                    ]
            flat = rows_ref[b].T
            if b < BLOCKS - 1:
                at = pl.ds(half * HU + b * LANES, LANES)
                fu_ref[at, :] = flat
                send_ref[at, :] = (flat * theta_inv).astype(bf16)
            else:
                fp_ref[pl.ds(half * HP, HP), :] = flat
    marks = fp_ref[pl.ds(PB - 1, NZ, stride=PB), :]
    weight = jnp.where(marks == jnp.inf, 0.0, 1.0)
    mask_ref[...] = weight
    send_ref[pl.ds(RU, NZ), :] = weight.astype(bf16)
    fp_ref[...] = jnp.where(fp_ref[...] == jnp.inf, 0.0, fp_ref[...])


def lane_iota(rows):
    return lax.broadcasted_iota(jnp.int32, (rows, LANES), 1)


def neighbours(parts, which):
    own = parts[which]
    lane = lane_iota(BU)
    y = lane % NY
    zero = jnp.zeros_like(own)
    below_y = jnp.where(y == 0, zero, pltpu.roll(own, 1, 1))
    above_y = jnp.where(y == NY - 1, zero, pltpu.roll(own, LANES - 1, 1))
    below_x = pltpu.roll(own, NY, 1)
    if which > 0:
        below_x = jnp.where(lane < NY, pltpu.roll(parts[which - 1], NY, 1), below_x)
    above_x = pltpu.roll(own, LANES - NY, 1)
    if which < 2:
        above_x = jnp.where(
            lane >= LANES - NY, pltpu.roll(parts[which + 1], LANES - NY, 1), above_x
        )
    return jnp.concatenate([below_y, above_y, below_x, above_x], axis=0)


def apply_layer(z, lm_ref, table_ref, w_ref, blocks):
    table = table_ref[lm_ref[z]]
    first = blocks[0] * LANES
    width = len(blocks) * LANES
    parts = [
        w_ref[pl.ds(z * BU + BU, BU), pl.ds(b * LANES, LANES)] for b in range(3)
    ]
    side = jnp.concatenate([neighbours(parts, b) for b in blocks], axis=1)
    column = w_ref[pl.ds(z * BU, 3 * BU), pl.ds(first, width)]
    return jnp.dot(table[:, : 3 * BU], column, preferred_element_type=f32) + jnp.dot(
        table[:, 3 * BU :], side, preferred_element_type=f32
    )


def sweeps(coef_ref, lm_ref, table_ref, mask_ref, d_ref, r_ref, s_ref, w_refs, plan):
    for k, blocks in enumerate(plan):
        keep, scale = coef_ref[2 + 2 * k], coef_ref[3 + 2 * k]
        old, new = w_refs[k % 2], w_refs[(k + 1) % 2]
        lanes = pl.ds(blocks[0] * LANES, len(blocks) * LANES)

        def layer(z, carry):
            z64 = pl.multiple_of(z * BU, BU)
            rows = pl.ds(z64, BU)
            product = apply_layer(z, lm_ref, table_ref, old, blocks)
            r = r_ref[rows, lanes] - product * mask_ref[z, pl.ds(0, 1), lanes]
            d = keep * d_ref[rows, lanes] + scale * r
            s = s_ref[rows, lanes] + d
            r_ref[rows, lanes] = r
            d_ref[rows, lanes] = d
            s_ref[rows, lanes] = s
            if k + 1 < len(plan):
                new[pl.ds(z64 + BU, BU), lanes] = d.astype(bf16)
            return carry

        lax.fori_loop(0, NZ, layer, 0)


def widen(wide_ref, mask_ref, low_ref, high_ref):
    low = low_ref[pl.ds(RU, NZ), :].astype(f32)
    high = high_ref[pl.ds(RU, NZ), :].astype(f32)
    whole = jnp.concatenate([low, mask_ref[...], high], axis=1)
    for z in range(NZ):
        wide_ref[z] = jnp.broadcast_to(whole[z : z + 1], (8, 3 * LANES))


def fill(own_r, thetas, own_w, low, high, d_ref, r_ref, s_ref, w_ref):
    theta_inv, theta = thetas
    edge = jnp.zeros((BU, 3 * LANES), bf16)
    w_ref[pl.ds(0, BU), :] = edge
    w_ref[pl.ds(RU + BU, BU), :] = edge
    for at, src in ((0, low), (2, high)):
        w = src[pl.ds(0, RU), :]
        lanes = pl.ds(at * LANES, LANES)
        w_ref[pl.ds(BU, RU), lanes] = w
        d = w.astype(f32)
        d_ref[:, lanes] = d
        s_ref[:, lanes] = d
        r_ref[:, lanes] = d * theta
    lanes = pl.ds(LANES, LANES)
    d = own_r[...] * theta_inv
    r_ref[:, lanes] = own_r[...]
    d_ref[:, lanes] = d
    s_ref[:, lanes] = d
    w_ref[pl.ds(BU, RU), lanes] = own_w[pl.ds(0, RU), :]


def first_kernel(coef_ref, lm_ref, table_ref, coup_ref, coup_t_ref, schur_ref,
                 fu_ref, fp_ref, mask_ref, own_ref, low_ref, high_ref,
                 ru_ref, du_ref, dp_ref, q_ref, send_ref,
                 wide_ref, d_ref, r_ref, s_ref, wa_ref, wb_ref):
    thetas = (coef_ref[0], coef_ref[1])
    widen(wide_ref, mask_ref, low_ref, high_ref)
    fill(fu_ref, thetas, own_ref, low_ref, high_ref, d_ref, r_ref, s_ref, wa_ref)
    wb_ref[pl.ds(0, BU), :] = jnp.zeros((BU, 3 * LANES), bf16)
    wb_ref[pl.ds(RU + BU, BU), :] = jnp.zeros((BU, 3 * LANES), bf16)
    full = (0, 1, 2)
    sweeps(coef_ref, lm_ref, table_ref, wide_ref, d_ref, r_ref, s_ref, (wa_ref, wb_ref),
           (full, full, full))
    own = pl.ds(LANES, LANES)
    wa_ref[pl.ds(BU, RU), :] = s_ref[...].astype(bf16)
    du_ref[...] = s_ref[:, own]

    def gather(z, carry):
        du = du_ref[pl.ds(pl.multiple_of(z * BU, BU), BU), :]
        here = pl.ds(pl.multiple_of(z * PB, PB), PB)
        q = jnp.dot(coup_ref[lm_ref[z]], du, precision=HIGHEST, preferred_element_type=f32)
        q_ref[here, :] = q * mask_ref[pl.ds(z, 1), :] - fp_ref[here, :]
        return carry

    lax.fori_loop(0, NZ, gather, 0)
    dp_ref[...] = jnp.dot(schur_ref[...], q_ref[...], precision=HIGHEST,
                          preferred_element_type=f32)

    def finish(z, carry):
        here = pl.ds(pl.multiple_of(z * PB, PB), PB)
        rows = pl.ds(pl.multiple_of(z * BU, BU), BU)
        weight = mask_ref[pl.ds(z, 1), :]
        dp = dp_ref[here, :] * weight
        dp_ref[here, :] = dp
        back = jnp.dot(coup_t_ref[lm_ref[z]], dp, precision=HIGHEST,
                       preferred_element_type=f32)
        product = apply_layer(z, lm_ref, table_ref, wa_ref, (1,))
        ru = fu_ref[rows, :] - product * weight - back * weight
        ru_ref[rows, :] = ru
        send_ref[rows, :] = (ru * thetas[0]).astype(bf16)
        return carry

    lax.fori_loop(0, NZ, finish, 0)


def second_kernel(coef_ref, lm_ref, table_ref, coup_ref, schur_ref,
                  fu_ref, mask_ref, ru_ref, du_ref, dp_ref, q_ref, own_ref, low_ref,
                  high_ref, mlow_ref, mhigh_ref, out_ref,
                  wide_ref, d_ref, r_ref, s_ref, wa_ref, wb_ref, p_ref, rows_ref, sort_ref):
    thetas = (coef_ref[0], coef_ref[1])
    widen(wide_ref, mask_ref, mlow_ref, mhigh_ref)
    fill(ru_ref, thetas, own_ref, low_ref, high_ref, d_ref, r_ref, s_ref, wa_ref)
    wb_ref[pl.ds(0, BU), :] = jnp.zeros((BU, 3 * LANES), bf16)
    wb_ref[pl.ds(RU + BU, BU), :] = jnp.zeros((BU, 3 * LANES), bf16)
    full = (0, 1, 2)
    sweeps(coef_ref, lm_ref, table_ref, wide_ref, d_ref, r_ref, s_ref, (wa_ref, wb_ref),
           (full, full, (1,)))
    own = pl.ds(LANES, LANES)

    def gather(z, carry):
        rows = pl.ds(pl.multiple_of(z * BU, BU), BU)
        here = pl.ds(pl.multiple_of(z * PB, PB), PB)
        du = s_ref[rows, own]
        q = jnp.dot(coup_ref[lm_ref[z]], du, precision=HIGHEST, preferred_element_type=f32)
        p_ref[here, :] = q * mask_ref[pl.ds(z, 1), :] + q_ref[here, :]
        return carry

    lax.fori_loop(0, NZ, gather, 0)
    p_ref[...] = jnp.dot(schur_ref[...], p_ref[...], precision=HIGHEST,
                         preferred_element_type=f32)
    for half in range(2):
        for b in range(BLOCKS):
            if b < BLOCKS - 1:
                rows = pl.ds(half * HU + b * LANES, LANES)
                flat = s_ref[rows, own] + du_ref[rows, :] - fu_ref[rows, :]
            else:
                pressure = []
                for z in range(half * ZL, half * ZL + ZL):
                    here = pl.ds(z * PB, PB)
                    dp = p_ref[here, :] * mask_ref[pl.ds(z, 1), :]
                    pressure.append(dp + dp_ref[here, :])
                flat = jnp.concatenate(pressure, axis=0)
            rows_ref[b] = flat.T
            for x in range(XL):
                for yl in range(YL):
                    sort_ref[
                        pl.ds((half * BLOCKS + b) * 8 + yl * XL + x, CH // 2, stride=STEP), :
                    ] = rows_ref[b, pl.ds(x * NY + yl, CH // 2, stride=YL), :]
    out_ref[...] = sort_ref[...].astype(bf16)


def unpack_kernel(var_ref, got_ref, fu_ref, mask_ref, disp_ref, pres_ref, rows_ref):
    variant = var_ref[0]
    for k in range(CH):
        src = slot_of(variant, k) * BLOCKS
        for b in range(BLOCKS):
            piece = got_ref[src + b].astype(f32)
            for yl in range(YL):
                rows_ref[yl, b, pl.ds(XL * k, XL), :] = piece[yl * XL : yl * XL + XL]
    for yl in range(YL):
        for b in range(BLOCKS - 1):
            flat = rows_ref[yl, b].T
            for i in range(2):
                z = 2 * b + i
                weight = (mask_ref[pl.ds(z * YL + yl, 1), :] != 0).astype(f32)
                at = pl.ds(z * BU * YL + yl, BU, stride=YL)
                disp_ref[at, :] = flat[i * BU : i * BU + BU] + fu_ref[at, :] * weight
        pres_ref[pl.ds(yl, HP, stride=YL), :] = rows_ref[yl, BLOCKS - 1].T


VM = pl.BlockSpec(memory_space=pltpu.VMEM)
SM = pl.BlockSpec(memory_space=pltpu.SMEM)


def call(kernel, scalars, arrays, outs, scratch):
    return pl.pallas_call(
        kernel,
        out_shape=[jax.ShapeDtypeStruct(*o) for o in outs],
        in_specs=[SM] * len(scalars) + [VM] * len(arrays),
        out_specs=[VM] * len(outs),
        scratch_shapes=[pltpu.VMEM(*s) for s in scratch],
    )(*scalars, *arrays)


def coefficients(spectrum):
    lower, upper = spectrum[0], spectrum[1]
    theta = (upper + lower) / 2.0
    delta = (upper - lower) / 2.0
    sigma = theta / delta
    rho = 1.0 / sigma
    values = [1.0 / theta, theta]
    for _ in range(SWEEPS - 1):
        rho_next = 1.0 / (2.0 * sigma - rho)
        values += [rho_next * rho, 2.0 * rho_next / delta]
        rho = rho_next
    return jnp.stack(values)


def schur_matrix(sinv, band_offsets):
    depth = jnp.arange(NZ, dtype=jnp.int32)
    hit = (depth[None, :, None] + band_offsets[:, None, None] == depth[None, None, :])
    picked = jnp.where(hit[:, :, None, :, None], sinv[:, :, :, None, :], 0.0)
    return jnp.sum(picked, axis=0).reshape(RP, RP)


def body(force_u, force_p, cellmask, layer_mats, kblocks, bcoup, sinv, band_offsets, spectrum):
    up, down = chain()
    other = lax.ppermute(layer_mats, "gz", [(0, 1), (1, 0)])
    gz = lax.axis_index("gz")
    layers = jnp.where(
        gz == 0, jnp.concatenate([layer_mats, other]), jnp.concatenate([other, layer_mats])
    )
    variant = (lax.axis_index("gx") % 4).astype(jnp.int32)[None]
    fu_in = force_u.reshape(ZL * BU * YL, LANES)
    fp_in = force_p.reshape(ZL * PB * YL, LANES)
    mask_in = cellmask.reshape(ZL * YL, LANES)
    coefs = coefficients(spectrum)
    table = jnp.stack([kblocks[:, d] for d in (1, 0, 2, 3, 4, 5, 6)], axis=2).reshape(4, BU, 7 * BU)
    matrix = schur_matrix(sinv, band_offsets)
    coup_t = bcoup.transpose(0, 2, 1)

    (packed,) = call(
        pack_kernel, [variant], [fu_in, fp_in, mask_in],
        [((CH * BLOCKS, 8, LANES), f32)],
        [((YL, BLOCKS, LANES, LANES), f32)],
    )
    got = lax.all_to_all(packed, PLANE, 0, 0, tiled=True)
    fu, fp, mask, send = call(
        spread_kernel, [coefs], [got.reshape(CH * BLOCKS * 8, LANES)],
        [((RU, LANES), f32), ((RP, LANES), f32), ((NZ, LANES), f32), ((RU + NZ, LANES), bf16)],
        [((BLOCKS, LANES, LANES), f32)],
    )
    low = lax.ppermute(send, ALL, up)
    high = lax.ppermute(send, ALL, down)
    wide = [((NZ, 8, 3 * LANES), f32)] + [((RU, 3 * LANES), f32)] * 3 + [
        ((RU + 2 * BU, 3 * LANES), bf16)
    ] * 2
    ru, du, dp, q, send2 = call(
        first_kernel, [coefs, layers],
        [table, bcoup, coup_t, matrix, fu, fp, mask, send, low, high],
        [((RU, LANES), f32), ((RU, LANES), f32), ((RP, LANES), f32), ((RP, LANES), f32),
         ((RU, LANES), bf16)],
        wide,
    )
    low2 = lax.ppermute(send2, ALL, up)
    high2 = lax.ppermute(send2, ALL, down)
    (back,) = call(
        second_kernel, [coefs, layers],
        [table, bcoup, matrix, fu, mask, ru, du, dp, q, send2, low2, high2, low, high],
        [((CH * BLOCKS * 8, LANES), bf16)],
        wide + [((RP, LANES), f32), ((BLOCKS, LANES, LANES), f32),
                ((CH * BLOCKS * 8, LANES), f32)],
    )
    home = lax.all_to_all(back.reshape(CH * BLOCKS, 8, LANES), PLANE, 0, 0, tiled=True)
    disp, pres = call(
        unpack_kernel, [variant], [home, fu_in, mask_in],
        [((ZL * BU * YL, LANES), f32), ((ZL * PB * YL, LANES), f32)],
        [((YL, BLOCKS, LANES, LANES), f32)],
    )
    return (disp.reshape(ZL, BU, YL, LANES), pres.reshape(ZL, PB, YL, LANES))


def solution(mesh):
    in_specs = (
        P("gz", None, "gy", "gx"),
        P("gz", None, "gy", "gx"),
        P("gz", "gy", "gx"),
        P("gz"),
        P(),
        P(),
        P(),
        P(),
        P(),
    )
    out_specs = (P("gz", None, "gy", "gx"), P("gz", None, "gy", "gx"))
    return jax.shard_map(body, mesh=mesh, in_specs=in_specs, out_specs=out_specs, check_vma=False)
```

time: 351 us -> 131 us (0.37); the launches traced: 345 us -> 130 us
  waiting for transfers between devices: 147 us -> 15 us
  starting transfers between devices: 116 us -> 23.5 us
  Pallas kernels: 0 us -> 50.7 us
  other arithmetic: 31.9 us -> 4.51 us
  matrix products: 20.6 us -> 0 us
  blocking collectives: 6.85 us -> 20.5 us
  between operations: 14.4 us -> 3.72 us
  local copies, waits for them, and re-layouts: 8.13 us -> 12.5 us
    ppermute x42 -> x5, waiting for transfers between devices: 144 us -> 6.71 us  [the longest x1 3.82 us: body(): high2 = lax.ppermute(send2, ALL, down)]
    ppermute x42 -> x5, starting transfers between devices: 106 us -> 13.1 us  [the longest x1 3.43 us: body(): low = lax.ppermute(send, ALL, up)]
    pallas_call x0 -> x5, Pallas kernels: none -> 50.7 us  [call(): pl.pallas_call(kernel, out_shape=[jax.ShapeDtypeStruct(*o) for o in outs]...]
    unnamed x36 -> x0, other arithmetic: 22.8 us -> none
    dot_general x28 -> x0, matrix products: 20.6 us -> none  [the longest x7 12.3 us: stacked_apply(): jnp.einsum('zdij,zdjyx->ziyx', tables, parts, preferred_element_type=jnp....]
    all_to_all x1, blocking collectives: 6.85 us -> 20.5 us  [body(): lax.all_to_all(back.reshape(CH * BLOCKS, 8, LANES), PLANE, 0, 0, tiled=True)]
    all_to_all x3 -> x1, waiting for transfers between devices: 3.26 us -> 8.3 us  [body(): got = lax.all_to_all(packed, PLANE, 0, 0, tiled=True)]
    another operation x7 -> x0, other arithmetic: 4.52 us -> none  [stacked_apply(): jnp.stack([padded[1:-1, :, 1:-1, 1:-1], padded[:-2, :, 1:-1, 1:-1], padde...]
  transfers between devices with their start and end apart: 45 -> 6, of which waited for: 39 -> 4; matrix products, arithmetic and copies ran while one was open for 6% -> 11% of each run, Pallas kernels for 0% -> 4%
where the time goes in v1:
time: 131 us; the launch traced here: 130 us
  Pallas kernels  50.7 us (39%)
  starting transfers between devices  23.5 us (18%)
  blocking collectives  20.5 us (16%)
  waiting for transfers between devices  15 us (11%)
  local copies, waits for them, and re-layouts  12.5 us (10%)
  other arithmetic  4.51 us (3%)
  between operations  3.72 us (3%)
    pallas_call x5, Pallas kernels, call(): pl.pallas_call(kernel, out_shape=[jax.ShapeDtypeStruct(*o) for o in outs]...  50.7 us
    all_to_all x1, blocking collectives, body(): lax.all_to_all(back.reshape(CH * BLOCKS, 8, LANES), PLANE, 0, 0, tiled=True)  20.5 us
    all_to_all x1, starting transfers between devices, body(): got = lax.all_to_all(packed, PLANE, 0, 0, tiled=True)  10.4 us
    all_to_all x1, waiting for transfers between devices, body(): got = lax.all_to_all(packed, PLANE, 0, 0, tiled=True)  8.3 us
    unnamed x27, local copies, waits for them, and re-layouts  6.8 us
    ppermute x1, waiting for transfers between devices, body(): high2 = lax.ppermute(send2, ALL, down)  3.82 us
    reduce_sum x1, other arithmetic, schur_matrix(): return jnp.sum(picked, axis=0).reshape(RP, RP)  3.79 us
    ppermute x1, starting transfers between devices, body(): low = lax.ppermute(send, ALL, up)  3.43 us
  transfers between devices with their start and end apart: 6, of which 4 were waited for; matrix products, arithmetic and copies ran while one was open for 11% of the time, Pallas kernels for 4%

profile of v1, /device:TPU:16, one launch (start us, length us, event | category | flops | bytes accessed | tf_op | source)
XLA Modules:
  0.0 130.4 jit_solution(1233118099354228695)
XLA Ops:
  0.7 2.0 %collective-permute-start = (s32[8]{0:T(128)}, s32[8]{0:T(128)S(1)}, u32[]{:S(2)}, u32[]{:S(2)}) collective-permute-start(s32[8]{0:T(128)} %param.12), channel_id=1, source_target_pairs={{0,1},{1,0},{2,3},{3,2},{4,5},{5,4},{6,7},{7,6},{8,9},{9,8},{10,11... | collective-permute-start | bytes 104 | tf_op jit(solution)/shard_map/ppermute | solution.py:337
  2.7 2.2 %shard_map.104 = f32[160,8,128]{2,1,0:T(8,128)} custom-call(s32[1]{0:T(128)} %bitcast.var_ref, f32[1024,128]{1,0:T(8,128)} %bitcast.47, f32[256,128]{1,0:T(8,128)} %bitcast.51, s32[16,128]{1,0:T(8,128)} %bitcast.52), custom_call_target="tpu_custom_call" | custom-call | tf_op jit(solution)/shard_map/pallas_call | solution.py:305
  4.9 10.4 %all-to-all-start = ((f32[160,8,128]{2,1,0:T(8,128)}), f32[160,8,128]{2,1,0:T(8,128)S(1)}, u32[]{:S(2)}, u32[]{:S(2)}) async-start(f32[160,8,128]{2,1,0:T(8,128)} %shard_map.104), calls=%async_computation | async-start | bytes 1310720 | tf_op jit(solution)/shard_map/all_to_all | solution.py:356
  15.3 0.6 fusion
  18.9 0.6 bitcast_dynamic-update-slice_fusion.5
  19.5 0.6 bitcast_dynamic-update-slice_fusion.4
  20.2 0.6 bitcast_dynamic-update-slice_fusion.3
  20.9 0.6 stack.35.coef_ref
  21.6 0.6 bitcast_dynamic-update-slice_fusion.2
  22.2 0.6 bitcast_dynamic-update-slice_fusion.6
  22.8 0.6 bitcast_dynamic-update-slice_fusion.1
  23.5 3.8 %select_reduce_fusion = f32[16,16,16,16]{3,2,1,0:T(8,128)S(1)} fusion(f32[8,16,16,16]{3,2,1,0:T(8,128)} %param.15, pred[8,16,16]{2,1,0:T(8,128)(4,1)S(1)} %iota_compare_fusion), kind=kLoop, calls=%fused_computation | loop fusion | flops 983040 | bytes 395264 | tf_op jit(solution)/shard_map/reduce_sum | solution.py:332
  27.3 8.3 %all-to-all-done = f32[160,8,128]{2,1,0:T(8,128)S(1)} async-done(((f32[160,8,128]{2,1,0:T(8,128)}), f32[160,8,128]{2,1,0:T(8,128)S(1)}, u32[]{:S(2)}, u32[]{:S(2)}) %all-to-all-start) | async-done | bytes 655392 | tf_op jit(solution)/shard_map/all_to_all | solution.py:356
  35.6 0.8 copy-done
  36.4 2.4 %shard_map.105 = (f32[1024,128]{1,0:T(8,128)}, f32[256,128]{1,0:T(8,128)}, f32[16,128]{1,0:T(8,128)}, bf16[1040,128]{1,0:T(8,128)(2,1)}) custom-call(f32[8]{0:T(128)} %stack.35.coef_ref, f32[1280,128]{1,0:T(8,128)} %bitcast.46), custom_call_target="tpu_custom_call" | custom-call | tf_op jit(solution)/shard_map/pallas_call | solution.py:305
  38.8 3.4 %collective-permute-start.1 = (bf16[1040,128]{1,0:T(8,128)(2,1)}, bf16[1040,128]{1,0:T(8,128)(2,1)S(1)}, u32[]{:S(2)}, u32[]{:S(2)}) collective-permute-start(bf16[1040,128]{1,0:T(8,128)(2,1)} %get-tuple-element.16.own_ref), channel_id=1, source_target_pairs={{0,1},{1,2},{2,3},{3,4},{4,5},{5,6},{6,7},{7,15},{15,14},{14,13},{... | collective-permute-start | bytes 798728 | tf_op jit(solution)/shard_map/ppermute | solution.py:362
  42.3 2.1 %collective-permute-start.2 = (bf16[1040,128]{1,0:T(8,128)(2,1)}, bf16[1040,128]{1,0:T(8,128)(2,1)S(1)}, u32[]{:S(2)}, u32[]{:S(2)}) collective-permute-start(bf16[1040,128]{1,0:T(8,128)(2,1)} %get-tuple-element.16.own_ref), channel_id=1, source_target_pairs={{1,0},{2,1},{3,2},{4,3},{5,4},{6,5},{7,6},{15,7},{14,15},{13,14},{... | collective-permute-start | bytes 798728 | tf_op jit(solution)/shard_map/ppermute | solution.py:363
  44.4 0.6 bitcast_dynamic-update-slice_fusion
  45.0 1.3 %copy.33 = bf16[4,64,7,64]{3,2,1,0:T(8,128)(2,1)S(1)} copy(bf16[4,64,7,64]{3,1,0,2:T(8,128)(2,1)} %bitcast_dynamic-update-slice_fusion) | data formatting | bytes 458752 | tf_op jit(solution)/shard_map/stack | solution.py:347
  46.4 1.0 reshape.67.table_ref
  47.4 1.5 %reshape.68.schur_ref = f32[256,256]{1,0:T(8,128)} reshape(f32[16,16,16,16]{3,2,1,0:T(8,128)S(1)} %select_reduce_fusion) | data formatting | bytes 524288 | tf_op jit(solution)/shard_map/reshape | solution.py:332
  48.9 0.8 copy.34
  50.9 0.6 copy-done.2
  51.5 24.3 %shard_map.106 = (f32[1024,128]{1,0:T(8,128)}, f32[1024,128]{1,0:T(8,128)}, f32[256,128]{1,0:T(8,128)}, f32[256,128]{1,0:T(8,128)}, bf16[1024,128]{1,0:T(8,128)(2,1)}) custom-call(f32[8]{0:T(128)} %stack.35.coef_ref, s32[16]{0:T(128)} %broadcast_select_fusion.lm_ref, bf16[4,64,448]{2,1,0:T(8,128)(2,1)} %reshape.67.table_ref, f32[4,16,64]{2,1,0:T(8,128)} %coup_ref.3, ...), custom_call_target="tpu_custom_call" | custom-call | tf_op jit(solution)/shard_map/pallas_call | solution.py:305
  75.8 3.2 %collective-permute-start.3 = (bf16[1024,128]{1,0:T(8,128)(2,1)}, bf16[1024,128]{1,0:T(8,128)(2,1)S(1)}, u32[]{:S(2)}, u32[]{:S(2)}) collective-permute-start(bf16[1024,128]{1,0:T(8,128)(2,1)} %get-tuple-element.21.own_ref), channel_id=1, source_target_pairs={{0,1},{1,2},{2,3},{3,4},{4,5},{5,6},{6,7},{7,15},{15,14},{14,13},{... | collective-permute-start | bytes 786440 | tf_op jit(solution)/shard_map/ppermute | solution.py:374
  79.0 2.3 %collective-permute-start.4 = (bf16[1024,128]{1,0:T(8,128)(2,1)}, bf16[1024,128]{1,0:T(8,128)(2,1)S(1)}, u32[]{:S(2)}, u32[]{:S(2)}) collective-permute-start(bf16[1024,128]{1,0:T(8,128)(2,1)} %get-tuple-element.21.own_ref), channel_id=1, source_target_pairs={{1,0},{2,1},{3,2},{4,3},{5,4},{6,5},{7,6},{15,7},{14,15},{13,14},{... | collective-permute-start | bytes 786440 | tf_op jit(solution)/shard_map/ppermute | solution.py:375
  81.3 2.3 %collective-permute-done.3.low_ref = bf16[1024,128]{1,0:T(8,128)(2,1)S(1)} collective-permute-done((bf16[1024,128]{1,0:T(8,128)(2,1)}, bf16[1024,128]{1,0:T(8,128)(2,1)S(1)}, u32[]{:S(2)}, u32[]{:S(2)}) %collective-permute-start.3) | collective-permute-done | bytes 262176 | tf_op jit(solution)/shard_map/ppermute | solution.py:374
  83.7 3.8 %collective-permute-done.4.high_ref = bf16[1024,128]{1,0:T(8,128)(2,1)S(1)} collective-permute-done((bf16[1024,128]{1,0:T(8,128)(2,1)}, bf16[1024,128]{1,0:T(8,128)(2,1)S(1)}, u32[]{:S(2)}, u32[]{:S(2)}) %collective-permute-start.4) | collective-permute-done | bytes 262176 | tf_op jit(solution)/shard_map/ppermute | solution.py:375
  87.5 0.7 copy-done.6
  88.2 19.4 %shard_map.107 = bf16[1280,128]{1,0:T(8,128)(2,1)} custom-call(f32[8]{0:T(128)} %stack.35.coef_ref, s32[16]{0:T(128)} %broadcast_select_fusion.lm_ref, bf16[4,64,448]{2,1,0:T(8,128)(2,1)} %reshape.67.table_ref, f32[4,16,64]{2,1,0:T(8,128)} %coup_ref.3, f32[256,256]{1,0:T(8,128)} %reshape.68.schur_ref, f32[1024,128]{1,0:T(8,128)} %get-tuple-element.13.fu_ref, ...), custom_call_target="tpu_custom_call" | custom-call | tf_op jit(solution)/shard_map/pallas_call | solution.py:305
  107.6 20.5 %all_to_all.10.got_ref = bf16[160,8,128]{2,1,0:T(8,128)(2,1)} all-to-all(bf16[160,8,128]{2,1,0:T(8,128)(2,1)} %bitcast.49), channel_id=1, replica_groups=mesh['gx'=8,'gy'=16,'gz'=2] {'gy','gz'}, dimensions={0} | all-to-all | bytes 655360 | tf_op jit(solution)/shard_map/all_to_all | solution.py:383
  128.1 2.3 %shard_map.108 = (f32[1024,128]{1,0:T(8,128)}, f32[256,128]{1,0:T(8,128)}) custom-call(s32[1]{0:T(128)} %bitcast.var_ref, bf16[160,8,128]{2,1,0:T(8,128)(2,1)} %all_to_all.10.got_ref, f32[1024,128]{1,0:T(8,128)} %bitcast.48, s32[16,128]{1,0:T(8,128)} %bitcast.53), custom_call_target="tpu_custom_call" | custom-call | tf_op jit(solution)/shard_map/pallas_call | solution.py:305
  (23 shorter events, 1.4 us)
Async XLA Ops:
  0.6 14.7 %copy-start.7 = (f32[2]{0:T(128)S(1)}, f32[2]{0:T(128)}, u32[]{:S(2)}) copy-start(f32[2]{0:T(128)} %param.17) | copy-start | bytes 28
  0.6 18.2 %copy-start.3 = (bf16[4,7,64,64]{3,2,1,0:T(8,128)(2,1)S(1)}, bf16[4,7,64,64]{3,2,1,0:T(8,128)(2,1)}, u32[]{:S(2)}) copy-start(bf16[4,7,64,64]{3,2,1,0:T(8,128)(2,1)} %param.13) | copy-start | bytes 688132
  0.7 20.1 %copy-start.8 = (s32[8]{0:T(128)S(1)}, s32[8]{0:T(128)}, u32[]{:S(2)}) copy-start(s32[8]{0:T(128)} %param.16) | copy-start | bytes 100
  0.7 49.0 %collective-permute-start = (s32[8]{0:T(128)}, s32[8]{0:T(128)S(1)}, u32[]{:S(2)}, u32[]{:S(2)}) collective-permute-start(s32[8]{0:T(128)} %param.12), channel_id=1, source_target_pairs={{0,1},{1,0},{2,3},{3,2},{4,5},{5,4},{6,7},{7,6},{8,9},{9,8},{10,11... | collective-permute-start | bytes 104 | tf_op jit(solution)/shard_map/ppermute | solution.py:337
  4.9 30.7 %all-to-all-start = ((f32[160,8,128]{2,1,0:T(8,128)}), f32[160,8,128]{2,1,0:T(8,128)S(1)}, u32[]{:S(2)}, u32[]{:S(2)}) async-start(f32[160,8,128]{2,1,0:T(8,128)} %shard_map.104), calls=%async_computation | async-start | bytes 1310720 | tf_op jit(solution)/shard_map/all_to_all | solution.py:356
  35.6 0.8 copy-start
  38.8 11.4 %collective-permute-start.1 = (bf16[1040,128]{1,0:T(8,128)(2,1)}, bf16[1040,128]{1,0:T(8,128)(2,1)S(1)}, u32[]{:S(2)}, u32[]{:S(2)}) collective-permute-start(bf16[1040,128]{1,0:T(8,128)(2,1)} %get-tuple-element.16.own_ref), channel_id=1, source_target_pairs={{0,1},{1,2},{2,3},{3,4},{4,5},{5,6},{6,7},{7,15},{15,14},{14,13},{... | collective-permute-start | bytes 798728 | tf_op jit(solution)/shard_map/ppermute | solution.py:362
  42.3 8.5 %collective-permute-start.2 = (bf16[1040,128]{1,0:T(8,128)(2,1)}, bf16[1040,128]{1,0:T(8,128)(2,1)S(1)}, u32[]{:S(2)}, u32[]{:S(2)}) collective-permute-start(bf16[1040,128]{1,0:T(8,128)(2,1)} %get-tuple-element.16.own_ref), channel_id=1, source_target_pairs={{1,0},{2,1},{3,2},{4,3},{5,4},{6,5},{7,6},{15,7},{14,15},{13,14},{... | collective-permute-start | bytes 798728 | tf_op jit(solution)/shard_map/ppermute | solution.py:363
  45.0 3.9 %copy-start.4 = (f32[4,16,64]{2,1,0:T(8,128)S(1)}, f32[4,16,64]{2,1,0:T(8,128)}, u32[]{:S(2)}) copy-start(f32[4,16,64]{2,1,0:T(8,128)} %coup_ref.3) | copy-start | bytes 49156
  45.0 4.6 %copy-start.9 = (s32[8]{0:T(128)S(1)}, s32[8]{0:T(128)}, u32[]{:S(2)}) copy-start(s32[8]{0:T(128)} %param.12) | copy-start | bytes 100
  50.2 0.7 copy-start.1
  50.8 0.7 copy-start.2
  75.8 7.9 %collective-permute-start.3 = (bf16[1024,128]{1,0:T(8,128)(2,1)}, bf16[1024,128]{1,0:T(8,128)(2,1)S(1)}, u32[]{:S(2)}, u32[]{:S(2)}) collective-permute-start(bf16[1024,128]{1,0:T(8,128)(2,1)} %get-tuple-element.21.own_ref), channel_id=1, source_target_pairs={{0,1},{1,2},{2,3},{3,4},{4,5},{5,6},{6,7},{7,15},{15,14},{14,13},{... | collective-permute-start | bytes 786440 | tf_op jit(solution)/shard_map/ppermute | solution.py:374
  79.0 8.5 %collective-permute-start.4 = (bf16[1024,128]{1,0:T(8,128)(2,1)}, bf16[1024,128]{1,0:T(8,128)(2,1)S(1)}, u32[]{:S(2)}, u32[]{:S(2)}) collective-permute-start(bf16[1024,128]{1,0:T(8,128)(2,1)} %get-tuple-element.21.own_ref), channel_id=1, source_target_pairs={{1,0},{2,1},{3,2},{4,3},{5,4},{6,5},{7,6},{15,7},{14,15},{13,14},{... | collective-permute-start | bytes 786440 | tf_op jit(solution)/shard_map/ppermute | solution.py:375
  83.7 3.8 %copy-start.5 = (bf16[1024,128]{1,0:T(8,128)(2,1)}, bf16[1024,128]{1,0:T(8,128)(2,1)S(1)}, u32[]{:S(2)}) copy-start(bf16[1024,128]{1,0:T(8,128)(2,1)S(1)} %collective-permute-done.3.low_ref) | copy-start | bytes 786436
  87.5 0.7 copy-start.6

commit v2 on v1

--- a/solution.py
+++ b/solution.py
@@ -17,6 +17,7 @@
 LANES = 128
 BLOCKS = WIDE // LANES
 STEP = 2 * BLOCKS * 8
+UNROLL = 4
 f32, bf16 = jnp.float32, jnp.bfloat16
 
 
@@ -122,41 +123,70 @@
     return jnp.concatenate([below_y, above_y, below_x, above_x], axis=0)
 
 
-def apply_layer(z, lm_ref, table_ref, w_ref, blocks):
-    table = table_ref[lm_ref[z]]
+def operands(z64, w_ref, blocks):
     first = blocks[0] * LANES
     width = len(blocks) * LANES
     parts = [
-        w_ref[pl.ds(z * BU + BU, BU), pl.ds(b * LANES, LANES)] for b in range(3)
+        w_ref[pl.ds(z64 + BU, BU), pl.ds(b * LANES, LANES)] for b in range(3)
     ]
     side = jnp.concatenate([neighbours(parts, b) for b in blocks], axis=1)
-    column = w_ref[pl.ds(z * BU, 3 * BU), pl.ds(first, width)]
-    return jnp.dot(table[:, : 3 * BU], column, preferred_element_type=f32) + jnp.dot(
-        table[:, 3 * BU :], side, preferred_element_type=f32
-    )
-
-
-def sweeps(coef_ref, lm_ref, table_ref, mask_ref, d_ref, r_ref, s_ref, w_refs, plan):
-    for k, blocks in enumerate(plan):
-        keep, scale = coef_ref[2 + 2 * k], coef_ref[3 + 2 * k]
-        old, new = w_refs[k % 2], w_refs[(k + 1) % 2]
-        lanes = pl.ds(blocks[0] * LANES, len(blocks) * LANES)
-
-        def layer(z, carry):
-            z64 = pl.multiple_of(z * BU, BU)
+    column = w_ref[pl.ds(z64, 3 * BU), pl.ds(first, width)]
+    return [side, column]
+
+
+def layers_of(group):
+    return [group * UNROLL + i for i in range(UNROLL)]
+
+
+def sweep(k, blocks, begin, last, scal, refs, old, new):
+    coef_ref, lm_ref, table_ref, mask_ref, d_ref, r_ref, s_ref = refs
+    keep, scale = coef_ref[2 + 2 * k], coef_ref[3 + 2 * k]
+    lanes = pl.ds(blocks[0] * LANES, len(blocks) * LANES)
+
+    def group(g, carry):
+        at = [pl.multiple_of(z * BU, BU) for z in layers_of(g)]
+        products = []
+        for z, z64 in zip(layers_of(g), at):
+            table = table_ref[lm_ref[z]]
+            stack = jnp.concatenate(operands(z64, old, blocks), axis=0)
+            products.append(
+                jnp.dot(table[:, : 7 * BU], stack, preferred_element_type=f32)
+            )
+        for z, z64, product in zip(layers_of(g), at, products):
             rows = pl.ds(z64, BU)
-            product = apply_layer(z, lm_ref, table_ref, old, blocks)
-            r = r_ref[rows, lanes] - product * mask_ref[z, pl.ds(0, 1), lanes]
-            d = keep * d_ref[rows, lanes] + scale * r
-            s = s_ref[rows, lanes] + d
-            r_ref[rows, lanes] = r
-            d_ref[rows, lanes] = d
-            s_ref[rows, lanes] = s
-            if k + 1 < len(plan):
+            if begin is None:
+                r, d, s = r_ref[rows, lanes], d_ref[rows, lanes], s_ref[rows, lanes]
+            else:
+                r, d = begin(rows)
+                s = d
+            r = r - product * mask_ref[z, pl.ds(0, 1), lanes]
+            d = keep * d + scale * r
+            s = s + d
+            if last is None:
+                r_ref[rows, lanes] = r
+                d_ref[rows, lanes] = d
+                s_ref[rows, lanes] = s
                 new[pl.ds(z64 + BU, BU), lanes] = d.astype(bf16)
-            return carry
-
-        lax.fori_loop(0, NZ, layer, 0)
+            else:
+                last(z64, s)
+        return carry
+
+    lax.fori_loop(0, NZ // UNROLL, group, 0)
+
+
+def starter(scal, own_ref, low_ref, high_ref):
+    theta_inv, theta = scal
+
+    def begin(rows):
+        r = own_ref[rows, :]
+        low = low_ref[rows, :].astype(f32)
+        high = high_ref[rows, :].astype(f32)
+        return (
+            jnp.concatenate([low * theta, r, high * theta], axis=1),
+            jnp.concatenate([low, r * theta_inv, high], axis=1),
+        )
+
+    return begin
 
 
 def widen(wide_ref, mask_ref, low_ref, high_ref):
@@ -167,96 +197,122 @@
         wide_ref[z] = jnp.broadcast_to(whole[z : z + 1], (8, 3 * LANES))
 
 
-def fill(own_r, thetas, own_w, low, high, d_ref, r_ref, s_ref, w_ref):
-    theta_inv, theta = thetas
+def pad_in(w_refs, sources):
     edge = jnp.zeros((BU, 3 * LANES), bf16)
-    w_ref[pl.ds(0, BU), :] = edge
-    w_ref[pl.ds(RU + BU, BU), :] = edge
-    for at, src in ((0, low), (2, high)):
-        w = src[pl.ds(0, RU), :]
-        lanes = pl.ds(at * LANES, LANES)
-        w_ref[pl.ds(BU, RU), lanes] = w
-        d = w.astype(f32)
-        d_ref[:, lanes] = d
-        s_ref[:, lanes] = d
-        r_ref[:, lanes] = d * theta
-    lanes = pl.ds(LANES, LANES)
-    d = own_r[...] * theta_inv
-    r_ref[:, lanes] = own_r[...]
-    d_ref[:, lanes] = d
-    s_ref[:, lanes] = d
-    w_ref[pl.ds(BU, RU), lanes] = own_w[pl.ds(0, RU), :]
-
-
-def first_kernel(coef_ref, lm_ref, table_ref, coup_ref, coup_t_ref, schur_ref,
+    for w_ref in w_refs:
+        w_ref[pl.ds(0, BU), :] = edge
+        w_ref[pl.ds(RU + BU, BU), :] = edge
+    for at, src in enumerate(sources):
+        w_refs[0][pl.ds(BU, RU), pl.ds(at * LANES, LANES)] = src[pl.ds(0, RU), :]
+
+
+def thirds(v):
+    high = v.astype(bf16)
+    low = (v - high.astype(f32)).astype(bf16)
+    return [high, low, high]
+
+
+def couple(get, lm_ref, coup_ref, mask_ref, rest_ref, sign, q_ref):
+    def group(g, carry):
+        for z in layers_of(g):
+            here = pl.ds(pl.multiple_of(z * PB, PB), PB)
+            du = get(pl.multiple_of(z * BU, BU))
+            q = jnp.dot(coup_ref[lm_ref[z]], jnp.concatenate(thirds(du), axis=0),
+                        preferred_element_type=f32)
+            q_ref[here, :] = q * mask_ref[z, pl.ds(0, 1), pl.ds(LANES, LANES)] + sign * rest_ref[here, :]
+        return carry
+
+    lax.fori_loop(0, NZ // UNROLL, group, 0)
+
+
+def bands(schur_ref, q_ref):
+    return jnp.dot(schur_ref[...], jnp.concatenate(thirds(q_ref[...]), axis=0),
+                   preferred_element_type=f32)
+
+
+OWN = pl.ds(LANES, LANES)
+FULL = (0, 1, 2)
+
+
+def prep_kernel(kb_ref, coup_ref, schur_ref, table_ref, pair_ref, band_ref):
+    for m in range(4):
+        coup = coup_ref[m]
+        high = coup.astype(bf16)
+        low = (coup - high.astype(f32)).astype(bf16)
+        pair_ref[m] = jnp.concatenate([high, high, low], axis=1)
+        back = coup.T
+        bhigh = back.astype(bf16)
+        blow = (back - bhigh.astype(f32)).astype(bf16)
+        blocks = [kb_ref[m, d] for d in (3, 4, 5, 6, 1, 0, 2)]
+        pad = jnp.zeros((BU, PB), bf16)
+        table_ref[m] = jnp.concatenate(blocks + [bhigh, bhigh, blow, pad], axis=1)
+    whole = schur_ref[...]
+    high = whole.astype(bf16)
+    low = (whole - high.astype(f32)).astype(bf16)
+    band_ref[...] = jnp.concatenate([high, high, low], axis=1)
+
+
+def first_kernel(coef_ref, lm_ref, table_ref, coup_ref, schur_ref,
                  fu_ref, fp_ref, mask_ref, own_ref, low_ref, high_ref,
                  ru_ref, du_ref, dp_ref, q_ref, send_ref,
                  wide_ref, d_ref, r_ref, s_ref, wa_ref, wb_ref):
-    thetas = (coef_ref[0], coef_ref[1])
+    scal = (coef_ref[0], coef_ref[1])
     widen(wide_ref, mask_ref, low_ref, high_ref)
-    fill(fu_ref, thetas, own_ref, low_ref, high_ref, d_ref, r_ref, s_ref, wa_ref)
-    wb_ref[pl.ds(0, BU), :] = jnp.zeros((BU, 3 * LANES), bf16)
-    wb_ref[pl.ds(RU + BU, BU), :] = jnp.zeros((BU, 3 * LANES), bf16)
-    full = (0, 1, 2)
-    sweeps(coef_ref, lm_ref, table_ref, wide_ref, d_ref, r_ref, s_ref, (wa_ref, wb_ref),
-           (full, full, full))
-    own = pl.ds(LANES, LANES)
-    wa_ref[pl.ds(BU, RU), :] = s_ref[...].astype(bf16)
-    du_ref[...] = s_ref[:, own]
-
-    def gather(z, carry):
-        du = du_ref[pl.ds(pl.multiple_of(z * BU, BU), BU), :]
-        here = pl.ds(pl.multiple_of(z * PB, PB), PB)
-        q = jnp.dot(coup_ref[lm_ref[z]], du, precision=HIGHEST, preferred_element_type=f32)
-        q_ref[here, :] = q * mask_ref[pl.ds(z, 1), :] - fp_ref[here, :]
+    pad_in((wa_ref, wb_ref), (low_ref, own_ref, high_ref))
+    refs = (coef_ref, lm_ref, table_ref, wide_ref, d_ref, r_ref, s_ref)
+    begin = starter(scal, fu_ref, low_ref, high_ref)
+
+    def last(z64, s):
+        wb_ref[pl.ds(z64 + BU, BU), :] = s.astype(bf16)
+        du_ref[pl.ds(z64, BU), :] = s[:, LANES : 2 * LANES]
+
+    sweep(0, FULL, begin, None, scal, refs, wa_ref, wb_ref)
+    sweep(1, FULL, None, None, scal, refs, wb_ref, wa_ref)
+    sweep(2, FULL, None, last, scal, refs, wa_ref, wb_ref)
+    couple(lambda z64: du_ref[pl.ds(z64, BU), :], lm_ref, coup_ref, wide_ref, fp_ref, -1.0, q_ref)
+    dp_ref[...] = bands(schur_ref, q_ref)
+
+    def finish(g, carry):
+        at = [pl.multiple_of(z * BU, BU) for z in layers_of(g)]
+        products = []
+        for z, z64 in zip(layers_of(g), at):
+            here = pl.ds(pl.multiple_of(z * PB, PB), PB)
+            dp = dp_ref[here, :] * wide_ref[z, pl.ds(0, 1), OWN]
+            dp_ref[here, :] = dp
+            stack = operands(z64, wb_ref, (1,)) + thirds(dp)
+            products.append(
+                jnp.dot(table_ref[lm_ref[z]][:, : 7 * BU + 3 * PB],
+                        jnp.concatenate(stack, axis=0), preferred_element_type=f32)
+            )
+        for z, z64, product in zip(layers_of(g), at, products):
+            rows = pl.ds(z64, BU)
+            ru = fu_ref[rows, :] - product * wide_ref[z, pl.ds(0, 1), OWN]
+            ru_ref[rows, :] = ru
+            send_ref[rows, :] = (ru * scal[0]).astype(bf16)
         return carry
 
-    lax.fori_loop(0, NZ, gather, 0)
-    dp_ref[...] = jnp.dot(schur_ref[...], q_ref[...], precision=HIGHEST,
-                          preferred_element_type=f32)
-
-    def finish(z, carry):
-        here = pl.ds(pl.multiple_of(z * PB, PB), PB)
-        rows = pl.ds(pl.multiple_of(z * BU, BU), BU)
-        weight = mask_ref[pl.ds(z, 1), :]
-        dp = dp_ref[here, :] * weight
-        dp_ref[here, :] = dp
-        back = jnp.dot(coup_t_ref[lm_ref[z]], dp, precision=HIGHEST,
-                       preferred_element_type=f32)
-        product = apply_layer(z, lm_ref, table_ref, wa_ref, (1,))
-        ru = fu_ref[rows, :] - product * weight - back * weight
-        ru_ref[rows, :] = ru
-        send_ref[rows, :] = (ru * thetas[0]).astype(bf16)
-        return carry
-
-    lax.fori_loop(0, NZ, finish, 0)
+    lax.fori_loop(0, NZ // UNROLL, finish, 0)
 
 
 def second_kernel(coef_ref, lm_ref, table_ref, coup_ref, schur_ref,
                   fu_ref, mask_ref, ru_ref, du_ref, dp_ref, q_ref, own_ref, low_ref,
                   high_ref, mlow_ref, mhigh_ref, out_ref,
                   wide_ref, d_ref, r_ref, s_ref, wa_ref, wb_ref, p_ref, rows_ref, sort_ref):
-    thetas = (coef_ref[0], coef_ref[1])
+    scal = (coef_ref[0], coef_ref[1])
     widen(wide_ref, mask_ref, mlow_ref, mhigh_ref)
-    fill(ru_ref, thetas, own_ref, low_ref, high_ref, d_ref, r_ref, s_ref, wa_ref)
-    wb_ref[pl.ds(0, BU), :] = jnp.zeros((BU, 3 * LANES), bf16)
-    wb_ref[pl.ds(RU + BU, BU), :] = jnp.zeros((BU, 3 * LANES), bf16)
-    full = (0, 1, 2)
-    sweeps(coef_ref, lm_ref, table_ref, wide_ref, d_ref, r_ref, s_ref, (wa_ref, wb_ref),
-           (full, full, (1,)))
-    own = pl.ds(LANES, LANES)
-
-    def gather(z, carry):
-        rows = pl.ds(pl.multiple_of(z * BU, BU), BU)
-        here = pl.ds(pl.multiple_of(z * PB, PB), PB)
-        du = s_ref[rows, own]
-        q = jnp.dot(coup_ref[lm_ref[z]], du, precision=HIGHEST, preferred_element_type=f32)
-        p_ref[here, :] = q * mask_ref[pl.ds(z, 1), :] + q_ref[here, :]
-        return carry
-
-    lax.fori_loop(0, NZ, gather, 0)
-    p_ref[...] = jnp.dot(schur_ref[...], p_ref[...], precision=HIGHEST,
-                         preferred_element_type=f32)
+    pad_in((wa_ref, wb_ref), (low_ref, own_ref, high_ref))
+    refs = (coef_ref, lm_ref, table_ref, wide_ref, d_ref, r_ref, s_ref)
+    begin = starter(scal, ru_ref, low_ref, high_ref)
+
+    def last(z64, s):
+        s_ref[pl.ds(z64, BU), OWN] = s
+
+    sweep(0, FULL, begin, None, scal, refs, wa_ref, wb_ref)
+    sweep(1, FULL, None, None, scal, refs, wb_ref, wa_ref)
+    sweep(2, (1,), None, last, scal, refs, wa_ref, wb_ref)
+    couple(lambda z64: s_ref[pl.ds(z64, BU), OWN], lm_ref, coup_ref, wide_ref, q_ref, 1.0, p_ref)
+    p_ref[...] = bands(schur_ref, p_ref)
+    own = OWN
     for half in range(2):
         for b in range(BLOCKS):
             if b < BLOCKS - 1:
@@ -301,13 +357,14 @@
 SM = pl.BlockSpec(memory_space=pltpu.SMEM)
 
 
-def call(kernel, scalars, arrays, outs, scratch):
+def call(kernel, scalars, arrays, outs, scratch, limit=24):
     return pl.pallas_call(
         kernel,
         out_shape=[jax.ShapeDtypeStruct(*o) for o in outs],
         in_specs=[SM] * len(scalars) + [VM] * len(arrays),
         out_specs=[VM] * len(outs),
         scratch_shapes=[pltpu.VMEM(*s) for s in scratch],
+        compiler_params=pltpu.CompilerParams(vmem_limit_bytes=limit << 20),
     )(*scalars, *arrays)
 
 
@@ -344,9 +401,10 @@
     fp_in = force_p.reshape(ZL * PB * YL, LANES)
     mask_in = cellmask.reshape(ZL * YL, LANES)
     coefs = coefficients(spectrum)
-    table = jnp.stack([kblocks[:, d] for d in (1, 0, 2, 3, 4, 5, 6)], axis=2).reshape(4, BU, 7 * BU)
-    matrix = schur_matrix(sinv, band_offsets)
-    coup_t = bcoup.transpose(0, 2, 1)
+    table, pair, matrix = call(
+        prep_kernel, [], [kblocks, bcoup, schur_matrix(sinv, band_offsets)],
+        [((4, BU, 8 * BU), bf16), ((4, PB, 3 * BU), bf16), ((RP, 3 * RP), bf16)], [],
+    )
 
     (packed,) = call(
         pack_kernel, [variant], [fu_in, fp_in, mask_in],
@@ -354,6 +412,9 @@
         [((YL, BLOCKS, LANES, LANES), f32)],
     )
     got = lax.all_to_all(packed, PLANE, 0, 0, tiled=True)
+    got, table, pair, matrix, coefs, layers = lax.optimization_barrier(
+        (got, table, pair, matrix, coefs, layers)
+    )
     fu, fp, mask, send = call(
         spread_kernel, [coefs], [got.reshape(CH * BLOCKS * 8, LANES)],
         [((RU, LANES), f32), ((RP, LANES), f32), ((NZ, LANES), f32), ((RU + NZ, LANES), bf16)],
@@ -366,7 +427,7 @@
     ] * 2
     ru, du, dp, q, send2 = call(
         first_kernel, [coefs, layers],
-        [table, bcoup, coup_t, matrix, fu, fp, mask, send, low, high],
+        [table, pair, matrix, fu, fp, mask, send, low, high],
         [((RU, LANES), f32), ((RU, LANES), f32), ((RP, LANES), f32), ((RP, LANES), f32),
          ((RU, LANES), bf16)],
         wide,
@@ -375,7 +436,7 @@
     high2 = lax.ppermute(send2, ALL, down)
     (back,) = call(
         second_kernel, [coefs, layers],
-        [table, bcoup, matrix, fu, mask, ru, du, dp, q, send2, low2, high2, low, high],
+        [table, pair, matrix, fu, mask, ru, du, dp, q, send2, low2, high2, low, high],
         [((CH * BLOCKS * 8, LANES), bf16)],
         wide + [((RP, LANES), f32), ((BLOCKS, LANES, LANES), f32),
                 ((CH * BLOCKS * 8, LANES), f32)],

time: 131 us -> 96.8 us (0.74)
  Pallas kernels: 50.7 us -> 18.8 us
  local copies, waits for them, and re-layouts: 12.5 us -> 5.79 us
  blocking collectives: 20.5 us -> 22.9 us
  starting transfers between devices: 23.5 us -> 25.3 us
    pallas_call x5 -> x6, Pallas kernels: 50.7 us -> 18.8 us  [call(): pl.pallas_call(kernel, out_shape=[jax.ShapeDtypeStruct(*o) for o in outs]...]
    all_to_all x1, waiting for transfers between devices: 8.3 us -> 3.94 us  [body(): got = lax.all_to_all(packed, PLANE, 0, 0, tiled=True)]
    unnamed x27 -> x22, local copies, waits for them, and re-layouts: 6.8 us -> 2.67 us
    ppermute x1, waiting for transfers between devices: 0.01 us -> 3.87 us  [body(): other = lax.ppermute(layer_mats, 'gz', [(0, 1), (1, 0)])]
    all_to_all x1, blocking collectives: 20.5 us -> 22.9 us  [body(): lax.all_to_all(back.reshape(CH * BLOCKS, 8, LANES), PLANE, 0, 0, tiled=True)]
    another operation x2 -> x0, local copies, waits for them, and re-layouts: 1.97 us -> none  [body(): jnp.stack([kblocks[:, d] for d in (1, 0, 2, 3, 4, 5, 6)], axis=2)]
    ppermute x1, waiting for transfers between devices: 0.56 us -> 2.45 us  [body(): high = lax.ppermute(send, ALL, down)]
    ppermute x1, waiting for transfers between devices: 0.01 us -> 1.46 us  [body(): low = lax.ppermute(send, ALL, up)]
  transfers between devices with their start and end apart: 6 -> 6, of which waited for: 4 -> 6; matrix products, arithmetic and copies ran while one was open for 11% -> 7% of each run, Pallas kernels for 4% -> 0%
where the time goes in v2:
time: 96.8 us; the launch traced here: 96.2 us
  starting transfers between devices  25.3 us (26%)
  blocking collectives  22.9 us (24%)
  Pallas kernels  18.8 us (19%)
  waiting for transfers between devices  15.6 us (16%)
  local copies, waits for them, and re-layouts  5.79 us (6%)
  other arithmetic  4.01 us (4%)
  between operations  3.79 us (4%)
    all_to_all x1, blocking collectives, body(): lax.all_to_all(back.reshape(CH * BLOCKS, 8, LANES), PLANE, 0, 0, tiled=True)  22.9 us
    pallas_call x6, Pallas kernels, call(): pl.pallas_call(kernel, out_shape=[jax.ShapeDtypeStruct(*o) for o in outs]...  18.8 us
    all_to_all x1, starting transfers between devices, body(): got = lax.all_to_all(packed, PLANE, 0, 0, tiled=True)  11.3 us
    ppermute x1, starting transfers between devices, body(): low2 = lax.ppermute(send2, ALL, up)  4.39 us
    all_to_all x1, waiting for transfers between devices, body(): got = lax.all_to_all(packed, PLANE, 0, 0, tiled=True)  3.94 us
    ppermute x1, starting transfers between devices, body(): low = lax.ppermute(send, ALL, up)  3.92 us
    ppermute x1, waiting for transfers between devices, body(): other = lax.ppermute(layer_mats, 'gz', [(0, 1), (1, 0)])  3.87 us
    reduce_sum x1, other arithmetic, schur_matrix(): return jnp.sum(picked, axis=0).reshape(RP, RP)  3.78 us
  transfers between devices with their start and end apart: 6, of which 6 were waited for; matrix products, arithmetic and copies ran while one was open for 7% of the time, Pallas kernels for 0%

profile of v2, /device:TPU:16, one launch (start us, length us, event | category | flops | bytes accessed | tf_op | source)
XLA Modules:
  0.0 96.2 jit_solution(14797254629129162442)
XLA Ops:
  0.7 0.0 copy-start
  0.7 1.0 %copy-done = f32[8,64,2,128]{3,2,1,0:T(2,128)S(1)} copy-done((f32[8,64,2,128]{3,2,1,0:T(2,128)S(1)}, f32[8,64,2,128]{3,2,1,0:T(2,128)}, u32[]{:S(2)}) %copy-start) | copy-done | bytes 524312
  1.7 0.9 copy-done.3
  2.6 0.7 copy-done.4
  3.3 1.1 %shard_map.104 = f32[160,8,128]{2,1,0:T(8,128)} custom-call(s32[1]{0:T(128)} %bitcast.var_ref, f32[1024,128]{1,0:T(8,128)S(1)} %bitcast.20, f32[256,128]{1,0:T(8,128)S(1)} %bitcast.23, s32[16,128]{1,0:T(8,128)S(1)} %bitcast.24), custom_call_target="tpu_custom_call" | custom-call | tf_op jit(solution)/shard_map/pallas_call | solution.py:361
  4.5 11.3 %all-to-all-start = ((f32[160,8,128]{2,1,0:T(8,128)}), f32[160,8,128]{2,1,0:T(8,128)S(1)}, u32[]{:S(2)}, u32[]{:S(2)}) async-start(f32[160,8,128]{2,1,0:T(8,128)} %shard_map.104), calls=%async_computation | async-start | bytes 1310720 | tf_op jit(solution)/shard_map/all_to_all | solution.py:414
  15.8 1.9 %collective-permute-start = (s32[8]{0:T(128)S(1)}, s32[8]{0:T(128)S(1)}, u32[]{:S(2)}, u32[]{:S(2)}) collective-permute-start(s32[8]{0:T(128)S(1)} %copy-done.10), channel_id=1, source_target_pairs={{0,1},{1,0},{2,3},{3,2},{4,5},{5,4},{6,7},{7,6},{8,9},{9,8},{10,11... | collective-permute-start | bytes 104 | tf_op jit(solution)/shard_map/ppermute | solution.py:394
  17.7 0.6 fusion
  21.2 0.1 iota_add_fusion
  21.3 0.1 iota_compare_fusion
  21.4 0.0 copy-start.2
  21.4 0.0 copy-start.6
  21.4 3.8 %select_reduce_fusion = f32[16,16,16,16]{3,2,1,0:T(8,128)} fusion(f32[8,16,16,16]{3,2,1,0:T(8,128)S(1)} %copy-done.7, pred[8,16,16]{2,1,0:T(8,128)(4,1)S(1)} %iota_compare_fusion), kind=kLoop, calls=%fused_computation | loop fusion | flops 983040 | bytes 395264 | tf_op jit(solution)/shard_map/reduce_sum | solution.py:389
  25.2 2.4 %reshape.67.schur_ref = f32[256,256]{1,0:T(8,128)S(1)} reshape(f32[16,16,16,16]{3,2,1,0:T(8,128)} %select_reduce_fusion) | data formatting | bytes 524288 | tf_op jit(solution)/shard_map/reshape | solution.py:389
  27.7 0.2 shard_map.105
  27.9 0.1 stack.32.coef_ref
  28.0 3.9 %collective-permute-done = s32[8]{0:T(128)S(1)} collective-permute-done((s32[8]{0:T(128)S(1)}, s32[8]{0:T(128)S(1)}, u32[]{:S(2)}, u32[]{:S(2)}) %collective-permute-start) | collective-permute-done | bytes 64 | tf_op jit(solution)/shard_map/ppermute | solution.py:394
  31.9 0.1 broadcast_select_fusion.lm_ref
  32.0 3.9 %all-to-all-done = f32[160,8,128]{2,1,0:T(8,128)S(1)} async-done(((f32[160,8,128]{2,1,0:T(8,128)}), f32[160,8,128]{2,1,0:T(8,128)S(1)}, u32[]{:S(2)}, u32[]{:S(2)}) %all-to-all-start) | async-done | bytes 655392 | tf_op jit(solution)/shard_map/all_to_all | solution.py:414
  35.9 1.0 shard_map.106
  36.9 1.9 %collective-permute-start.2 = (bf16[1040,128]{1,0:T(8,128)(2,1)S(1)}, bf16[1040,128]{1,0:T(8,128)(2,1)S(1)}, u32[]{:S(2)}, u32[]{:S(2)}) collective-permute-start(bf16[1040,128]{1,0:T(8,128)(2,1)S(1)} %get-tuple-element.34.own_ref), channel_id=1, source_target_pairs={{1,0},{2,1},{3,2},{4,3},{5,4},{6,5},{7,6},{15,7},{14,15},{13,14},{... | collective-permute-start | bytes 798728 | tf_op jit(solution)/shard_map/ppermute | solution.py:424
  38.8 3.9 %collective-permute-start.1 = (bf16[1040,128]{1,0:T(8,128)(2,1)S(1)}, bf16[1040,128]{1,0:T(8,128)(2,1)S(1)}, u32[]{:S(2)}, u32[]{:S(2)}) collective-permute-start(bf16[1040,128]{1,0:T(8,128)(2,1)S(1)} %get-tuple-element.34.own_ref), channel_id=1, source_target_pairs={{0,1},{1,2},{2,3},{3,4},{4,5},{5,6},{6,7},{7,15},{15,14},{14,13},{... | collective-permute-start | bytes 798728 | tf_op jit(solution)/shard_map/ppermute | solution.py:423
  42.7 2.5 %collective-permute-done.2.high_ref.mhigh_ref = bf16[1040,128]{1,0:T(8,128)(2,1)S(1)} collective-permute-done((bf16[1040,128]{1,0:T(8,128)(2,1)S(1)}, bf16[1040,128]{1,0:T(8,128)(2,1)S(1)}, u32[]{:S(2)}, u32[]{:S(2)}) %collective-permute-start.2) | collective-permute-done | bytes 266272 | tf_op jit(solution)/shard_map/ppermute | solution.py:424
  45.2 1.5 %collective-permute-done.1.low_ref.mlow_ref = bf16[1040,128]{1,0:T(8,128)(2,1)S(1)} collective-permute-done((bf16[1040,128]{1,0:T(8,128)(2,1)S(1)}, bf16[1040,128]{1,0:T(8,128)(2,1)S(1)}, u32[]{:S(2)}, u32[]{:S(2)}) %collective-permute-start.1) | collective-permute-done | bytes 266272 | tf_op jit(solution)/shard_map/ppermute | solution.py:423
  46.6 8.5 %shard_map.107 = (f32[1024,128]{1,0:T(8,128)S(1)}, f32[1024,128]{1,0:T(8,128)S(1)}, f32[256,128]{1,0:T(8,128)S(1)}, f32[256,128]{1,0:T(8,128)S(1)}, bf16[1024,128]{1,0:T(8,128)(2,1)S(1)}) custom-call(f32[8]{0:T(128)S(1)} %stack.32.coef_ref, s32[16]{0:T(128)S(1)} %broadcast_select_fusion.lm_ref, bf16[4,64,512]{2,1,0:T(8,128)(2,1)S(1)} %get-tuple-element.27.table_ref, ...), custom_call_target="tpu_custom_call" | custom-call | tf_op jit(solution)/shard_map/pallas_call | solution.py:361
  55.1 1.9 %collective-permute-start.4 = (bf16[1024,128]{1,0:T(8,128)(2,1)S(1)}, bf16[1024,128]{1,0:T(8,128)(2,1)S(1)}, u32[]{:S(2)}, u32[]{:S(2)}) collective-permute-start(bf16[1024,128]{1,0:T(8,128)(2,1)S(1)} %get-tuple-element.39.own_ref), channel_id=1, source_target_pairs={{1,0},{2,1},{3,2},{4,3},{5,4},{6,5},{7,6},{15,7},{14,15},{13,14},{... | collective-permute-start | bytes 786440 | tf_op jit(solution)/shard_map/ppermute | solution.py:436
  57.1 4.4 %collective-permute-start.3 = (bf16[1024,128]{1,0:T(8,128)(2,1)S(1)}, bf16[1024,128]{1,0:T(8,128)(2,1)S(1)}, u32[]{:S(2)}, u32[]{:S(2)}) collective-permute-start(bf16[1024,128]{1,0:T(8,128)(2,1)S(1)} %get-tuple-element.39.own_ref), channel_id=1, source_target_pairs={{0,1},{1,2},{2,3},{3,4},{4,5},{5,6},{6,7},{7,15},{15,14},{14,13},{... | collective-permute-start | bytes 786440 | tf_op jit(solution)/shard_map/ppermute | solution.py:435
  61.5 2.4 %collective-permute-done.4.high_ref = bf16[1024,128]{1,0:T(8,128)(2,1)S(1)} collective-permute-done((bf16[1024,128]{1,0:T(8,128)(2,1)S(1)}, bf16[1024,128]{1,0:T(8,128)(2,1)S(1)}, u32[]{:S(2)}, u32[]{:S(2)}) %collective-permute-start.4) | collective-permute-done | bytes 262176 | tf_op jit(solution)/shard_map/ppermute | solution.py:436
  63.9 1.5 %collective-permute-done.3.low_ref = bf16[1024,128]{1,0:T(8,128)(2,1)S(1)} collective-permute-done((bf16[1024,128]{1,0:T(8,128)(2,1)S(1)}, bf16[1024,128]{1,0:T(8,128)(2,1)S(1)}, u32[]{:S(2)}, u32[]{:S(2)}) %collective-permute-start.3) | collective-permute-done | bytes 262176 | tf_op jit(solution)/shard_map/ppermute | solution.py:435
  65.3 6.9 %shard_map.108 = bf16[1280,128]{1,0:T(8,128)(2,1)S(1)} custom-call(f32[8]{0:T(128)S(1)} %stack.32.coef_ref, s32[16]{0:T(128)S(1)} %broadcast_select_fusion.lm_ref, bf16[4,64,512]{2,1,0:T(8,128)(2,1)S(1)} %get-tuple-element.27.table_ref, bf16[4,16,192]{2,1,0:T(8,128)(2,1)S(1)} %get-tuple-element.28.coup_ref, ...), custom_call_target="tpu_custom_call" | custom-call | tf_op jit(solution)/shard_map/pallas_call | solution.py:361
  72.2 22.9 %all_to_all.10.got_ref = bf16[160,8,128]{2,1,0:T(8,128)(2,1)S(1)} all-to-all(bf16[160,8,128]{2,1,0:T(8,128)(2,1)S(1)} %bitcast.22), channel_id=1, replica_groups=mesh['gx'=8,'gy'=16,'gz'=2] {'gy','gz'}, dimensions={0} | all-to-all | bytes 655360 | tf_op jit(solution)/shard_map/all_to_all | solution.py:444
  95.1 1.1 %shard_map.109 = (f32[1024,128]{1,0:T(8,128)}, f32[256,128]{1,0:T(8,128)}) custom-call(s32[1]{0:T(128)} %bitcast.var_ref, bf16[160,8,128]{2,1,0:T(8,128)(2,1)S(1)} %all_to_all.10.got_ref, f32[1024,128]{1,0:T(8,128)S(1)} %bitcast.21, s32[16,128]{1,0:T(8,128)S(1)} %bitcast.25), custom_call_target="tpu_custom_call" | custom-call | tf_op jit(solution)/shard_map/pallas_call | solution.py:361
  (16 shorter events, 0.0 us)
Async XLA Ops:
  0.6 15.1 %copy-start.10 = (s32[8]{0:T(128)S(1)}, s32[8]{0:T(128)}, u32[]{:S(2)}) copy-start(s32[8]{0:T(128)} %param.12) | copy-start | bytes 100
  0.6 17.0 %copy-start.8 = (f32[2]{0:T(128)S(1)}, f32[2]{0:T(128)}, u32[]{:S(2)}) copy-start(f32[2]{0:T(128)} %param.17) | copy-start | bytes 28
  0.7 20.6 %copy-start.9 = (s32[8]{0:T(128)S(1)}, s32[8]{0:T(128)}, u32[]{:S(2)}) copy-start(s32[8]{0:T(128)} %param.16) | copy-start | bytes 100
  0.7 1.0 %copy-start = (f32[8,64,2,128]{3,2,1,0:T(2,128)S(1)}, f32[8,64,2,128]{3,2,1,0:T(2,128)}, u32[]{:S(2)}) copy-start(f32[8,64,2,128]{3,2,1,0:T(2,128)} %param.9) | copy-start | bytes 1572868
  1.7 0.9 copy-start.3
  2.6 0.7 copy-start.4
  3.3 18.1 %copy-start.7 = (f32[8,16,16,16]{3,2,1,0:T(8,128)S(1)}, f32[8,16,16,16]{3,2,1,0:T(8,128)}, u32[]{:S(2)}) copy-start(f32[8,16,16,16]{3,2,1,0:T(8,128)} %param.15) | copy-start | bytes 393220
  4.5 31.5 %all-to-all-start = ((f32[160,8,128]{2,1,0:T(8,128)}), f32[160,8,128]{2,1,0:T(8,128)S(1)}, u32[]{:S(2)}, u32[]{:S(2)}) async-start(f32[160,8,128]{2,1,0:T(8,128)} %shard_map.104), calls=%async_computation | async-start | bytes 1310720 | tf_op jit(solution)/shard_map/all_to_all | solution.py:414
  15.8 16.1 %collective-permute-start = (s32[8]{0:T(128)S(1)}, s32[8]{0:T(128)S(1)}, u32[]{:S(2)}, u32[]{:S(2)}) collective-permute-start(s32[8]{0:T(128)S(1)} %copy-done.10), channel_id=1, source_target_pairs={{0,1},{1,0},{2,3},{3,2},{4,5},{5,4},{6,7},{7,6},{8,9},{9,8},{10,11... | collective-permute-start | bytes 104 | tf_op jit(solution)/shard_map/ppermute | solution.py:394
  21.4 6.3 %copy-start.2 = (bf16[4,7,64,64]{3,2,1,0:T(8,128)(2,1)S(1)}, bf16[4,7,64,64]{3,2,1,0:T(8,128)(2,1)}, u32[]{:S(2)}) copy-start(bf16[4,7,64,64]{3,2,1,0:T(8,128)(2,1)} %kb_ref.1) | copy-start | bytes 688132
  21.4 6.3 %copy-start.6 = (f32[4,16,64]{2,1,0:T(8,128)S(1)}, f32[4,16,64]{2,1,0:T(8,128)}, u32[]{:S(2)}) copy-start(f32[4,16,64]{2,1,0:T(8,128)} %coup_ref.1) | copy-start | bytes 49156
  36.9 8.3 %collective-permute-start.2 = (bf16[1040,128]{1,0:T(8,128)(2,1)S(1)}, bf16[1040,128]{1,0:T(8,128)(2,1)S(1)}, u32[]{:S(2)}, u32[]{:S(2)}) collective-permute-start(bf16[1040,128]{1,0:T(8,128)(2,1)S(1)} %get-tuple-element.34.own_ref), channel_id=1, source_target_pairs={{1,0},{2,1},{3,2},{4,3},{5,4},{6,5},{7,6},{15,7},{14,15},{13,14},{... | collective-permute-start | bytes 798728 | tf_op jit(solution)/shard_map/ppermute | solution.py:424
  38.8 7.8 %collective-permute-start.1 = (bf16[1040,128]{1,0:T(8,128)(2,1)S(1)}, bf16[1040,128]{1,0:T(8,128)(2,1)S(1)}, u32[]{:S(2)}, u32[]{:S(2)}) collective-permute-start(bf16[1040,128]{1,0:T(8,128)(2,1)S(1)} %get-tuple-element.34.own_ref), channel_id=1, source_target_pairs={{0,1},{1,2},{2,3},{3,4},{4,5},{5,6},{6,7},{7,15},{15,14},{14,13},{... | collective-permute-start | bytes 798728 | tf_op jit(solution)/shard_map/ppermute | solution.py:423
  55.1 8.7 %collective-permute-start.4 = (bf16[1024,128]{1,0:T(8,128)(2,1)S(1)}, bf16[1024,128]{1,0:T(8,128)(2,1)S(1)}, u32[]{:S(2)}, u32[]{:S(2)}) collective-permute-start(bf16[1024,128]{1,0:T(8,128)(2,1)S(1)} %get-tuple-element.39.own_ref), channel_id=1, source_target_pairs={{1,0},{2,1},{3,2},{4,3},{5,4},{6,5},{7,6},{15,7},{14,15},{13,14},{... | collective-permute-start | bytes 786440 | tf_op jit(solution)/shard_map/ppermute | solution.py:436
  57.1 8.3 %collective-permute-start.3 = (bf16[1024,128]{1,0:T(8,128)(2,1)S(1)}, bf16[1024,128]{1,0:T(8,128)(2,1)S(1)}, u32[]{:S(2)}, u32[]{:S(2)}) collective-permute-start(bf16[1024,128]{1,0:T(8,128)(2,1)S(1)} %get-tuple-element.39.own_ref), channel_id=1, source_target_pairs={{0,1},{1,2},{2,3},{3,4},{4,5},{5,6},{6,7},{7,15},{15,14},{14,13},{... | collective-permute-start | bytes 786440 | tf_op jit(solution)/shard_map/ppermute | solution.py:435
  65.3 29.8 %copy-start.1 = (f32[8,64,2,128]{3,2,1,0:T(2,128)S(1)}, f32[8,64,2,128]{3,2,1,0:T(2,128)}, u32[]{:S(2)}) copy-start(f32[8,64,2,128]{3,2,1,0:T(2,128)} %param.9) | copy-start | bytes 1572868
  65.3 29.8 %copy-start.5 = (s32[8,2,128]{2,1,0:T(2,128)S(1)}, s32[8,2,128]{2,1,0:T(2,128)}, u32[]{:S(2)}) copy-start(s32[8,2,128]{2,1,0:T(2,128)} %param.11) | copy-start | bytes 24580

commit v3 on v2

v3 whole, which is shorter than its diff:
```python
import jax
import jax.numpy as jnp
from jax import lax
from jax.experimental import pallas as pl
from jax.experimental.pallas import tpu as pltpu
from jax.sharding import PartitionSpec as P

SWEEPS = 4
ALL = ("gx", "gy", "gz")
PLANE = ("gy", "gz")
HIGHEST = lax.Precision.HIGHEST
NZ, BU, PB, NY = 16, 64, 16, 32
ZL, YL, XL, CH = 8, 2, 4, 32
RU, RP = NZ * BU, NZ * PB
HU, HP = ZL * BU, ZL * PB
WIDE = HU + HP
LANES = 128
BLOCKS = WIDE // LANES
STEP = 2 * BLOCKS * 8
UNROLL = 8
f32, bf16 = jnp.float32, jnp.bfloat16


def place(variant, k):
    if variant == 0:
        cx, r = k // 8, k % 8
        cz = r if cx % 2 == 0 else 7 - r
    elif variant == 1:
        cz, r = k // 4, k % 4
        cx = 3 - r if cz % 2 == 0 else r
    elif variant == 2:
        q, r = k // 8, k % 8
        cx = 3 - q
        cz = 7 - r if q % 2 == 0 else r
    else:
        q, r = k // 4, k % 4
        cz = 7 - q
        cx = r if q % 2 == 0 else 3 - r
    return cx * 8 + cz


def slot_of(variant, k):
    a, b, c, d = (place(v, k) for v in range(4))
    return jnp.where(
        variant < 2, jnp.where(variant == 0, a, b), jnp.where(variant == 2, c, d)
    )


def chain():
    order = [g * CH + place(g % 4, k) for g in range(8) for k in range(CH)]
    up = [(order[i], order[i + 1]) for i in range(len(order) - 1)]
    return up, [(b, a) for a, b in up]


def pack_kernel(var_ref, fu_ref, fp_ref, mask_ref, out_ref, flip_ref):
    for yl in range(YL):
        pressure = []
        for z in range(ZL):
            live = mask_ref[pl.ds(z * YL + yl, 1), :] != 0
            weight = live.astype(f32)
            fp = fp_ref[pl.ds(z * PB * YL + yl, PB, stride=YL), :] * weight
            last = lax.broadcasted_iota(jnp.int32, (PB, LANES), 0) == PB - 1
            dead = jnp.broadcast_to(weight, (PB, LANES)) == 0.0
            pressure.append(jnp.where(jnp.logical_and(last, dead), jnp.inf, fp))
        for b in range(BLOCKS - 1):
            pair = []
            for z in (2 * b, 2 * b + 1):
                weight = (mask_ref[pl.ds(z * YL + yl, 1), :] != 0).astype(f32)
                pair.append(fu_ref[pl.ds(z * BU * YL + yl, BU, stride=YL), :] * weight)
            flip_ref[yl, b] = jnp.concatenate(pair, axis=0).T
        flip_ref[yl, BLOCKS - 1] = jnp.concatenate(pressure, axis=0).T
    variant = var_ref[0]
    for k in range(CH):
        dest = slot_of(variant, k) * BLOCKS
        for b in range(BLOCKS):
            out_ref[dest + b] = jnp.concatenate(
                [flip_ref[yl, b, pl.ds(XL * k, XL), :] for yl in range(YL)], axis=0
            )


def spread_kernel(coef_ref, got_ref, fu_ref, fp_ref, mask_ref, send_ref, rows_ref):
    theta_inv = coef_ref[pl.ds(0, 1), pl.ds(0, LANES)]
    for half in range(2):
        for b in range(BLOCKS):
            for x in range(XL):
                for yl in range(YL):
                    rows_ref[b, pl.ds(x * NY + yl, CH // 2, stride=YL), :] = got_ref[
                        pl.ds((half * BLOCKS + b) * 8 + yl * XL + x, CH // 2, stride=STEP), :
                    ]
            flat = rows_ref[b].T
            if b < BLOCKS - 1:
                at = pl.ds(half * HU + b * LANES, LANES)
                fu_ref[at, :] = flat
                send_ref[at, :] = (flat * theta_inv).astype(bf16)
            else:
                fp_ref[pl.ds(half * HP, HP), :] = flat
    marks = fp_ref[pl.ds(PB - 1, NZ, stride=PB), :]
    weight = jnp.where(marks == jnp.inf, 0.0, 1.0)
    mask_ref[...] = weight
    send_ref[pl.ds(RU, NZ), :] = weight.astype(bf16)
    fp_ref[...] = jnp.where(fp_ref[...] == jnp.inf, 0.0, fp_ref[...])


LOW, HIGH, OWN, EDGE = 0, 1, 2, 3
WIDTH = 4 * LANES


def block(b, count=1):
    return pl.ds(b * LANES, count * LANES)


def lane_of(rows):
    return lax.broadcasted_iota(jnp.int32, (rows, LANES), 1)


def edge_of(low, high):
    return jnp.where(lane_of(low.shape[0]) < LANES // 2, high, low)


def stack_of(z64, w_ref, mode):
    lane = lane_of(BU)
    y = lane % NY
    ins = {"wide": (LOW, HIGH, OWN), "shrink": (LOW, HIGH, OWN), "ring": (OWN, EDGE),
           "own": (OWN, EDGE)}[mode]
    outs = {"wide": (LOW, HIGH, OWN), "shrink": (OWN, EDGE), "ring": (OWN, EDGE),
            "own": (OWN,)}[mode]
    rows = pl.ds(z64 + BU, BU)
    part = {b: w_ref[rows, block(b)] for b in sorted(set(ins) | set(outs))}
    up = {b: pltpu.roll(part[b], NY, 1) for b in ins}
    down = {b: pltpu.roll(part[b], LANES - NY, 1) for b in ins}
    zero = jnp.zeros_like(part[OWN])
    first, half, tail = lane < NY, lane < LANES // 2, lane >= LANES - NY
    if mode in ("wide", "shrink"):
        below = {LOW: up[LOW], OWN: jnp.where(first, up[LOW], up[OWN])}
        above = {HIGH: down[HIGH], OWN: jnp.where(tail, down[HIGH], down[OWN])}
        if mode == "wide":
            below[HIGH] = jnp.where(first, up[OWN], up[HIGH])
            above[LOW] = jnp.where(tail, down[OWN], down[LOW])
        else:
            below[EDGE] = jnp.where(first, up[OWN], jnp.where(half, up[HIGH], up[LOW]))
            above[EDGE] = jnp.where(tail, down[OWN], jnp.where(half, down[HIGH], down[LOW]))
    else:
        below = {OWN: jnp.where(first, up[EDGE], up[OWN]), EDGE: jnp.where(first, up[OWN], up[EDGE])}
        above = {OWN: jnp.where(tail, down[EDGE], down[OWN]),
                 EDGE: jnp.where(tail, down[OWN], down[EDGE])}
    columns = []
    for b in outs:
        below_y = jnp.where(y == 0, zero, pltpu.roll(part[b], 1, 1))
        above_y = jnp.where(y == NY - 1, zero, pltpu.roll(part[b], LANES - 1, 1))
        columns.append(jnp.concatenate([below_y, above_y, below[b], above[b]], axis=0))
    depth = w_ref[pl.ds(z64, 3 * BU), block(outs[0], len(outs))]
    return [jnp.concatenate(columns, axis=1), depth]


def layers_of(group):
    return [group * UNROLL + i for i in range(UNROLL)]


def sweep(k, mode, begin, last, refs, old, new):
    coef_ref, lm_ref, table_ref, mask_ref, state = refs
    count = {"wide": 3, "own": 1}.get(mode, 2)
    lanes = block(LOW if mode == "wide" else OWN, count)
    inner = block(0, min(count, 2))
    keep = coef_ref[pl.ds(2 + 2 * k, 1), block(0, count)]
    scale = coef_ref[pl.ds(3 + 2 * k, 1), block(0, count)]

    def group(g, carry):
        for z in layers_of(g):
            z64 = pl.multiple_of(z * BU, BU)
            table = table_ref[lm_ref[z]]
            stack = jnp.concatenate(stack_of(z64, old, mode), axis=0)
            product = jnp.dot(table[:, : 7 * BU], stack, preferred_element_type=f32)
            rows = pl.ds(z64, BU)
            if begin is None:
                r, d, s = [ref[rows, inner] for ref in state]
            else:
                r, d = begin(rows)
                s = d
            r = r - product * mask_ref[z, pl.ds(0, 1), lanes]
            d = keep * d + scale * r
            s = s + d
            if last is not None:
                last(z64, s)
                continue
            here = pl.ds(z64 + BU, BU)
            if mode == "wide":
                w = d.astype(bf16)
                new[here, block(LOW, 3)] = w
                new[here, block(EDGE)] = edge_of(w[:, :LANES], w[:, LANES : 2 * LANES])
                for ref, v in zip(state, (r, d, s)):
                    ref[rows, block(0)] = v[:, 2 * LANES :]
                    ref[rows, block(1)] = edge_of(v[:, :LANES], v[:, LANES : 2 * LANES])
            else:
                new[here, lanes] = d.astype(bf16)
                for ref, v in zip(state, (r, d, s)):
                    ref[rows, inner] = v
        return carry

    lax.fori_loop(0, NZ // UNROLL, group, 0)


def starter(coef_ref, own_ref, low_ref, high_ref, wide):
    theta_inv = coef_ref[pl.ds(0, 1), block(0)]
    theta = coef_ref[pl.ds(1, 1), block(0)]

    def begin(rows):
        r = own_ref[rows, :]
        d = r * theta_inv
        low = low_ref[rows, :].astype(f32)
        high = high_ref[rows, :].astype(f32)
        if wide:
            return (
                jnp.concatenate([low * theta, high * theta, r], axis=1),
                jnp.concatenate([low, high, d], axis=1),
            )
        edge = edge_of(low, high)
        return (
            jnp.concatenate([r, edge * theta], axis=1),
            jnp.concatenate([d, edge], axis=1),
        )

    return begin


def widen(wide_ref, mask_ref, low_ref, high_ref):
    low = low_ref[pl.ds(RU, NZ), :].astype(f32)
    high = high_ref[pl.ds(RU, NZ), :].astype(f32)
    whole = jnp.concatenate([low, high, mask_ref[...], edge_of(low, high)], axis=1)
    for z in range(NZ):
        wide_ref[z] = jnp.broadcast_to(whole[z : z + 1], (8, WIDTH))


def pad_in(w_refs, low_ref, high_ref, own_ref, with_edge):
    edge = jnp.zeros((BU, WIDTH), bf16)
    for w_ref in w_refs:
        w_ref[pl.ds(0, BU), :] = edge
        w_ref[pl.ds(RU + BU, BU), :] = edge
    for b, src in ((LOW, low_ref), (HIGH, high_ref), (OWN, own_ref)):
        w_refs[0][pl.ds(BU, RU), block(b)] = src[pl.ds(0, RU), :]
    if with_edge:
        w_refs[0][pl.ds(BU, RU), block(EDGE)] = edge_of(
            low_ref[pl.ds(0, RU), :], high_ref[pl.ds(0, RU), :]
        )


def thirds(v):
    high = v.astype(bf16)
    low = (v - high.astype(f32)).astype(bf16)
    return [high, low, high]


def halves(v):
    high = v.astype(bf16)
    return high, (v - high.astype(f32)).astype(bf16)


def couple(get, lm_ref, coup_ref, mask_ref, rest_ref, sign, q_ref):
    def group(g, carry):
        for z in layers_of(g):
            here = pl.ds(pl.multiple_of(z * PB, PB), PB)
            du = get(pl.multiple_of(z * BU, BU))
            q = jnp.dot(coup_ref[lm_ref[z]], jnp.concatenate(thirds(du), axis=0),
                        preferred_element_type=f32)
            q_ref[here, :] = q * mask_ref[z, pl.ds(0, 1), block(OWN)] + sign * rest_ref[here, :]
        return carry

    lax.fori_loop(0, NZ // UNROLL, group, 0)


def bands(schur_ref, q_ref):
    return jnp.dot(schur_ref[...], jnp.concatenate(thirds(q_ref[...]), axis=0),
                   preferred_element_type=f32)


def prep_kernel(spec_ref, off_ref, kb_ref, coup_ref, sinv_ref,
                coef_ref, table_ref, pair_ref, band_ref):
    lower = jnp.full((1, WIDTH), spec_ref[0], f32)
    upper = jnp.full((1, WIDTH), spec_ref[1], f32)
    theta = (upper + lower) / 2.0
    delta = (upper - lower) / 2.0
    sigma = theta / delta
    rho = 1.0 / sigma
    coef_ref[pl.ds(0, 1), :] = 1.0 / theta
    coef_ref[pl.ds(1, 1), :] = theta
    for k in range(SWEEPS - 1):
        rho_next = 1.0 / (2.0 * sigma - rho)
        coef_ref[pl.ds(2 + 2 * k, 1), :] = rho_next * rho
        coef_ref[pl.ds(3 + 2 * k, 1), :] = 2.0 * rho_next / delta
        rho = rho_next
    for m in range(4):
        high, low = halves(coup_ref[m])
        pair_ref[m] = jnp.concatenate([high, high, low], axis=1)
        high, low = halves(coup_ref[m].T)
        blocks = [kb_ref[m, d] for d in (3, 4, 5, 6, 1, 0, 2)]
        pad = jnp.zeros((BU, PB), bf16)
        table_ref[m] = jnp.concatenate(blocks + [high, high, low, pad], axis=1)
    row = lax.broadcasted_iota(jnp.int32, (PB, RP), 0)
    col = lax.broadcasted_iota(jnp.int32, (PB, RP), 1)
    spread = (col % PB == row).astype(f32).astype(bf16)
    gap = (lax.broadcasted_iota(jnp.int32, (RP, RP), 1) // PB
           - lax.broadcasted_iota(jnp.int32, (RP, RP), 0) // PB)
    total = [jnp.zeros((RP, RP), f32)] * 2
    for k in range(8):
        hit = gap == off_ref[k]
        for i, part in enumerate(halves(sinv_ref[k].reshape(RP, PB))):
            wide = jnp.dot(part, spread, preferred_element_type=f32)
            total[i] = total[i] + jnp.where(hit, wide, 0.0)
    high, low = total[0].astype(bf16), total[1].astype(bf16)
    band_ref[...] = jnp.concatenate([high, high, low], axis=1)


def first_kernel(lm_ref, coef_ref, table_ref, coup_ref, schur_ref,
                 fu_ref, fp_ref, mask_ref, own_ref, low_ref, high_ref,
                 ru_ref, du_ref, dp_ref, q_ref, send_ref,
                 wide_ref, d_ref, r_ref, s_ref, wa_ref, wb_ref):
    widen(wide_ref, mask_ref, low_ref, high_ref)
    pad_in((wa_ref, wb_ref), low_ref, high_ref, own_ref, False)
    refs = (coef_ref, lm_ref, table_ref, wide_ref, (r_ref, d_ref, s_ref))
    begin = starter(coef_ref, fu_ref, low_ref, high_ref, True)

    def last(z64, s):
        wb_ref[pl.ds(z64 + BU, BU), block(OWN, 2)] = s.astype(bf16)
        du_ref[pl.ds(z64, BU), :] = s[:, :LANES]

    sweep(0, "wide", begin, None, refs, wa_ref, wb_ref)
    sweep(1, "shrink", None, None, refs, wb_ref, wa_ref)
    sweep(2, "ring", None, last, refs, wa_ref, wb_ref)
    couple(lambda z64: du_ref[pl.ds(z64, BU), :], lm_ref, coup_ref, wide_ref, fp_ref, -1.0, q_ref)
    dp_ref[...] = bands(schur_ref, q_ref)
    theta_inv = coef_ref[pl.ds(0, 1), block(0)]

    def finish(g, carry):
        for z in layers_of(g):
            z64 = pl.multiple_of(z * BU, BU)
            here = pl.ds(pl.multiple_of(z * PB, PB), PB)
            weight = wide_ref[z, pl.ds(0, 1), block(OWN)]
            dp = dp_ref[here, :] * weight
            dp_ref[here, :] = dp
            stack = stack_of(z64, wb_ref, "own") + thirds(dp)
            product = jnp.dot(table_ref[lm_ref[z]][:, : 7 * BU + 3 * PB],
                              jnp.concatenate(stack, axis=0), preferred_element_type=f32)
            rows = pl.ds(z64, BU)
            ru = fu_ref[rows, :] - product * weight
            ru_ref[rows, :] = ru
            send_ref[rows, :] = (ru * theta_inv).astype(bf16)
        return carry

    lax.fori_loop(0, NZ // UNROLL, finish, 0)


def second_kernel(lm_ref, coef_ref, table_ref, coup_ref, schur_ref,
                  fu_ref, mask_ref, ru_ref, du_ref, dp_ref, q_ref, own_ref, low_ref,
                  high_ref, mlow_ref, mhigh_ref, out_ref,
                  wide_ref, d_ref, r_ref, s_ref, wa_ref, wb_ref, p_ref, rows_ref, sort_ref):
    widen(wide_ref, mask_ref, mlow_ref, mhigh_ref)
    pad_in((wa_ref, wb_ref), low_ref, high_ref, own_ref, True)
    refs = (coef_ref, lm_ref, table_ref, wide_ref, (r_ref, d_ref, s_ref))
    begin = starter(coef_ref, ru_ref, low_ref, high_ref, False)
    own = block(0)

    def last(z64, s):
        s_ref[pl.ds(z64, BU), own] = s

    sweep(0, "shrink", begin, None, refs, wa_ref, wb_ref)
    sweep(1, "ring", None, None, refs, wb_ref, wa_ref)
    sweep(2, "own", None, last, refs, wa_ref, wb_ref)
    couple(lambda z64: s_ref[pl.ds(z64, BU), own], lm_ref, coup_ref, wide_ref, q_ref, 1.0, p_ref)
    p_ref[...] = bands(schur_ref, p_ref)
    for half in range(2):
        for b in range(BLOCKS):
            if b < BLOCKS - 1:
                rows = pl.ds(half * HU + b * LANES, LANES)
                flat = s_ref[rows, own] + du_ref[rows, :] - fu_ref[rows, :]
            else:
                pressure = []
                for z in range(half * ZL, half * ZL + ZL):
                    here = pl.ds(z * PB, PB)
                    dp = p_ref[here, :] * mask_ref[pl.ds(z, 1), :]
                    pressure.append(dp + dp_ref[here, :])
                flat = jnp.concatenate(pressure, axis=0)
            rows_ref[b] = flat.T
            for x in range(XL):
                for yl in range(YL):
                    sort_ref[
                        pl.ds((half * BLOCKS + b) * 8 + yl * XL + x, CH // 2, stride=STEP), :
                    ] = rows_ref[b, pl.ds(x * NY + yl, CH // 2, stride=YL), :]
    out_ref[...] = sort_ref[...].astype(bf16)


def unpack_kernel(var_ref, got_ref, fu_ref, mask_ref, disp_ref, pres_ref, rows_ref):
    variant = var_ref[0]
    for k in range(CH):
        src = slot_of(variant, k) * BLOCKS
        for b in range(BLOCKS):
            piece = got_ref[src + b].astype(f32)
            for yl in range(YL):
                rows_ref[yl, b, pl.ds(XL * k, XL), :] = piece[yl * XL : yl * XL + XL]
    for yl in range(YL):
        for b in range(BLOCKS - 1):
            flat = rows_ref[yl, b].T
            for i in range(2):
                z = 2 * b + i
                weight = (mask_ref[pl.ds(z * YL + yl, 1), :] != 0).astype(f32)
                at = pl.ds(z * BU * YL + yl, BU, stride=YL)
                disp_ref[at, :] = flat[i * BU : i * BU + BU] + fu_ref[at, :] * weight
        pres_ref[pl.ds(yl, HP, stride=YL), :] = rows_ref[yl, BLOCKS - 1].T


VM = pl.BlockSpec(memory_space=pltpu.VMEM)
SM = pl.BlockSpec(memory_space=pltpu.SMEM)


def call(kernel, scalars, arrays, outs, scratch, limit=24):
    return pl.pallas_call(
        kernel,
        out_shape=[jax.ShapeDtypeStruct(*o) for o in outs],
        in_specs=[SM] * len(scalars) + [VM] * len(arrays),
        out_specs=[VM] * len(outs),
        scratch_shapes=[pltpu.VMEM(*s) for s in scratch],
        compiler_params=pltpu.CompilerParams(vmem_limit_bytes=limit << 20),
    )(*scalars, *arrays)


def body(force_u, force_p, cellmask, layer_mats, kblocks, bcoup, sinv, band_offsets, spectrum):
    up, down = chain()
    other = lax.ppermute(layer_mats, "gz", [(0, 1), (1, 0)])
    gz = lax.axis_index("gz")
    layers = jnp.where(
        gz == 0, jnp.concatenate([layer_mats, other]), jnp.concatenate([other, layer_mats])
    )
    variant = (lax.axis_index("gx") % 4).astype(jnp.int32)[None]
    fu_in = force_u.reshape(ZL * BU * YL, LANES)
    fp_in = force_p.reshape(ZL * PB * YL, LANES)
    mask_in = cellmask.reshape(ZL * YL, LANES)
    coefs, table, pair, matrix = call(
        prep_kernel, [spectrum, band_offsets], [kblocks, bcoup, sinv],
        [((8, WIDTH), f32), ((4, BU, 8 * BU), bf16), ((4, PB, 3 * BU), bf16),
         ((RP, 3 * RP), bf16)], [],
    )

    (packed,) = call(
        pack_kernel, [variant], [fu_in, fp_in, mask_in],
        [((CH * BLOCKS, 8, LANES), f32)],
        [((YL, BLOCKS, LANES, LANES), f32)],
        limit=60,
    )
    got = lax.all_to_all(packed, PLANE, 0, 0, tiled=True)
    got, table, pair, matrix, coefs = lax.optimization_barrier(
        (got, table, pair, matrix, coefs)
    )
    fu, fp, mask, send = call(
        spread_kernel, [], [coefs, got.reshape(CH * BLOCKS * 8, LANES)],
        [((RU, LANES), f32), ((RP, LANES), f32), ((NZ, LANES), f32), ((RU + NZ, LANES), bf16)],
        [((BLOCKS, LANES, LANES), f32)],
    )
    low = lax.ppermute(send, ALL, up)
    high = lax.ppermute(send, ALL, down)
    wide = [((NZ, 8, WIDTH), f32)] + [((RU, 2 * LANES), f32)] * 3 + [
        ((RU + 2 * BU, WIDTH), bf16)
    ] * 2
    ru, du, dp, q, send2 = call(
        first_kernel, [layers],
        [coefs, table, pair, matrix, fu, fp, mask, send, low, high],
        [((RU, LANES), f32), ((RU, LANES), f32), ((RP, LANES), f32), ((RP, LANES), f32),
         ((RU, LANES), bf16)],
        wide,
    )
    low2 = lax.ppermute(send2, ALL, up)
    high2 = lax.ppermute(send2, ALL, down)
    (back,) = call(
        second_kernel, [layers],
        [coefs, table, pair, matrix, fu, mask, ru, du, dp, q, send2, low2, high2, low, high],
        [((CH * BLOCKS * 8, LANES), bf16)],
        wide + [((RP, LANES), f32), ((BLOCKS, LANES, LANES), f32),
                ((CH * BLOCKS * 8, LANES), f32)],
    )
    home = lax.all_to_all(back.reshape(CH * BLOCKS, 8, LANES), PLANE, 0, 0, tiled=True)
    disp, pres = call(
        unpack_kernel, [variant], [home, fu_in, mask_in],
        [((ZL * BU * YL, LANES), f32), ((ZL * PB * YL, LANES), f32)],
        [((YL, BLOCKS, LANES, LANES), f32)],
    )
    return (disp.reshape(ZL, BU, YL, LANES), pres.reshape(ZL, PB, YL, LANES))


def solution(mesh):
    in_specs = (
        P("gz", None, "gy", "gx"),
        P("gz", None, "gy", "gx"),
        P("gz", "gy", "gx"),
        P("gz"),
        P(),
        P(),
        P(),
        P(),
        P(),
    )
    out_specs = (P("gz", None, "gy", "gx"), P("gz", None, "gy", "gx"))
    return jax.shard_map(body, mesh=mesh, in_specs=in_specs, out_specs=out_specs, check_vma=False)
```

time: 96.8 us -> 91.1 us (0.941)
  waiting for transfers between devices: 15.6 us -> 24.7 us
  local copies, waits for them, and re-layouts: 5.79 us -> 0.04 us
  other arithmetic: 4.01 us -> 0.08 us
  between operations: 3.79 us -> 0.79 us
  Pallas kernels: 18.8 us -> 16.6 us
    all_to_all x1, waiting for transfers between devices: 3.94 us -> 18.8 us  [body(): got = lax.all_to_all(packed, PLANE, 0, 0, tiled=True)]
    reduce_sum x1 -> x0, other arithmetic: 3.78 us -> none  [schur_matrix(): return jnp.sum(picked, axis=0).reshape(RP, RP)]
    unnamed x22 -> x16, local copies, waits for them, and re-layouts: 2.67 us -> 0.04 us
    ppermute x1, waiting for transfers between devices: 2.45 us -> 0.01 us  [body(): high = lax.ppermute(send, ALL, down)]
    reshape x1 -> x0, local copies, waits for them, and re-layouts: 2.44 us -> none  [schur_matrix(): return jnp.sum(picked, axis=0).reshape(RP, RP)]
    pallas_call x6, Pallas kernels: 18.8 us -> 16.6 us  [call(): pl.pallas_call(kernel, out_shape=[jax.ShapeDtypeStruct(*o) for o in outs]...]
    ppermute x1, waiting for transfers between devices: 3.87 us -> 1.95 us  [body(): other = lax.ppermute(layer_mats, 'gz', [(0, 1), (1, 0)])]
    ppermute x1, waiting for transfers between devices: 1.46 us -> 0.01 us  [body(): low = lax.ppermute(send, ALL, up)]
  transfers between devices with their start and end apart: 6 -> 6, of which waited for: 6 -> 4; matrix products, arithmetic and copies ran while one was open for 7% -> 0% of each run, Pallas kernels for 0% -> 1%
where the time goes in v3:
time: 91.1 us; the launch traced here: 90.7 us
  starting transfers between devices  25.7 us (28%)
  waiting for transfers between devices  24.7 us (27%)
  blocking collectives  22.9 us (25%)
  Pallas kernels  16.6 us (18%)
    all_to_all x1, blocking collectives, body(): lax.all_to_all(back.reshape(CH * BLOCKS, 8, LANES), PLANE, 0, 0, tiled=True)  22.9 us
    all_to_all x1, waiting for transfers between devices, body(): got = lax.all_to_all(packed, PLANE, 0, 0, tiled=True)  18.8 us
    pallas_call x6, Pallas kernels, call(): pl.pallas_call(kernel, out_shape=[jax.ShapeDtypeStruct(*o) for o in outs]...  16.6 us
    all_to_all x1, starting transfers between devices, body(): got = lax.all_to_all(packed, PLANE, 0, 0, tiled=True)  11.5 us
    ppermute x1, starting transfers between devices, body(): low2 = lax.ppermute(send2, ALL, up)  4.44 us
    ppermute x1, starting transfers between devices, body(): low = lax.ppermute(send, ALL, up)  3.92 us
    ppermute x1, waiting for transfers between devices, body(): high2 = lax.ppermute(send2, ALL, down)  2.41 us
    ppermute x1, starting transfers between devices, body(): other = lax.ppermute(layer_mats, 'gz', [(0, 1), (1, 0)])  1.99 us
  transfers between devices with their start and end apart: 6, of which 4 were waited for; matrix products, arithmetic and copies ran while one was open for 0% of the time, Pallas kernels for 1%

profile of v3, /device:TPU:16, one launch (start us, length us, event | category | flops | bytes accessed | tf_op | source)
XLA Modules:
  0.0 90.7 jit_solution(2848532563855363226)
XLA Ops:
  0.6 0.0 copy-start.1
  0.7 2.3 %shard_map.104 = f32[160,8,128]{2,1,0:T(8,128)} custom-call(s32[1]{0:T(128)} %bitcast.var_ref, f32[1024,128]{1,0:T(8,128)} %bitcast.9, f32[256,128]{1,0:T(8,128)} %bitcast.14, s32[16,128]{1,0:T(8,128)} %bitcast.12), custom_call_target="tpu_custom_call" | custom-call | tf_op jit(solution)/shard_map/pallas_call | solution.py:414
  3.0 11.5 %all-to-all-start = ((f32[160,8,128]{2,1,0:T(8,128)}), f32[160,8,128]{2,1,0:T(8,128)S(1)}, u32[]{:S(2)}, u32[]{:S(2)}) async-start(f32[160,8,128]{2,1,0:T(8,128)} %shard_map.104), calls=%async_computation | async-start | bytes 1310720 | tf_op jit(solution)/shard_map/all_to_all | solution.py:447
  14.5 0.0 copy-done.1
  14.5 0.0 copy-done.2
  14.5 0.0 copy-done.4
  14.5 0.0 copy-done.5
  14.5 0.0 copy-done.6
  14.5 1.3 %shard_map.105 = (f32[8,512]{1,0:T(8,128)S(1)}, bf16[4,64,512]{2,1,0:T(8,128)(2,1)S(1)}, bf16[4,16,192]{2,1,0:T(8,128)(2,1)S(1)}, bf16[256,768]{1,0:T(8,128)(2,1)S(1)}) custom-call(f32[2]{0:T(128)S(1)} %copy-done.5, s32[8]{0:T(128)S(1)} %copy-done.6, bf16[4,7,64,64]{3,2,1,0:T(8,128)(2,1)S(1)} %copy-done.2, f32[4,16,64]{2,1,0:T(8,128)S(1)} %copy-done.4, ...), custom_call_target="tpu_custom_call" | custom-call | tf_op jit(solution)/shard_map/pallas_call | solution.py:414
  15.8 18.8 %all-to-all-done = f32[160,8,128]{2,1,0:T(8,128)S(1)} async-done(((f32[160,8,128]{2,1,0:T(8,128)}), f32[160,8,128]{2,1,0:T(8,128)S(1)}, u32[]{:S(2)}, u32[]{:S(2)}) %all-to-all-start) | async-done | bytes 655392 | tf_op jit(solution)/shard_map/all_to_all | solution.py:447
  34.6 0.4 shard_map.106
  35.0 0.0 copy-start.7
  35.1 1.9 %collective-permute-start.2 = (bf16[1040,128]{1,0:T(8,128)(2,1)S(1)}, bf16[1040,128]{1,0:T(8,128)(2,1)S(1)}, u32[]{:S(2)}, u32[]{:S(2)}) collective-permute-start(bf16[1040,128]{1,0:T(8,128)(2,1)S(1)} %get-tuple-element.34.own_ref), channel_id=1, source_target_pairs={{1,0},{2,1},{3,2},{4,3},{5,4},{6,5},{7,6},{15,7},{14,15},{13,14},{... | collective-permute-start | bytes 798728 | tf_op jit(solution)/shard_map/ppermute | solution.py:457
  37.0 3.9 %collective-permute-start.1 = (bf16[1040,128]{1,0:T(8,128)(2,1)S(1)}, bf16[1040,128]{1,0:T(8,128)(2,1)S(1)}, u32[]{:S(2)}, u32[]{:S(2)}) collective-permute-start(bf16[1040,128]{1,0:T(8,128)(2,1)S(1)} %get-tuple-element.34.own_ref), channel_id=1, source_target_pairs={{0,1},{1,2},{2,3},{3,4},{4,5},{5,6},{6,7},{7,15},{15,14},{14,13},{... | collective-permute-start | bytes 798728 | tf_op jit(solution)/shard_map/ppermute | solution.py:456
  40.9 0.0 copy-done.7
  40.9 2.0 %collective-permute-start = (s32[8]{0:T(128)S(1)}, s32[8]{0:T(128)S(1)}, u32[]{:S(2)}, u32[]{:S(2)}) collective-permute-start(s32[8]{0:T(128)S(1)} %copy-done.7), channel_id=1, source_target_pairs={{0,1},{1,0},{2,3},{3,2},{4,5},{5,4},{6,7},{7,6},{8,9},{9,8},{10,11... | collective-permute-start | bytes 104 | tf_op jit(solution)/shard_map/ppermute | solution.py:426
  42.9 2.0 %collective-permute-done = s32[8]{0:T(128)S(1)} collective-permute-done((s32[8]{0:T(128)S(1)}, s32[8]{0:T(128)S(1)}, u32[]{:S(2)}, u32[]{:S(2)}) %collective-permute-start) | collective-permute-done | bytes 64 | tf_op jit(solution)/shard_map/ppermute | solution.py:426
  44.9 0.1 broadcast_select_fusion.lm_ref
  44.9 0.0 collective-permute-done.2.high_ref.mhigh_ref
  44.9 0.0 collective-permute-done.1.low_ref.mlow_ref
  44.9 6.3 %shard_map.107 = (f32[1024,128]{1,0:T(8,128)S(1)}, f32[1024,128]{1,0:T(8,128)S(1)}, f32[256,128]{1,0:T(8,128)S(1)}, f32[256,128]{1,0:T(8,128)S(1)}, bf16[1024,128]{1,0:T(8,128)(2,1)S(1)}) custom-call(s32[16]{0:T(128)S(1)} %broadcast_select_fusion.lm_ref, f32[8,512]{1,0:T(8,128)S(1)} %get-tuple-element.26.coef_ref, ...), custom_call_target="tpu_custom_call" | custom-call | tf_op jit(solution)/shard_map/pallas_call | solution.py:414
  51.3 1.9 %collective-permute-start.4 = (bf16[1024,128]{1,0:T(8,128)(2,1)S(1)}, bf16[1024,128]{1,0:T(8,128)(2,1)S(1)}, u32[]{:S(2)}, u32[]{:S(2)}) collective-permute-start(bf16[1024,128]{1,0:T(8,128)(2,1)S(1)} %get-tuple-element.39.own_ref), channel_id=1, source_target_pairs={{1,0},{2,1},{3,2},{4,3},{5,4},{6,5},{7,6},{15,7},{14,15},{13,14},{... | collective-permute-start | bytes 786440 | tf_op jit(solution)/shard_map/ppermute | solution.py:469
  53.2 4.4 %collective-permute-start.3 = (bf16[1024,128]{1,0:T(8,128)(2,1)S(1)}, bf16[1024,128]{1,0:T(8,128)(2,1)S(1)}, u32[]{:S(2)}, u32[]{:S(2)}) collective-permute-start(bf16[1024,128]{1,0:T(8,128)(2,1)S(1)} %get-tuple-element.39.own_ref), channel_id=1, source_target_pairs={{0,1},{1,2},{2,3},{3,4},{4,5},{5,6},{6,7},{7,15},{15,14},{14,13},{... | collective-permute-start | bytes 786440 | tf_op jit(solution)/shard_map/ppermute | solution.py:468
  57.6 2.4 %collective-permute-done.4.high_ref = bf16[1024,128]{1,0:T(8,128)(2,1)S(1)} collective-permute-done((bf16[1024,128]{1,0:T(8,128)(2,1)S(1)}, bf16[1024,128]{1,0:T(8,128)(2,1)S(1)}, u32[]{:S(2)}, u32[]{:S(2)}) %collective-permute-start.4) | collective-permute-done | bytes 262176 | tf_op jit(solution)/shard_map/ppermute | solution.py:469
  60.1 1.5 %collective-permute-done.3.low_ref = bf16[1024,128]{1,0:T(8,128)(2,1)S(1)} collective-permute-done((bf16[1024,128]{1,0:T(8,128)(2,1)S(1)}, bf16[1024,128]{1,0:T(8,128)(2,1)S(1)}, u32[]{:S(2)}, u32[]{:S(2)}) %collective-permute-start.3) | collective-permute-done | bytes 262176 | tf_op jit(solution)/shard_map/ppermute | solution.py:468
  61.5 5.2 %shard_map.108 = bf16[1280,128]{1,0:T(8,128)(2,1)S(1)} custom-call(s32[16]{0:T(128)S(1)} %broadcast_select_fusion.lm_ref, f32[8,512]{1,0:T(8,128)S(1)} %get-tuple-element.26.coef_ref, bf16[4,64,512]{2,1,0:T(8,128)(2,1)S(1)} %get-tuple-element.27.table_ref, bf16[4,16,192]{2,1,0:T(8,128)(2,1)S(1)} %get-tuple-element.28.coup_ref, ...), custom_call_target="tpu_custom_call" | custom-call | tf_op jit(solution)/shard_map/pallas_call | solution.py:414
  66.7 0.0 copy-start
  66.7 0.0 copy-start.3
  66.7 22.9 %all_to_all.10.got_ref = bf16[160,8,128]{2,1,0:T(8,128)(2,1)S(1)} all-to-all(bf16[160,8,128]{2,1,0:T(8,128)(2,1)S(1)} %bitcast.11), channel_id=1, replica_groups=mesh['gx'=8,'gy'=16,'gz'=2] {'gy','gz'}, dimensions={0} | all-to-all | bytes 655360 | tf_op jit(solution)/shard_map/all_to_all | solution.py:477
  89.6 0.0 copy-done
  89.6 0.0 copy-done.3
  89.6 1.1 %shard_map.109 = (f32[1024,128]{1,0:T(8,128)}, f32[256,128]{1,0:T(8,128)}) custom-call(s32[1]{0:T(128)} %bitcast.var_ref, bf16[160,8,128]{2,1,0:T(8,128)(2,1)S(1)} %all_to_all.10.got_ref, f32[1024,128]{1,0:T(8,128)S(1)} %bitcast.10, s32[16,128]{1,0:T(8,128)S(1)} %bitcast.13), custom_call_target="tpu_custom_call" | custom-call | tf_op jit(solution)/shard_map/pallas_call | solution.py:414
  (4 shorter events, 0.0 us)
Async XLA Ops:
  0.6 13.8 %copy-start.1 = (f32[8,16,16,16]{3,2,1,0:T(8,128)S(1)}, f32[8,16,16,16]{3,2,1,0:T(8,128)}, u32[]{:S(2)}) copy-start(f32[8,16,16,16]{3,2,1,0:T(8,128)} %sinv_ref.1) | copy-start | bytes 393220
  3.0 11.5 %copy-start.2 = (bf16[4,7,64,64]{3,2,1,0:T(8,128)(2,1)S(1)}, bf16[4,7,64,64]{3,2,1,0:T(8,128)(2,1)}, u32[]{:S(2)}) copy-start(bf16[4,7,64,64]{3,2,1,0:T(8,128)(2,1)} %kb_ref.1) | copy-start | bytes 688132
  3.0 11.5 %copy-start.4 = (f32[4,16,64]{2,1,0:T(8,128)S(1)}, f32[4,16,64]{2,1,0:T(8,128)}, u32[]{:S(2)}) copy-start(f32[4,16,64]{2,1,0:T(8,128)} %coup_ref.1) | copy-start | bytes 49156
  3.0 11.5 %copy-start.5 = (f32[2]{0:T(128)S(1)}, f32[2]{0:T(128)}, u32[]{:S(2)}) copy-start(f32[2]{0:T(128)} %spec_ref.1) | copy-start | bytes 28
  3.0 11.5 %copy-start.6 = (s32[8]{0:T(128)S(1)}, s32[8]{0:T(128)}, u32[]{:S(2)}) copy-start(s32[8]{0:T(128)} %off_ref.1) | copy-start | bytes 100
  3.0 31.6 %all-to-all-start = ((f32[160,8,128]{2,1,0:T(8,128)}), f32[160,8,128]{2,1,0:T(8,128)S(1)}, u32[]{:S(2)}, u32[]{:S(2)}) async-start(f32[160,8,128]{2,1,0:T(8,128)} %shard_map.104), calls=%async_computation | async-start | bytes 1310720 | tf_op jit(solution)/shard_map/all_to_all | solution.py:447
  35.0 5.9 %copy-start.7 = (s32[8]{0:T(128)S(1)}, s32[8]{0:T(128)}, u32[]{:S(2)}) copy-start(s32[8]{0:T(128)} %param.12) | copy-start | bytes 100
  35.1 9.9 %collective-permute-start.2 = (bf16[1040,128]{1,0:T(8,128)(2,1)S(1)}, bf16[1040,128]{1,0:T(8,128)(2,1)S(1)}, u32[]{:S(2)}, u32[]{:S(2)}) collective-permute-start(bf16[1040,128]{1,0:T(8,128)(2,1)S(1)} %get-tuple-element.34.own_ref), channel_id=1, source_target_pairs={{1,0},{2,1},{3,2},{4,3},{5,4},{6,5},{7,6},{15,7},{14,15},{13,14},{... | collective-permute-start | bytes 798728 | tf_op jit(solution)/shard_map/ppermute | solution.py:457
  37.0 8.0 %collective-permute-start.1 = (bf16[1040,128]{1,0:T(8,128)(2,1)S(1)}, bf16[1040,128]{1,0:T(8,128)(2,1)S(1)}, u32[]{:S(2)}, u32[]{:S(2)}) collective-permute-start(bf16[1040,128]{1,0:T(8,128)(2,1)S(1)} %get-tuple-element.34.own_ref), channel_id=1, source_target_pairs={{0,1},{1,2},{2,3},{3,4},{4,5},{5,6},{6,7},{7,15},{15,14},{14,13},{... | collective-permute-start | bytes 798728 | tf_op jit(solution)/shard_map/ppermute | solution.py:456
  40.9 3.9 %collective-permute-start = (s32[8]{0:T(128)S(1)}, s32[8]{0:T(128)S(1)}, u32[]{:S(2)}, u32[]{:S(2)}) collective-permute-start(s32[8]{0:T(128)S(1)} %copy-done.7), channel_id=1, source_target_pairs={{0,1},{1,0},{2,3},{3,2},{4,5},{5,4},{6,7},{7,6},{8,9},{9,8},{10,11... | collective-permute-start | bytes 104 | tf_op jit(solution)/shard_map/ppermute | solution.py:426
  51.3 8.8 %collective-permute-start.4 = (bf16[1024,128]{1,0:T(8,128)(2,1)S(1)}, bf16[1024,128]{1,0:T(8,128)(2,1)S(1)}, u32[]{:S(2)}, u32[]{:S(2)}) collective-permute-start(bf16[1024,128]{1,0:T(8,128)(2,1)S(1)} %get-tuple-element.39.own_ref), channel_id=1, source_target_pairs={{1,0},{2,1},{3,2},{4,3},{5,4},{6,5},{7,6},{15,7},{14,15},{13,14},{... | collective-permute-start | bytes 786440 | tf_op jit(solution)/shard_map/ppermute | solution.py:469
  53.2 8.3 %collective-permute-start.3 = (bf16[1024,128]{1,0:T(8,128)(2,1)S(1)}, bf16[1024,128]{1,0:T(8,128)(2,1)S(1)}, u32[]{:S(2)}, u32[]{:S(2)}) collective-permute-start(bf16[1024,128]{1,0:T(8,128)(2,1)S(1)} %get-tuple-element.39.own_ref), channel_id=1, source_target_pairs={{0,1},{1,2},{2,3},{3,4},{4,5},{5,6},{6,7},{7,15},{15,14},{14,13},{... | collective-permute-start | bytes 786440 | tf_op jit(solution)/shard_map/ppermute | solution.py:468
  66.7 22.9 %copy-start = (f32[8,64,2,128]{3,2,1,0:T(2,128)S(1)}, f32[8,64,2,128]{3,2,1,0:T(2,128)}, u32[]{:S(2)}) copy-start(f32[8,64,2,128]{3,2,1,0:T(2,128)} %param.9) | copy-start | bytes 1572868
  66.7 22.9 %copy-start.3 = (s32[8,2,128]{2,1,0:T(2,128)S(1)}, s32[8,2,128]{2,1,0:T(2,128)}, u32[]{:S(2)}) copy-start(s32[8,2,128]{2,1,0:T(2,128)} %param.11) | copy-start | bytes 24580

commit v4 on v3

--- a/solution.py
+++ b/solution.py
@@ -46,34 +46,47 @@
     )
 
 
-def chain():
+def ring():
     order = [g * CH + place(g % 4, k) for g in range(8) for k in range(CH)]
-    up = [(order[i], order[i + 1]) for i in range(len(order) - 1)]
+    up = [(order[i - 1], order[i]) for i in range(len(order))]
     return up, [(b, a) for a, b in up]
 
 
-def pack_kernel(var_ref, fu_ref, fp_ref, mask_ref, out_ref, flip_ref):
-    for yl in range(YL):
-        pressure = []
-        for z in range(ZL):
-            live = mask_ref[pl.ds(z * YL + yl, 1), :] != 0
-            weight = live.astype(f32)
-            fp = fp_ref[pl.ds(z * PB * YL + yl, PB, stride=YL), :] * weight
-            last = lax.broadcasted_iota(jnp.int32, (PB, LANES), 0) == PB - 1
-            dead = jnp.broadcast_to(weight, (PB, LANES)) == 0.0
-            pressure.append(jnp.where(jnp.logical_and(last, dead), jnp.inf, fp))
-        for b in range(BLOCKS - 1):
-            pair = []
-            for z in (2 * b, 2 * b + 1):
-                weight = (mask_ref[pl.ds(z * YL + yl, 1), :] != 0).astype(f32)
-                pair.append(fu_ref[pl.ds(z * BU * YL + yl, BU, stride=YL), :] * weight)
-            flip_ref[yl, b] = jnp.concatenate(pair, axis=0).T
-        flip_ref[yl, BLOCKS - 1] = jnp.concatenate(pressure, axis=0).T
-    variant = var_ref[0]
-    for k in range(CH):
-        dest = slot_of(variant, k) * BLOCKS
-        for b in range(BLOCKS):
-            out_ref[dest + b] = jnp.concatenate(
+def at_end(group):
+    plane = lax.axis_index("gy") + lax.axis_index("gz")
+    return jnp.logical_and(lax.axis_index("gx") == group, plane == 0)
+
+
+def pack_kernel(fu_hbm, fp_hbm, mask_hbm, out_ref, fu_ref, fp_ref, mask_ref, flip_ref, sem):
+    part = 2 * BU * YL
+    copies = [pltpu.make_async_copy(mask_hbm, mask_ref, sem.at[0])]
+    for b in range(BLOCKS - 1):
+        rows = pl.ds(b * part, part)
+        copies.append(pltpu.make_async_copy(fu_hbm.at[rows], fu_ref.at[rows], sem.at[1 + b]))
+    copies.append(pltpu.make_async_copy(fp_hbm, fp_ref, sem.at[BLOCKS]))
+    for copy in copies:
+        copy.start()
+    copies[0].wait()
+    variant = lax.axis_index("gx") % 4
+    dests = [slot_of(variant, k) * BLOCKS for k in range(CH)]
+    for b in range(BLOCKS):
+        copies[1 + b].wait()
+        for yl in range(YL):
+            rows = []
+            if b < BLOCKS - 1:
+                for z in (2 * b, 2 * b + 1):
+                    weight = (mask_ref[pl.ds(z * YL + yl, 1), :] != 0).astype(f32)
+                    rows.append(fu_ref[pl.ds(z * BU * YL + yl, BU, stride=YL), :] * weight)
+            else:
+                last = lax.broadcasted_iota(jnp.int32, (PB, LANES), 0) == PB - 1
+                for z in range(ZL):
+                    weight = (mask_ref[pl.ds(z * YL + yl, 1), :] != 0).astype(f32)
+                    fp = fp_ref[pl.ds(z * PB * YL + yl, PB, stride=YL), :] * weight
+                    dead = jnp.broadcast_to(weight, (PB, LANES)) == 0.0
+                    rows.append(jnp.where(jnp.logical_and(last, dead), jnp.inf, fp))
+            flip_ref[yl, b] = jnp.concatenate(rows, axis=0).T
+        for k in range(CH):
+            out_ref[dests[k] + b] = jnp.concatenate(
                 [flip_ref[yl, b, pl.ds(XL * k, XL), :] for yl in range(YL)], axis=0
             )
 
@@ -199,21 +212,22 @@
     lax.fori_loop(0, NZ // UNROLL, group, 0)
 
 
-def starter(coef_ref, own_ref, low_ref, high_ref, wide):
+def starter(coef_ref, own_ref, w_ref, wide):
     theta_inv = coef_ref[pl.ds(0, 1), block(0)]
     theta = coef_ref[pl.ds(1, 1), block(0)]
 
     def begin(rows):
         r = own_ref[rows, :]
         d = r * theta_inv
-        low = low_ref[rows, :].astype(f32)
-        high = high_ref[rows, :].astype(f32)
+        here = pl.ds(rows.start + BU, BU)
         if wide:
+            low = w_ref[here, block(LOW)].astype(f32)
+            high = w_ref[here, block(HIGH)].astype(f32)
             return (
                 jnp.concatenate([low * theta, high * theta, r], axis=1),
                 jnp.concatenate([low, high, d], axis=1),
             )
-        edge = edge_of(low, high)
+        edge = w_ref[here, block(EDGE)].astype(f32)
         return (
             jnp.concatenate([r, edge * theta], axis=1),
             jnp.concatenate([d, edge], axis=1),
@@ -223,8 +237,8 @@
 
 
 def widen(wide_ref, mask_ref, low_ref, high_ref):
-    low = low_ref[pl.ds(RU, NZ), :].astype(f32)
-    high = high_ref[pl.ds(RU, NZ), :].astype(f32)
+    low = low_ref[pl.ds(RU, NZ), :].astype(f32) * jnp.where(at_end(0), 0.0, 1.0)
+    high = high_ref[pl.ds(RU, NZ), :].astype(f32) * jnp.where(at_end(7), 0.0, 1.0)
     whole = jnp.concatenate([low, high, mask_ref[...], edge_of(low, high)], axis=1)
     for z in range(NZ):
         wide_ref[z] = jnp.broadcast_to(whole[z : z + 1], (8, WIDTH))
@@ -237,9 +251,16 @@
         w_ref[pl.ds(RU + BU, BU), :] = edge
     for b, src in ((LOW, low_ref), (HIGH, high_ref), (OWN, own_ref)):
         w_refs[0][pl.ds(BU, RU), block(b)] = src[pl.ds(0, RU), :]
+    inner = pl.ds(BU, RU)
+    for b, group in ((LOW, 0), (HIGH, 7)):
+
+        @pl.when(at_end(group))
+        def _():
+            w_refs[0][inner, block(b)] = jnp.zeros((RU, LANES), bf16)
+
     if with_edge:
-        w_refs[0][pl.ds(BU, RU), block(EDGE)] = edge_of(
-            low_ref[pl.ds(0, RU), :], high_ref[pl.ds(0, RU), :]
+        w_refs[0][inner, block(EDGE)] = edge_of(
+            w_refs[0][inner, block(LOW)], w_refs[0][inner, block(HIGH)]
         )
 
 
@@ -316,7 +337,7 @@
     widen(wide_ref, mask_ref, low_ref, high_ref)
     pad_in((wa_ref, wb_ref), low_ref, high_ref, own_ref, False)
     refs = (coef_ref, lm_ref, table_ref, wide_ref, (r_ref, d_ref, s_ref))
-    begin = starter(coef_ref, fu_ref, low_ref, high_ref, True)
+    begin = starter(coef_ref, fu_ref, wa_ref, True)
 
     def last(z64, s):
         wb_ref[pl.ds(z64 + BU, BU), block(OWN, 2)] = s.astype(bf16)
@@ -355,7 +376,7 @@
     widen(wide_ref, mask_ref, mlow_ref, mhigh_ref)
     pad_in((wa_ref, wb_ref), low_ref, high_ref, own_ref, True)
     refs = (coef_ref, lm_ref, table_ref, wide_ref, (r_ref, d_ref, s_ref))
-    begin = starter(coef_ref, ru_ref, low_ref, high_ref, False)
+    begin = starter(coef_ref, ru_ref, wa_ref, False)
     own = block(0)
 
     def last(z64, s):
@@ -387,8 +408,8 @@
     out_ref[...] = sort_ref[...].astype(bf16)
 
 
-def unpack_kernel(var_ref, got_ref, fu_ref, mask_ref, disp_ref, pres_ref, rows_ref):
-    variant = var_ref[0]
+def unpack_kernel(got_ref, fu_ref, mask_ref, disp_ref, pres_ref, rows_ref):
+    variant = lax.axis_index("gx") % 4
     for k in range(CH):
         src = slot_of(variant, k) * BLOCKS
         for b in range(BLOCKS):
@@ -422,13 +443,8 @@
 
 
 def body(force_u, force_p, cellmask, layer_mats, kblocks, bcoup, sinv, band_offsets, spectrum):
-    up, down = chain()
+    up, down = ring()
     other = lax.ppermute(layer_mats, "gz", [(0, 1), (1, 0)])
-    gz = lax.axis_index("gz")
-    layers = jnp.where(
-        gz == 0, jnp.concatenate([layer_mats, other]), jnp.concatenate([other, layer_mats])
-    )
-    variant = (lax.axis_index("gx") % 4).astype(jnp.int32)[None]
     fu_in = force_u.reshape(ZL * BU * YL, LANES)
     fp_in = force_p.reshape(ZL * PB * YL, LANES)
     mask_in = cellmask.reshape(ZL * YL, LANES)
@@ -438,11 +454,22 @@
          ((RP, 3 * RP), bf16)], [],
     )
 
-    (packed,) = call(
-        pack_kernel, [variant], [fu_in, fp_in, mask_in],
-        [((CH * BLOCKS, 8, LANES), f32)],
-        [((YL, BLOCKS, LANES, LANES), f32)],
-        limit=60,
+    packed = pl.pallas_call(
+        pack_kernel,
+        out_shape=jax.ShapeDtypeStruct((CH * BLOCKS, 8, LANES), f32),
+        in_specs=[pl.BlockSpec(memory_space=pltpu.HBM)] * 3,
+        out_specs=VM,
+        scratch_shapes=[
+            pltpu.VMEM(fu_in.shape, f32), pltpu.VMEM(fp_in.shape, f32),
+            pltpu.VMEM(mask_in.shape, jnp.int32),
+            pltpu.VMEM((YL, BLOCKS, LANES, LANES), f32), pltpu.SemaphoreType.DMA((BLOCKS + 1,)),
+        ],
+        compiler_params=pltpu.CompilerParams(vmem_limit_bytes=60 << 20),
+    )(fu_in, fp_in, mask_in)
+    packed, other = lax.optimization_barrier((packed, other))
+    gz = lax.axis_index("gz")
+    layers = jnp.where(
+        gz == 0, jnp.concatenate([layer_mats, other]), jnp.concatenate([other, layer_mats])
     )
     got = lax.all_to_all(packed, PLANE, 0, 0, tiled=True)
     got, table, pair, matrix, coefs = lax.optimization_barrier(
@@ -476,7 +503,7 @@
     )
     home = lax.all_to_all(back.reshape(CH * BLOCKS, 8, LANES), PLANE, 0, 0, tiled=True)
     disp, pres = call(
-        unpack_kernel, [variant], [home, fu_in, mask_in],
+        unpack_kernel, [], [home, fu_in, mask_in],
         [((ZL * BU * YL, LANES), f32), ((ZL * PB * YL, LANES), f32)],
         [((YL, BLOCKS, LANES, LANES), f32)],
     )

time: 91.1 us -> 84.9 us (0.932)
  starting transfers between devices: 25.7 us -> 16.9 us
  waiting for transfers between devices: 24.7 us -> 26.8 us
    ppermute x1, waiting for transfers between devices: 0.01 us -> 3.66 us  [body(): high = lax.ppermute(send, ALL, down)]
    pallas_call x0 -> x1, Pallas kernels: none -> 2.52 us  [body(): pl.pallas_call(pack_kernel, out_shape=jax.ShapeDtypeStruct((CH * BLOCKS,...]
    ppermute x1, starting transfers between devices: 4.44 us -> 2.09 us  [body(): low2 = lax.ppermute(send2, ALL, up)]
    pallas_call x6 -> x5, Pallas kernels: 16.6 us -> 14.3 us  [call(): pl.pallas_call(kernel, out_shape=[jax.ShapeDtypeStruct(*o) for o in outs]...]
    ppermute x1, waiting for transfers between devices: 1.95 us -> 0.01 us  [body(): other = lax.ppermute(layer_mats, 'gz', [(0, 1), (1, 0)])]
    ppermute x1, starting transfers between devices: 3.92 us -> 2.01 us  [body(): low = lax.ppermute(send, ALL, up)]
    ppermute x1, waiting for transfers between devices: 2.41 us -> 4.27 us  [body(): high2 = lax.ppermute(send2, ALL, down)]
    ppermute x1, starting transfers between devices: 1.92 us -> 0.09 us  [body(): high = lax.ppermute(send, ALL, down)]
  transfers between devices with their start and end apart: 6 -> 6, of which waited for: 4 -> 3; matrix products, arithmetic and copies ran while one was open for 0% -> 0% of each run, Pallas kernels for 1% -> 4%
where the time goes in v4:
time: 84.9 us; the launch traced here: 84.5 us
  waiting for transfers between devices  26.8 us (32%)
  blocking collectives  22.4 us (26%)
  starting transfers between devices  16.9 us (20%)
  Pallas kernels  16.8 us (20%)
    all_to_all x1, blocking collectives, body(): lax.all_to_all(back.reshape(CH * BLOCKS, 8, LANES), PLANE, 0, 0, tiled=True)  22.4 us
    all_to_all x1, waiting for transfers between devices, body(): got = lax.all_to_all(packed, PLANE, 0, 0, tiled=True)  18.9 us
    pallas_call x5, Pallas kernels, call(): pl.pallas_call(kernel, out_shape=[jax.ShapeDtypeStruct(*o) for o in outs]...  14.3 us
    all_to_all x1, starting transfers between devices, body(): got = lax.all_to_all(packed, PLANE, 0, 0, tiled=True)  10.6 us
    ppermute x1, waiting for transfers between devices, body(): high2 = lax.ppermute(send2, ALL, down)  4.27 us
    ppermute x1, waiting for transfers between devices, body(): high = lax.ppermute(send, ALL, down)  3.66 us
    pallas_call x1, Pallas kernels, body(): pl.pallas_call(pack_kernel, out_shape=jax.ShapeDtypeStruct((CH * BLOCKS,...  2.52 us
    ppermute x1, starting transfers between devices, body(): low2 = lax.ppermute(send2, ALL, up)  2.09 us
  transfers between devices with their start and end apart: 6, of which 3 were waited for; matrix products, arithmetic and copies ran while one was open for 0% of the time, Pallas kernels for 4%

profile of v4, /device:TPU:16, one launch (start us, length us, event | category | flops | bytes accessed | tf_op | source)
XLA Modules:
  0.0 84.5 jit_solution(9465852775516485348)
XLA Ops:
  0.6 2.0 %collective-permute-start = (s32[8]{0:T(128)}, s32[8]{0:T(128)S(1)}, u32[]{:S(2)}, u32[]{:S(2)}) collective-permute-start(s32[8]{0:T(128)} %param.12), channel_id=1, source_target_pairs={{0,1},{1,0},{2,3},{3,2},{4,5},{5,4},{6,7},{7,6},{8,9},{9,8},{10,11... | collective-permute-start | bytes 104 | tf_op jit(solution)/shard_map/ppermute | solution.py:447
  2.6 2.5 %shard_map.104 = f32[160,8,128]{2,1,0:T(8,128)} custom-call(f32[1024,128]{1,0:T(8,128)} %bitcast.8, f32[256,128]{1,0:T(8,128)} %bitcast.13, s32[16,128]{1,0:T(8,128)} %bitcast.11), custom_call_target="tpu_custom_call" | custom-call | tf_op jit(solution)/shard_map/pallas_call | solution.py:457
  5.2 0.0 copy-start.2
  5.2 0.0 copy-start.4
  5.2 0.0 copy-start.5
  5.2 0.0 copy-start.6
  5.2 0.0 collective-permute-done
  5.2 10.6 %all-to-all-start = ((f32[160,8,128]{2,1,0:T(8,128)}), f32[160,8,128]{2,1,0:T(8,128)S(1)}, u32[]{:S(2)}, u32[]{:S(2)}) async-start(f32[160,8,128]{2,1,0:T(8,128)} %shard_map.104), calls=%async_computation | async-start | bytes 1310720 | tf_op jit(solution)/shard_map/all_to_all | solution.py:474
  15.9 0.0 copy-done.1
  15.9 0.0 copy-done.2
  15.9 0.0 copy-done.4
  15.9 0.0 copy-done.5
  15.9 1.3 %shard_map.105 = (f32[8,512]{1,0:T(8,128)S(1)}, bf16[4,64,512]{2,1,0:T(8,128)(2,1)S(1)}, bf16[4,16,192]{2,1,0:T(8,128)(2,1)S(1)}, bf16[256,768]{1,0:T(8,128)(2,1)S(1)}) custom-call(f32[2]{0:T(128)S(1)} %copy-done.5, s32[8]{0:T(128)S(1)} %copy-done.6, bf16[4,7,64,64]{3,2,1,0:T(8,128)(2,1)S(1)} %copy-done.2, f32[4,16,64]{2,1,0:T(8,128)S(1)} %copy-done.4, ...), custom_call_target="tpu_custom_call" | custom-call | tf_op jit(solution)/shard_map/pallas_call | solution.py:435
  17.2 18.9 %all-to-all-done = f32[160,8,128]{2,1,0:T(8,128)S(1)} async-done(((f32[160,8,128]{2,1,0:T(8,128)}), f32[160,8,128]{2,1,0:T(8,128)S(1)}, u32[]{:S(2)}, u32[]{:S(2)}) %all-to-all-start) | async-done | bytes 655392 | tf_op jit(solution)/shard_map/all_to_all | solution.py:474
  36.1 0.4 shard_map.106
  36.5 0.1 collective-permute-start.2
  36.6 2.0 %collective-permute-start.1 = (bf16[1040,128]{1,0:T(8,128)(2,1)S(1)}, bf16[1040,128]{1,0:T(8,128)(2,1)S(1)}, u32[]{:S(2)}, u32[]{:S(2)}) collective-permute-start(bf16[1040,128]{1,0:T(8,128)(2,1)S(1)} %get-tuple-element.38.own_ref), channel_id=1, source_target_pairs={{224,0},{0,1},{1,2},{2,3},{3,4},{4,5},{5,6},{6,7},{7,15},{15,14},{... | collective-permute-start | bytes 798728 | tf_op jit(solution)/shard_map/ppermute | solution.py:483
  38.6 0.7 copy-done.7
  39.3 0.1 broadcast_select_fusion.lm_ref
  39.3 3.7 %collective-permute-done.2.high_ref.mhigh_ref = bf16[1040,128]{1,0:T(8,128)(2,1)S(1)} collective-permute-done((bf16[1040,128]{1,0:T(8,128)(2,1)S(1)}, bf16[1040,128]{1,0:T(8,128)(2,1)S(1)}, u32[]{:S(2)}, u32[]{:S(2)}) %collective-permute-start.2) | collective-permute-done | bytes 266272 | tf_op jit(solution)/shard_map/ppermute | solution.py:484
  43.0 0.0 collective-permute-done.1.low_ref.mlow_ref
  43.0 6.3 %shard_map.107 = (f32[1024,128]{1,0:T(8,128)S(1)}, f32[1024,128]{1,0:T(8,128)S(1)}, f32[256,128]{1,0:T(8,128)S(1)}, f32[256,128]{1,0:T(8,128)S(1)}, bf16[1024,128]{1,0:T(8,128)(2,1)S(1)}) custom-call(s32[16]{0:T(128)S(1)} %broadcast_select_fusion.lm_ref, f32[8,512]{1,0:T(8,128)S(1)} %get-tuple-element.30.coef_ref, ...), custom_call_target="tpu_custom_call" | custom-call | tf_op jit(solution)/shard_map/pallas_call | solution.py:435
  49.3 0.1 collective-permute-start.4
  49.4 2.1 %collective-permute-start.3 = (bf16[1024,128]{1,0:T(8,128)(2,1)S(1)}, bf16[1024,128]{1,0:T(8,128)(2,1)S(1)}, u32[]{:S(2)}, u32[]{:S(2)}) collective-permute-start(bf16[1024,128]{1,0:T(8,128)(2,1)S(1)} %get-tuple-element.43.own_ref), channel_id=1, source_target_pairs={{224,0},{0,1},{1,2},{2,3},{3,4},{4,5},{5,6},{6,7},{7,15},{15,14},{... | collective-permute-start | bytes 786440 | tf_op jit(solution)/shard_map/ppermute | solution.py:495
  51.5 4.3 %collective-permute-done.4.high_ref = bf16[1024,128]{1,0:T(8,128)(2,1)S(1)} collective-permute-done((bf16[1024,128]{1,0:T(8,128)(2,1)S(1)}, bf16[1024,128]{1,0:T(8,128)(2,1)S(1)}, u32[]{:S(2)}, u32[]{:S(2)}) %collective-permute-start.4) | collective-permute-done | bytes 262176 | tf_op jit(solution)/shard_map/ppermute | solution.py:496
  55.8 0.0 collective-permute-done.3.low_ref
  55.8 5.2 %shard_map.108 = bf16[1280,128]{1,0:T(8,128)(2,1)S(1)} custom-call(s32[16]{0:T(128)S(1)} %broadcast_select_fusion.lm_ref, f32[8,512]{1,0:T(8,128)S(1)} %get-tuple-element.30.coef_ref, bf16[4,64,512]{2,1,0:T(8,128)(2,1)S(1)} %get-tuple-element.31.table_ref, bf16[4,16,192]{2,1,0:T(8,128)(2,1)S(1)} %get-tuple-element.32.coup_ref, ...), custom_call_target="tpu_custom_call" | custom-call | tf_op jit(solution)/shard_map/pallas_call | solution.py:435
  61.0 0.0 copy-start
  61.0 0.0 copy-start.3
  61.0 22.4 %all_to_all.10.got_ref = bf16[160,8,128]{2,1,0:T(8,128)(2,1)S(1)} all-to-all(bf16[160,8,128]{2,1,0:T(8,128)(2,1)S(1)} %bitcast.10), channel_id=1, replica_groups=mesh['gx'=8,'gy'=16,'gz'=2] {'gy','gz'}, dimensions={0} | all-to-all | bytes 655360 | tf_op jit(solution)/shard_map/all_to_all | solution.py:504
  83.4 0.0 copy-done
  83.4 1.1 %shard_map.109 = (f32[1024,128]{1,0:T(8,128)}, f32[256,128]{1,0:T(8,128)}) custom-call(bf16[160,8,128]{2,1,0:T(8,128)(2,1)S(1)} %all_to_all.10.got_ref, f32[1024,128]{1,0:T(8,128)S(1)} %bitcast.9, s32[16,128]{1,0:T(8,128)S(1)} %bitcast.12), custom_call_target="tpu_custom_call" | custom-call | tf_op jit(solution)/shard_map/pallas_call | solution.py:435
  (4 shorter events, 0.0 us)
Async XLA Ops:
  0.6 4.6 %collective-permute-start = (s32[8]{0:T(128)}, s32[8]{0:T(128)S(1)}, u32[]{:S(2)}, u32[]{:S(2)}) collective-permute-start(s32[8]{0:T(128)} %param.12), channel_id=1, source_target_pairs={{0,1},{1,0},{2,3},{3,2},{4,5},{5,4},{6,7},{7,6},{8,9},{9,8},{10,11... | collective-permute-start | bytes 104 | tf_op jit(solution)/shard_map/ppermute | solution.py:447
  2.6 13.2 %copy-start.1 = (f32[8,16,16,16]{3,2,1,0:T(8,128)S(1)}, f32[8,16,16,16]{3,2,1,0:T(8,128)}, u32[]{:S(2)}) copy-start(f32[8,16,16,16]{3,2,1,0:T(8,128)} %sinv_ref.1) | copy-start | bytes 393220
  5.2 10.7 %copy-start.2 = (bf16[4,7,64,64]{3,2,1,0:T(8,128)(2,1)S(1)}, bf16[4,7,64,64]{3,2,1,0:T(8,128)(2,1)}, u32[]{:S(2)}) copy-start(bf16[4,7,64,64]{3,2,1,0:T(8,128)(2,1)} %kb_ref.1) | copy-start | bytes 688132
  5.2 10.7 %copy-start.4 = (f32[4,16,64]{2,1,0:T(8,128)S(1)}, f32[4,16,64]{2,1,0:T(8,128)}, u32[]{:S(2)}) copy-start(f32[4,16,64]{2,1,0:T(8,128)} %coup_ref.1) | copy-start | bytes 49156
  5.2 10.7 %copy-start.5 = (f32[2]{0:T(128)S(1)}, f32[2]{0:T(128)}, u32[]{:S(2)}) copy-start(f32[2]{0:T(128)} %spec_ref.1) | copy-start | bytes 28
  5.2 10.7 %copy-start.6 = (s32[8]{0:T(128)S(1)}, s32[8]{0:T(128)}, u32[]{:S(2)}) copy-start(s32[8]{0:T(128)} %off_ref.1) | copy-start | bytes 100
  5.2 30.8 %all-to-all-start = ((f32[160,8,128]{2,1,0:T(8,128)}), f32[160,8,128]{2,1,0:T(8,128)S(1)}, u32[]{:S(2)}, u32[]{:S(2)}) async-start(f32[160,8,128]{2,1,0:T(8,128)} %shard_map.104), calls=%async_computation | async-start | bytes 1310720 | tf_op jit(solution)/shard_map/all_to_all | solution.py:474
  36.5 6.5 %collective-permute-start.2 = (bf16[1040,128]{1,0:T(8,128)(2,1)S(1)}, bf16[1040,128]{1,0:T(8,128)(2,1)S(1)}, u32[]{:S(2)}, u32[]{:S(2)}) collective-permute-start(bf16[1040,128]{1,0:T(8,128)(2,1)S(1)} %get-tuple-element.38.own_ref), channel_id=1, source_target_pairs={{0,224},{1,0},{2,1},{3,2},{4,3},{5,4},{6,5},{7,6},{15,7},{14,15},{... | collective-permute-start | bytes 798728 | tf_op jit(solution)/shard_map/ppermute | solution.py:484
  36.6 6.4 %collective-permute-start.1 = (bf16[1040,128]{1,0:T(8,128)(2,1)S(1)}, bf16[1040,128]{1,0:T(8,128)(2,1)S(1)}, u32[]{:S(2)}, u32[]{:S(2)}) collective-permute-start(bf16[1040,128]{1,0:T(8,128)(2,1)S(1)} %get-tuple-element.38.own_ref), channel_id=1, source_target_pairs={{224,0},{0,1},{1,2},{2,3},{3,4},{4,5},{5,6},{6,7},{7,15},{15,14},{... | collective-permute-start | bytes 798728 | tf_op jit(solution)/shard_map/ppermute | solution.py:483
  38.6 0.7 copy-start.7
  49.3 6.5 %collective-permute-start.4 = (bf16[1024,128]{1,0:T(8,128)(2,1)S(1)}, bf16[1024,128]{1,0:T(8,128)(2,1)S(1)}, u32[]{:S(2)}, u32[]{:S(2)}) collective-permute-start(bf16[1024,128]{1,0:T(8,128)(2,1)S(1)} %get-tuple-element.43.own_ref), channel_id=1, source_target_pairs={{0,224},{1,0},{2,1},{3,2},{4,3},{5,4},{6,5},{7,6},{15,7},{14,15},{... | collective-permute-start | bytes 786440 | tf_op jit(solution)/shard_map/ppermute | solution.py:496
  49.4 6.4 %collective-permute-start.3 = (bf16[1024,128]{1,0:T(8,128)(2,1)S(1)}, bf16[1024,128]{1,0:T(8,128)(2,1)S(1)}, u32[]{:S(2)}, u32[]{:S(2)}) collective-permute-start(bf16[1024,128]{1,0:T(8,128)(2,1)S(1)} %get-tuple-element.43.own_ref), channel_id=1, source_target_pairs={{224,0},{0,1},{1,2},{2,3},{3,4},{4,5},{5,6},{6,7},{7,15},{15,14},{... | collective-permute-start | bytes 786440 | tf_op jit(solution)/shard_map/ppermute | solution.py:495
  61.0 22.4 %copy-start = (f32[8,64,2,128]{3,2,1,0:T(2,128)S(1)}, f32[8,64,2,128]{3,2,1,0:T(2,128)}, u32[]{:S(2)}) copy-start(f32[8,64,2,128]{3,2,1,0:T(2,128)} %param.9) | copy-start | bytes 1572868
  61.0 22.4 %copy-start.3 = (s32[8,2,128]{2,1,0:T(2,128)S(1)}, s32[8,2,128]{2,1,0:T(2,128)}, u32[]{:S(2)}) copy-start(s32[8,2,128]{2,1,0:T(2,128)} %param.11) | copy-start | bytes 24580

commit v5 on v4

--- a/solution.py
+++ b/solution.py
@@ -17,7 +17,7 @@
 LANES = 128
 BLOCKS = WIDE // LANES
 STEP = 2 * BLOCKS * 8
-UNROLL = 8
+UNROLL = {"wide": 16, "shrink": 16, "ring": 16, "own": 16}
 f32, bf16 = jnp.float32, jnp.bfloat16
 
 
@@ -91,8 +91,8 @@
             )
 
 
-def spread_kernel(coef_ref, got_ref, fu_ref, fp_ref, mask_ref, send_ref, rows_ref):
-    theta_inv = coef_ref[pl.ds(0, 1), pl.ds(0, LANES)]
+def spread_kernel(spec_ref, got_ref, fu_ref, fp_ref, mask_ref, send_ref, rows_ref):
+    theta_inv = 1.0 / (jnp.full((1, LANES), spec_ref[1] + spec_ref[0], f32) / 2.0)
     for half in range(2):
         for b in range(BLOCKS):
             for x in range(XL):
@@ -165,11 +165,12 @@
     return [jnp.concatenate(columns, axis=1), depth]
 
 
-def layers_of(group):
-    return [group * UNROLL + i for i in range(UNROLL)]
+def layers_of(group, unroll):
+    return [group * unroll + i for i in range(unroll)]
 
 
 def sweep(k, mode, begin, last, refs, old, new):
+    unroll = UNROLL[mode]
     coef_ref, lm_ref, table_ref, mask_ref, state = refs
     count = {"wide": 3, "own": 1}.get(mode, 2)
     lanes = block(LOW if mode == "wide" else OWN, count)
@@ -178,7 +179,7 @@
     scale = coef_ref[pl.ds(3 + 2 * k, 1), block(0, count)]
 
     def group(g, carry):
-        for z in layers_of(g):
+        for z in layers_of(g, unroll):
             z64 = pl.multiple_of(z * BU, BU)
             table = table_ref[lm_ref[z]]
             stack = jnp.concatenate(stack_of(z64, old, mode), axis=0)
@@ -209,7 +210,7 @@
                     ref[rows, inner] = v
         return carry
 
-    lax.fori_loop(0, NZ // UNROLL, group, 0)
+    lax.fori_loop(0, NZ // unroll, group, 0)
 
 
 def starter(coef_ref, own_ref, w_ref, wide):
@@ -277,7 +278,7 @@
 
 def couple(get, lm_ref, coup_ref, mask_ref, rest_ref, sign, q_ref):
     def group(g, carry):
-        for z in layers_of(g):
+        for z in layers_of(g, NZ):
             here = pl.ds(pl.multiple_of(z * PB, PB), PB)
             du = get(pl.multiple_of(z * BU, BU))
             q = jnp.dot(coup_ref[lm_ref[z]], jnp.concatenate(thirds(du), axis=0),
@@ -285,7 +286,7 @@
             q_ref[here, :] = q * mask_ref[z, pl.ds(0, 1), block(OWN)] + sign * rest_ref[here, :]
         return carry
 
-    lax.fori_loop(0, NZ // UNROLL, group, 0)
+    lax.fori_loop(0, 1, group, 0)
 
 
 def bands(schur_ref, q_ref):
@@ -351,7 +352,7 @@
     theta_inv = coef_ref[pl.ds(0, 1), block(0)]
 
     def finish(g, carry):
-        for z in layers_of(g):
+        for z in layers_of(g, 8):
             z64 = pl.multiple_of(z * BU, BU)
             here = pl.ds(pl.multiple_of(z * PB, PB), PB)
             weight = wide_ref[z, pl.ds(0, 1), block(OWN)]
@@ -366,7 +367,7 @@
             send_ref[rows, :] = (ru * theta_inv).astype(bf16)
         return carry
 
-    lax.fori_loop(0, NZ // UNROLL, finish, 0)
+    lax.fori_loop(0, 2, finish, 0)
 
 
 def second_kernel(lm_ref, coef_ref, table_ref, coup_ref, schur_ref,
@@ -448,12 +449,6 @@
     fu_in = force_u.reshape(ZL * BU * YL, LANES)
     fp_in = force_p.reshape(ZL * PB * YL, LANES)
     mask_in = cellmask.reshape(ZL * YL, LANES)
-    coefs, table, pair, matrix = call(
-        prep_kernel, [spectrum, band_offsets], [kblocks, bcoup, sinv],
-        [((8, WIDTH), f32), ((4, BU, 8 * BU), bf16), ((4, PB, 3 * BU), bf16),
-         ((RP, 3 * RP), bf16)], [],
-    )
-
     packed = pl.pallas_call(
         pack_kernel,
         out_shape=jax.ShapeDtypeStruct((CH * BLOCKS, 8, LANES), f32),
@@ -464,21 +459,24 @@
             pltpu.VMEM(mask_in.shape, jnp.int32),
             pltpu.VMEM((YL, BLOCKS, LANES, LANES), f32), pltpu.SemaphoreType.DMA((BLOCKS + 1,)),
         ],
-        compiler_params=pltpu.CompilerParams(vmem_limit_bytes=60 << 20),
-    )(fu_in, fp_in, mask_in)
+        compiler_params=pltpu.CompilerParams(vmem_limit_bytes=24 << 20),
+    )(*(pltpu.with_memory_space_constraint(v, pltpu.HBM) for v in (fu_in, fp_in, mask_in)))
     packed, other = lax.optimization_barrier((packed, other))
     gz = lax.axis_index("gz")
     layers = jnp.where(
         gz == 0, jnp.concatenate([layer_mats, other]), jnp.concatenate([other, layer_mats])
     )
     got = lax.all_to_all(packed, PLANE, 0, 0, tiled=True)
-    got, table, pair, matrix, coefs = lax.optimization_barrier(
-        (got, table, pair, matrix, coefs)
-    )
     fu, fp, mask, send = call(
-        spread_kernel, [], [coefs, got.reshape(CH * BLOCKS * 8, LANES)],
+        spread_kernel, [spectrum], [got.reshape(CH * BLOCKS * 8, LANES)],
         [((RU, LANES), f32), ((RP, LANES), f32), ((NZ, LANES), f32), ((RU + NZ, LANES), bf16)],
         [((BLOCKS, LANES, LANES), f32)],
+    )
+    send, spectrum = lax.optimization_barrier((send, spectrum))
+    coefs, table, pair, matrix = call(
+        prep_kernel, [spectrum, band_offsets], [kblocks, bcoup, sinv],
+        [((8, WIDTH), f32), ((4, BU, 8 * BU), bf16), ((4, PB, 3 * BU), bf16),
+         ((RP, 3 * RP), bf16)], [],
     )
     low = lax.ppermute(send, ALL, up)
     high = lax.ppermute(send, ALL, down)

time: 84.9 us -> 80.9 us (0.953)
  blocking collectives: 22.4 us -> 51.7 us
  waiting for transfers between devices: 26.8 us -> 6.24 us
  starting transfers between devices: 16.9 us -> 6.28 us
  Pallas kernels: 16.8 us -> 13.9 us
    all_to_all x0 -> x1, blocking collectives: none -> 30.3 us  [body(): got = lax.all_to_all(packed, PLANE, 0, 0, tiled=True)]
    all_to_all x1 -> x0, waiting for transfers between devices: 18.9 us -> none  [body(): got = lax.all_to_all(packed, PLANE, 0, 0, tiled=True)]
    all_to_all x1 -> x0, starting transfers between devices: 10.6 us -> none  [body(): got = lax.all_to_all(packed, PLANE, 0, 0, tiled=True)]
    pallas_call x5, Pallas kernels: 14.3 us -> 12.3 us  [call(): pl.pallas_call(kernel, out_shape=[jax.ShapeDtypeStruct(*o) for o in outs]...]
    ppermute x1, waiting for transfers between devices: 3.66 us -> 1.79 us  [body(): high = lax.ppermute(send, ALL, down)]
    all_to_all x1, blocking collectives: 22.4 us -> 21.4 us  [body(): lax.all_to_all(back.reshape(CH * BLOCKS, 8, LANES), PLANE, 0, 0, tiled=True)]
    pallas_call x1, Pallas kernels: 2.52 us -> 1.59 us  [body(): pl.pallas_call(pack_kernel, out_shape=jax.ShapeDtypeStruct((CH * BLOCKS,...]
  transfers between devices with their start and end apart: 6 -> 5, of which waited for: 3 -> 3; matrix products, arithmetic and copies ran while one was open for 0% -> 0% of each run, Pallas kernels for 4% -> 4%
where the time goes in v5:
time: 80.9 us; the launch traced here: 80.2 us
  blocking collectives  51.7 us (64%)
  Pallas kernels  13.9 us (17%)
  starting transfers between devices  6.28 us (8%)
  waiting for transfers between devices  6.24 us (8%)
  local copies, waits for them, and re-layouts  1.25 us (2%)
    all_to_all x1, blocking collectives, body(): got = lax.all_to_all(packed, PLANE, 0, 0, tiled=True)  30.3 us
    all_to_all x1, blocking collectives, body(): lax.all_to_all(back.reshape(CH * BLOCKS, 8, LANES), PLANE, 0, 0, tiled=True)  21.4 us
    pallas_call x5, Pallas kernels, call(): pl.pallas_call(kernel, out_shape=[jax.ShapeDtypeStruct(*o) for o in outs]...  12.3 us
    ppermute x1, waiting for transfers between devices, body(): high2 = lax.ppermute(send2, ALL, down)  4.27 us
    ppermute x1, starting transfers between devices, body(): low2 = lax.ppermute(send2, ALL, up)  2.09 us
    ppermute x1, starting transfers between devices, body(): low = lax.ppermute(send, ALL, up)  2.01 us
    ppermute x1, starting transfers between devices, body(): other = lax.ppermute(layer_mats, 'gz', [(0, 1), (1, 0)])  2 us
    ppermute x1, waiting for transfers between devices, body(): high = lax.ppermute(send, ALL, down)  1.79 us
  transfers between devices with their start and end apart: 5, of which 3 were waited for; matrix products, arithmetic and copies ran while one was open for 0% of the time, Pallas kernels for 4%

profile of v5, /device:TPU:16, one launch (start us, length us, event | category | flops | bytes accessed | tf_op | source)
XLA Modules:
  0.0 80.2 jit_solution(15242031115165812145)
XLA Ops:
  0.6 2.0 %collective-permute-start = (s32[8]{0:T(128)}, s32[8]{0:T(128)S(1)}, u32[]{:S(2)}, u32[]{:S(2)}) collective-permute-start(s32[8]{0:T(128)} %param.12), channel_id=1, source_target_pairs={{0,1},{1,0},{2,3},{3,2},{4,5},{5,4},{6,7},{7,6},{8,9},{9,8},{10,11... | collective-permute-start | bytes 104 | tf_op jit(solution)/shard_map/ppermute | solution.py:448
  2.6 1.6 %shard_map.104 = f32[160,8,128]{2,1,0:T(8,128)S(1)} custom-call(f32[1024,128]{1,0:T(8,128)} %bitcast.8, f32[256,128]{1,0:T(8,128)} %bitcast.13, s32[16,128]{1,0:T(8,128)} %bitcast.11), custom_call_target="tpu_custom_call" | custom-call | tf_op jit(solution)/shard_map/pallas_call | solution.py:452
  4.2 0.0 copy-start.1
  4.2 0.2 collective-permute-done
  4.4 0.0 copy-start.5
  4.4 30.3 %all_to_all.10 = f32[160,8,128]{2,1,0:T(8,128)S(1)} all-to-all(f32[160,8,128]{2,1,0:T(8,128)S(1)} %shard_map.104), channel_id=1, replica_groups=mesh['gx'=8,'gy'=16,'gz'=2] {'gy','gz'}, dimensions={0} | all-to-all | bytes 1310720 | tf_op jit(solution)/shard_map/all_to_all | solution.py:469
  34.8 0.0 copy-start.2
  34.8 0.0 copy-done.5
  34.8 1.0 %shard_map.105 = (f32[1024,128]{1,0:T(8,128)S(1)}, f32[256,128]{1,0:T(8,128)S(1)}, f32[16,128]{1,0:T(8,128)S(1)}, bf16[1040,128]{1,0:T(8,128)(2,1)S(1)}) custom-call(f32[2]{0:T(128)S(1)} %copy-done.5, f32[1280,128]{1,0:T(8,128)S(1)} %bitcast.7), custom_call_target="tpu_custom_call" | custom-call | tf_op jit(solution)/shard_map/pallas_call | solution.py:436
  35.8 0.1 collective-permute-start.2
  35.8 2.0 %collective-permute-start.1 = (bf16[1040,128]{1,0:T(8,128)(2,1)S(1)}, bf16[1040,128]{1,0:T(8,128)(2,1)S(1)}, u32[]{:S(2)}, u32[]{:S(2)}) collective-permute-start(bf16[1040,128]{1,0:T(8,128)(2,1)S(1)} %get-tuple-element.32.own_ref), channel_id=1, source_target_pairs={{224,0},{0,1},{1,2},{2,3},{3,4},{4,5},{5,6},{6,7},{7,15},{15,14},{... | collective-permute-start | bytes 798728 | tf_op jit(solution)/shard_map/ppermute | solution.py:481
  37.9 0.7 copy-done.7
  38.5 0.1 broadcast_select_fusion.lm_ref
  38.6 0.0 copy-done.1
  38.6 0.0 copy-done.2
  38.6 0.0 copy-done.4
  38.6 0.6 copy-done.6
  39.2 1.3 %shard_map.106 = (f32[8,512]{1,0:T(8,128)S(1)}, bf16[4,64,512]{2,1,0:T(8,128)(2,1)S(1)}, bf16[4,16,192]{2,1,0:T(8,128)(2,1)S(1)}, bf16[256,768]{1,0:T(8,128)(2,1)S(1)}) custom-call(f32[2]{0:T(128)S(1)} %copy-done.5, s32[8]{0:T(128)S(1)} %copy-done.6, bf16[4,7,64,64]{3,2,1,0:T(8,128)(2,1)S(1)} %copy-done.2, f32[4,16,64]{2,1,0:T(8,128)S(1)} %copy-done.4, ...), custom_call_target="tpu_custom_call" | custom-call | tf_op jit(solution)/shard_map/pallas_call | solution.py:436
  40.5 1.8 %collective-permute-done.2.high_ref.mhigh_ref = bf16[1040,128]{1,0:T(8,128)(2,1)S(1)} collective-permute-done((bf16[1040,128]{1,0:T(8,128)(2,1)S(1)}, bf16[1040,128]{1,0:T(8,128)(2,1)S(1)}, u32[]{:S(2)}, u32[]{:S(2)}) %collective-permute-start.2) | collective-permute-done | bytes 266272 | tf_op jit(solution)/shard_map/ppermute | solution.py:482
  42.3 0.0 collective-permute-done.1.low_ref.mlow_ref
  42.3 5.1 %shard_map.107 = (f32[1024,128]{1,0:T(8,128)S(1)}, f32[1024,128]{1,0:T(8,128)S(1)}, f32[256,128]{1,0:T(8,128)S(1)}, f32[256,128]{1,0:T(8,128)S(1)}, bf16[1024,128]{1,0:T(8,128)(2,1)S(1)}) custom-call(s32[16]{0:T(128)S(1)} %broadcast_select_fusion.lm_ref, f32[8,512]{1,0:T(8,128)S(1)} %get-tuple-element.25.coef_ref, ...), custom_call_target="tpu_custom_call" | custom-call | tf_op jit(solution)/shard_map/pallas_call | solution.py:436
  47.4 0.1 collective-permute-start.4
  47.5 2.1 %collective-permute-start.3 = (bf16[1024,128]{1,0:T(8,128)(2,1)S(1)}, bf16[1024,128]{1,0:T(8,128)(2,1)S(1)}, u32[]{:S(2)}, u32[]{:S(2)}) collective-permute-start(bf16[1024,128]{1,0:T(8,128)(2,1)S(1)} %get-tuple-element.37.own_ref), channel_id=1, source_target_pairs={{224,0},{0,1},{1,2},{2,3},{3,4},{4,5},{5,6},{6,7},{7,15},{15,14},{... | collective-permute-start | bytes 786440 | tf_op jit(solution)/shard_map/ppermute | solution.py:493
  49.6 4.3 %collective-permute-done.4.high_ref = bf16[1024,128]{1,0:T(8,128)(2,1)S(1)} collective-permute-done((bf16[1024,128]{1,0:T(8,128)(2,1)S(1)}, bf16[1024,128]{1,0:T(8,128)(2,1)S(1)}, u32[]{:S(2)}, u32[]{:S(2)}) %collective-permute-start.4) | collective-permute-done | bytes 262176 | tf_op jit(solution)/shard_map/ppermute | solution.py:494
  53.9 0.0 collective-permute-done.3.low_ref
  53.9 3.8 %shard_map.108 = bf16[1280,128]{1,0:T(8,128)(2,1)S(1)} custom-call(s32[16]{0:T(128)S(1)} %broadcast_select_fusion.lm_ref, f32[8,512]{1,0:T(8,128)S(1)} %get-tuple-element.25.coef_ref, bf16[4,64,512]{2,1,0:T(8,128)(2,1)S(1)} %get-tuple-element.26.table_ref, bf16[4,16,192]{2,1,0:T(8,128)(2,1)S(1)} %get-tuple-element.27.coup_ref, ...), custom_call_target="tpu_custom_call" | custom-call | tf_op jit(solution)/shard_map/pallas_call | solution.py:436
  57.6 0.0 copy-start
  57.7 0.0 copy-start.3
  57.7 21.4 %all_to_all.11.got_ref = bf16[160,8,128]{2,1,0:T(8,128)(2,1)S(1)} all-to-all(bf16[160,8,128]{2,1,0:T(8,128)(2,1)S(1)} %bitcast.10), channel_id=1, replica_groups=mesh['gx'=8,'gy'=16,'gz'=2] {'gy','gz'}, dimensions={0} | all-to-all | bytes 655360 | tf_op jit(solution)/shard_map/all_to_all | solution.py:502
  79.1 0.0 copy-done
  79.1 0.0 copy-done.3
  79.1 1.1 %shard_map.109 = (f32[1024,128]{1,0:T(8,128)}, f32[256,128]{1,0:T(8,128)}) custom-call(bf16[160,8,128]{2,1,0:T(8,128)(2,1)S(1)} %all_to_all.11.got_ref, f32[1024,128]{1,0:T(8,128)S(1)} %bitcast.9, s32[16,128]{1,0:T(8,128)S(1)} %bitcast.12), custom_call_target="tpu_custom_call" | custom-call | tf_op jit(solution)/shard_map/pallas_call | solution.py:436
  (3 shorter events, 0.0 us)
Async XLA Ops:
  0.6 3.8 %collective-permute-start = (s32[8]{0:T(128)}, s32[8]{0:T(128)S(1)}, u32[]{:S(2)}, u32[]{:S(2)}) collective-permute-start(s32[8]{0:T(128)} %param.12), channel_id=1, source_target_pairs={{0,1},{1,0},{2,3},{3,2},{4,5},{5,4},{6,7},{7,6},{8,9},{9,8},{10,11... | collective-permute-start | bytes 104 | tf_op jit(solution)/shard_map/ppermute | solution.py:448
  4.2 34.4 %copy-start.1 = (f32[8,16,16,16]{3,2,1,0:T(8,128)S(1)}, f32[8,16,16,16]{3,2,1,0:T(8,128)}, u32[]{:S(2)}) copy-start(f32[8,16,16,16]{3,2,1,0:T(8,128)} %sinv_ref.1) | copy-start | bytes 393220
  4.4 30.3 %copy-start.5 = (f32[2]{0:T(128)S(1)}, f32[2]{0:T(128)}, u32[]{:S(2)}) copy-start(f32[2]{0:T(128)} %spec_ref.2) | copy-start | bytes 28
  34.8 3.8 %copy-start.2 = (bf16[4,7,64,64]{3,2,1,0:T(8,128)(2,1)S(1)}, bf16[4,7,64,64]{3,2,1,0:T(8,128)(2,1)}, u32[]{:S(2)}) copy-start(bf16[4,7,64,64]{3,2,1,0:T(8,128)(2,1)} %kb_ref.1) | copy-start | bytes 688132
  34.8 3.8 %copy-start.4 = (f32[4,16,64]{2,1,0:T(8,128)S(1)}, f32[4,16,64]{2,1,0:T(8,128)}, u32[]{:S(2)}) copy-start(f32[4,16,64]{2,1,0:T(8,128)} %coup_ref.1) | copy-start | bytes 49156
  35.8 6.5 %collective-permute-start.2 = (bf16[1040,128]{1,0:T(8,128)(2,1)S(1)}, bf16[1040,128]{1,0:T(8,128)(2,1)S(1)}, u32[]{:S(2)}, u32[]{:S(2)}) collective-permute-start(bf16[1040,128]{1,0:T(8,128)(2,1)S(1)} %get-tuple-element.32.own_ref), channel_id=1, source_target_pairs={{0,224},{1,0},{2,1},{3,2},{4,3},{5,4},{6,5},{7,6},{15,7},{14,15},{... | collective-permute-start | bytes 798728 | tf_op jit(solution)/shard_map/ppermute | solution.py:482
  35.8 6.4 %collective-permute-start.1 = (bf16[1040,128]{1,0:T(8,128)(2,1)S(1)}, bf16[1040,128]{1,0:T(8,128)(2,1)S(1)}, u32[]{:S(2)}, u32[]{:S(2)}) collective-permute-start(bf16[1040,128]{1,0:T(8,128)(2,1)S(1)} %get-tuple-element.32.own_ref), channel_id=1, source_target_pairs={{224,0},{0,1},{1,2},{2,3},{3,4},{4,5},{5,6},{6,7},{7,15},{15,14},{... | collective-permute-start | bytes 798728 | tf_op jit(solution)/shard_map/ppermute | solution.py:481
  37.9 0.7 copy-start.7
  38.5 0.7 copy-start.6
  47.4 6.5 %collective-permute-start.4 = (bf16[1024,128]{1,0:T(8,128)(2,1)S(1)}, bf16[1024,128]{1,0:T(8,128)(2,1)S(1)}, u32[]{:S(2)}, u32[]{:S(2)}) collective-permute-start(bf16[1024,128]{1,0:T(8,128)(2,1)S(1)} %get-tuple-element.37.own_ref), channel_id=1, source_target_pairs={{0,224},{1,0},{2,1},{3,2},{4,3},{5,4},{6,5},{7,6},{15,7},{14,15},{... | collective-permute-start | bytes 786440 | tf_op jit(solution)/shard_map/ppermute | solution.py:494
  47.5 6.4 %collective-permute-start.3 = (bf16[1024,128]{1,0:T(8,128)(2,1)S(1)}, bf16[1024,128]{1,0:T(8,128)(2,1)S(1)}, u32[]{:S(2)}, u32[]{:S(2)}) collective-permute-start(bf16[1024,128]{1,0:T(8,128)(2,1)S(1)} %get-tuple-element.37.own_ref), channel_id=1, source_target_pairs={{224,0},{0,1},{1,2},{2,3},{3,4},{4,5},{5,6},{6,7},{7,15},{15,14},{... | collective-permute-start | bytes 786440 | tf_op jit(solution)/shard_map/ppermute | solution.py:493
  57.6 21.4 %copy-start = (f32[8,64,2,128]{3,2,1,0:T(2,128)S(1)}, f32[8,64,2,128]{3,2,1,0:T(2,128)}, u32[]{:S(2)}) copy-start(f32[8,64,2,128]{3,2,1,0:T(2,128)} %param.9) | copy-start | bytes 1572868
  57.7 21.4 %copy-start.3 = (s32[8,2,128]{2,1,0:T(2,128)S(1)}, s32[8,2,128]{2,1,0:T(2,128)}, u32[]{:S(2)}) copy-start(s32[8,2,128]{2,1,0:T(2,128)} %param.11) | copy-start | bytes 24580

commit v6 on v5

--- a/solution.py
+++ b/solution.py
@@ -16,6 +16,7 @@
 WIDE = HU + HP
 LANES = 128
 BLOCKS = WIDE // LANES
+PACKED = NZ * 3 // 4
 STEP = 2 * BLOCKS * 8
 UNROLL = {"wide": 16, "shrink": 16, "ring": 16, "own": 16}
 f32, bf16 = jnp.float32, jnp.bfloat16
@@ -133,29 +134,36 @@
 def stack_of(z64, w_ref, mode):
     lane = lane_of(BU)
     y = lane % NY
-    ins = {"wide": (LOW, HIGH, OWN), "shrink": (LOW, HIGH, OWN), "ring": (OWN, EDGE),
-           "own": (OWN, EDGE)}[mode]
     outs = {"wide": (LOW, HIGH, OWN), "shrink": (OWN, EDGE), "ring": (OWN, EDGE),
             "own": (OWN,)}[mode]
     rows = pl.ds(z64 + BU, BU)
-    part = {b: w_ref[rows, block(b)] for b in sorted(set(ins) | set(outs))}
-    up = {b: pltpu.roll(part[b], NY, 1) for b in ins}
-    down = {b: pltpu.roll(part[b], LANES - NY, 1) for b in ins}
+    near = {"wide": (), "shrink": (LOW, HIGH), "ring": (), "own": (EDGE,)}[mode]
+    part = {b: w_ref[rows, block(b)] for b in outs + near}
     zero = jnp.zeros_like(part[OWN])
-    first, half, tail = lane < NY, lane < LANES // 2, lane >= LANES - NY
-    if mode in ("wide", "shrink"):
-        below = {LOW: up[LOW], OWN: jnp.where(first, up[LOW], up[OWN])}
-        above = {HIGH: down[HIGH], OWN: jnp.where(tail, down[HIGH], down[OWN])}
-        if mode == "wide":
-            below[HIGH] = jnp.where(first, up[OWN], up[HIGH])
-            above[LOW] = jnp.where(tail, down[OWN], down[LOW])
-        else:
-            below[EDGE] = jnp.where(first, up[OWN], jnp.where(half, up[HIGH], up[LOW]))
-            above[EDGE] = jnp.where(tail, down[OWN], jnp.where(half, down[HIGH], down[LOW]))
-    else:
+    first, tail = lane < NY, lane >= LANES - NY
+    if mode in ("wide", "ring"):
+        up = {b: pltpu.roll(part[b], NY, 1) for b in outs}
+        down = {b: pltpu.roll(part[b], LANES - NY, 1) for b in outs}
+    if mode == "wide":
+        below = {LOW: up[LOW], OWN: jnp.where(first, up[LOW], up[OWN]),
+                 HIGH: jnp.where(first, up[OWN], up[HIGH])}
+        above = {HIGH: down[HIGH], OWN: jnp.where(tail, down[HIGH], down[OWN]),
+                 LOW: jnp.where(tail, down[OWN], down[LOW])}
+    elif mode == "ring":
         below = {OWN: jnp.where(first, up[EDGE], up[OWN]), EDGE: jnp.where(first, up[OWN], up[EDGE])}
         above = {OWN: jnp.where(tail, down[EDGE], down[OWN]),
                  EDGE: jnp.where(tail, down[OWN], down[EDGE])}
+    else:
+        if mode == "shrink":
+            under = {OWN: jnp.where(tail, part[LOW], part[OWN]),
+                     EDGE: jnp.where(first, part[HIGH], jnp.where(tail, part[OWN], part[LOW]))}
+            over = {OWN: jnp.where(first, part[HIGH], part[OWN]),
+                    EDGE: jnp.where(first, part[OWN], jnp.where(tail, part[LOW], part[HIGH]))}
+        else:
+            under = {OWN: jnp.where(tail, part[EDGE], part[OWN])}
+            over = {OWN: jnp.where(first, part[EDGE], part[OWN])}
+        below = {b: pltpu.roll(under[b], NY, 1) for b in outs}
+        above = {b: pltpu.roll(over[b], LANES - NY, 1) for b in outs}
     columns = []
     for b in outs:
         below_y = jnp.where(y == 0, zero, pltpu.roll(part[b], 1, 1))
@@ -245,13 +253,31 @@
         wide_ref[z] = jnp.broadcast_to(whole[z : z + 1], (8, WIDTH))
 
 
+def unfold(z, src_ref, shifted):
+    if z < PACKED:
+        return src_ref[pl.ds(z * BU, BU), :]
+    pieces = [src_ref[pl.ds((3 * (z - PACKED) + at) * BU, BU), :] for at in range(3)]
+    if shifted:
+        pieces = [pltpu.roll(p, NY * (at + 1), 1) for at, p in enumerate(pieces)]
+        edges = (2 * NY, 3 * NY)
+    else:
+        pieces = [pltpu.roll(p, LANES - NY * (3 - at), 1) for at, p in enumerate(pieces)]
+        edges = (NY, 2 * NY)
+    lane = lane_of(BU)
+    return jnp.where(lane < edges[0], pieces[0], jnp.where(lane < edges[1], pieces[1], pieces[2]))
+
+
 def pad_in(w_refs, low_ref, high_ref, own_ref, with_edge):
     edge = jnp.zeros((BU, WIDTH), bf16)
     for w_ref in w_refs:
         w_ref[pl.ds(0, BU), :] = edge
         w_ref[pl.ds(RU + BU, BU), :] = edge
     for b, src in ((LOW, low_ref), (HIGH, high_ref), (OWN, own_ref)):
-        w_refs[0][pl.ds(BU, RU), block(b)] = src[pl.ds(0, RU), :]
+        if b != OWN and with_edge:
+            for z in range(NZ):
+                w_refs[0][pl.ds(z * BU + BU, BU), block(b)] = unfold(z, src, b == LOW)
+        else:
+            w_refs[0][pl.ds(BU, RU), block(b)] = src[pl.ds(0, RU), :]
     inner = pl.ds(BU, RU)
     for b, group in ((LOW, 0), (HIGH, 7)):
 
@@ -333,7 +359,7 @@
 
 def first_kernel(lm_ref, coef_ref, table_ref, coup_ref, schur_ref,
                  fu_ref, fp_ref, mask_ref, own_ref, low_ref, high_ref,
-                 ru_ref, du_ref, dp_ref, q_ref, send_ref,
+                 ru_ref, du_ref, dp_ref, q_ref, send_ref, up_ref, down_ref,
                  wide_ref, d_ref, r_ref, s_ref, wa_ref, wb_ref):
     widen(wide_ref, mask_ref, low_ref, high_ref)
     pad_in((wa_ref, wb_ref), low_ref, high_ref, own_ref, False)
@@ -368,6 +394,16 @@
         return carry
 
     lax.fori_loop(0, 2, finish, 0)
+    lane = lane_of(BU)
+    for z in range(PACKED):
+        rows, spare = pl.ds(z * BU, BU), pl.ds((PACKED + z // 3) * BU, BU)
+        mine, moved, at = send_ref[rows, :], send_ref[spare, :], z % 3
+        up_ref[rows, :] = jnp.where(
+            lane < NY, pltpu.roll(moved, LANES - NY * (at + 1), 1), mine
+        )
+        down_ref[rows, :] = jnp.where(
+            lane >= 3 * NY, pltpu.roll(moved, NY * (3 - at), 1), mine
+        )
 
 
 def second_kernel(lm_ref, coef_ref, table_ref, coup_ref, schur_ref,
@@ -483,15 +519,15 @@
     wide = [((NZ, 8, WIDTH), f32)] + [((RU, 2 * LANES), f32)] * 3 + [
         ((RU + 2 * BU, WIDTH), bf16)
     ] * 2
-    ru, du, dp, q, send2 = call(
+    ru, du, dp, q, send2, up2, down2 = call(
         first_kernel, [layers],
         [coefs, table, pair, matrix, fu, fp, mask, send, low, high],
         [((RU, LANES), f32), ((RU, LANES), f32), ((RP, LANES), f32), ((RP, LANES), f32),
-         ((RU, LANES), bf16)],
+         ((RU, LANES), bf16), ((PACKED * BU, LANES), bf16), ((PACKED * BU, LANES), bf16)],
         wide,
     )
-    low2 = lax.ppermute(send2, ALL, up)
-    high2 = lax.ppermute(send2, ALL, down)
+    low2 = lax.ppermute(up2, ALL, up)
+    high2 = lax.ppermute(down2, ALL, down)
     (back,) = call(
         second_kernel, [layers],
         [coefs, table, pair, matrix, fu, mask, ru, du, dp, q, send2, low2, high2, low, high],

time: 80.9 us -> 79.9 us (0.988)
  blocking collectives: 51.7 us -> 50.2 us
  waiting for transfers between devices: 6.24 us -> 7.62 us
    all_to_all x1, blocking collectives: 21.4 us -> 19.9 us  [body(): lax.all_to_all(back.reshape(CH * BLOCKS, 8, LANES), PLANE, 0, 0, tiled=True)]
    ppermute x2, waiting for transfers between devices: 4.27 us -> 5.67 us  [the longest x1 3.19 us: body(): low2 = lax.ppermute(up2, ALL, up)]
  transfers between devices with their start and end apart: 5 -> 5, of which waited for: 3 -> 4; matrix products, arithmetic and copies ran while one was open for 0% -> 0% of each run, Pallas kernels for 4% -> 4%
where the time goes in v6:
time: 79.9 us; the launch traced here: 79.2 us
  blocking collectives  50.2 us (63%)
  Pallas kernels  13.2 us (17%)
  waiting for transfers between devices  7.62 us (10%)
  starting transfers between devices  6.2 us (8%)
  local copies, waits for them, and re-layouts  1.25 us (2%)
    all_to_all x1, blocking collectives, body(): got = lax.all_to_all(packed, PLANE, 0, 0, tiled=True)  30.3 us
    all_to_all x1, blocking collectives, body(): lax.all_to_all(back.reshape(CH * BLOCKS, 8, LANES), PLANE, 0, 0, tiled=True)  19.9 us
    pallas_call x5, Pallas kernels, call(): pl.pallas_call(kernel, out_shape=[jax.ShapeDtypeStruct(*o) for o in outs]...  11.6 us
    ppermute x1, waiting for transfers between devices, body(): low2 = lax.ppermute(up2, ALL, up)  3.19 us
    ppermute x1, waiting for transfers between devices, body(): high2 = lax.ppermute(down2, ALL, down)  2.48 us
    ppermute x1, starting transfers between devices, body(): low2 = lax.ppermute(up2, ALL, up)  2.1 us
    ppermute x1, starting transfers between devices, body(): low = lax.ppermute(send, ALL, up)  2.01 us
    ppermute x1, starting transfers between devices, body(): other = lax.ppermute(layer_mats, 'gz', [(0, 1), (1, 0)])  2 us
  transfers between devices with their start and end apart: 5, of which 4 were waited for; matrix products, arithmetic and copies ran while one was open for 0% of the time, Pallas kernels for 4%

profile of v6, /device:TPU:16, one launch (start us, length us, event | category | flops | bytes accessed | tf_op | source)
XLA Modules:
  0.0 79.2 jit_solution(10251711831748567497)
XLA Ops:
  0.6 2.0 %collective-permute-start = (s32[8]{0:T(128)}, s32[8]{0:T(128)S(1)}, u32[]{:S(2)}, u32[]{:S(2)}) collective-permute-start(s32[8]{0:T(128)} %param.12), channel_id=1, source_target_pairs={{0,1},{1,0},{2,3},{3,2},{4,5},{5,4},{6,7},{7,6},{8,9},{9,8},{10,11... | collective-permute-start | bytes 104 | tf_op jit(solution)/shard_map/ppermute | solution.py:484
  2.6 1.6 %shard_map.104 = f32[160,8,128]{2,1,0:T(8,128)S(1)} custom-call(f32[1024,128]{1,0:T(8,128)} %bitcast.8, f32[256,128]{1,0:T(8,128)} %bitcast.13, s32[16,128]{1,0:T(8,128)} %bitcast.11), custom_call_target="tpu_custom_call" | custom-call | tf_op jit(solution)/shard_map/pallas_call | solution.py:488
  4.2 0.0 copy-start.1
  4.2 0.2 collective-permute-done
  4.4 0.0 copy-start.5
  4.4 30.3 %all_to_all.10 = f32[160,8,128]{2,1,0:T(8,128)S(1)} all-to-all(f32[160,8,128]{2,1,0:T(8,128)S(1)} %shard_map.104), channel_id=1, replica_groups=mesh['gx'=8,'gy'=16,'gz'=2] {'gy','gz'}, dimensions={0} | all-to-all | bytes 1310720 | tf_op jit(solution)/shard_map/all_to_all | solution.py:505
  34.8 0.0 copy-start.2
  34.8 0.0 copy-done.5
  34.8 1.0 %shard_map.105 = (f32[1024,128]{1,0:T(8,128)S(1)}, f32[256,128]{1,0:T(8,128)S(1)}, f32[16,128]{1,0:T(8,128)S(1)}, bf16[1040,128]{1,0:T(8,128)(2,1)S(1)}) custom-call(f32[2]{0:T(128)S(1)} %copy-done.5, f32[1280,128]{1,0:T(8,128)S(1)} %bitcast.7), custom_call_target="tpu_custom_call" | custom-call | tf_op jit(solution)/shard_map/pallas_call | solution.py:472
  35.8 0.1 collective-permute-start.2
  35.8 2.0 %collective-permute-start.1 = (bf16[1040,128]{1,0:T(8,128)(2,1)S(1)}, bf16[1040,128]{1,0:T(8,128)(2,1)S(1)}, u32[]{:S(2)}, u32[]{:S(2)}) collective-permute-start(bf16[1040,128]{1,0:T(8,128)(2,1)S(1)} %get-tuple-element.34.own_ref), channel_id=1, source_target_pairs={{224,0},{0,1},{1,2},{2,3},{3,4},{4,5},{5,6},{6,7},{7,15},{15,14},{... | collective-permute-start | bytes 798728 | tf_op jit(solution)/shard_map/ppermute | solution.py:517
  37.9 0.7 copy-done.7
  38.5 0.1 broadcast_select_fusion.lm_ref
  38.6 0.0 copy-done.1
  38.6 0.0 copy-done.2
  38.6 0.0 copy-done.4
  38.6 0.6 copy-done.6
  39.2 1.3 %shard_map.106 = (f32[8,512]{1,0:T(8,128)S(1)}, bf16[4,64,512]{2,1,0:T(8,128)(2,1)S(1)}, bf16[4,16,192]{2,1,0:T(8,128)(2,1)S(1)}, bf16[256,768]{1,0:T(8,128)(2,1)S(1)}) custom-call(f32[2]{0:T(128)S(1)} %copy-done.5, s32[8]{0:T(128)S(1)} %copy-done.6, bf16[4,7,64,64]{3,2,1,0:T(8,128)(2,1)S(1)} %copy-done.2, f32[4,16,64]{2,1,0:T(8,128)S(1)} %copy-done.4, ...), custom_call_target="tpu_custom_call" | custom-call | tf_op jit(solution)/shard_map/pallas_call | solution.py:472
  40.5 1.8 %collective-permute-done.2.high_ref.mhigh_ref = bf16[1040,128]{1,0:T(8,128)(2,1)S(1)} collective-permute-done((bf16[1040,128]{1,0:T(8,128)(2,1)S(1)}, bf16[1040,128]{1,0:T(8,128)(2,1)S(1)}, u32[]{:S(2)}, u32[]{:S(2)}) %collective-permute-start.2) | collective-permute-done | bytes 266272 | tf_op jit(solution)/shard_map/ppermute | solution.py:518
  42.3 0.0 collective-permute-done.1.low_ref.mlow_ref
  42.3 4.9 %shard_map.107 = (f32[1024,128]{1,0:T(8,128)S(1)}, f32[1024,128]{1,0:T(8,128)S(1)}, f32[256,128]{1,0:T(8,128)S(1)}, f32[256,128]{1,0:T(8,128)S(1)}, bf16[1024,12...) custom-call(s32[16]{0:T(128)S(1)} %broadcast_select_fusion.lm_ref, ...), custom_call_target="tpu_custom_call" | custom-call | tf_op jit(solution)/shard_map/pallas_call | solution.py:472
  47.1 2.1 %collective-permute-start.3 = (bf16[768,128]{1,0:T(8,128)(2,1)S(1)}, bf16[768,128]{1,0:T(8,128)(2,1)S(1)}, u32[]{:S(2)}, u32[]{:S(2)}) collective-permute-start(bf16[768,128]{1,0:T(8,128)(2,1)S(1)} %get-tuple-element.40), channel_id=1, source_target_pairs={{224,0},{0,1},{1,2},{2,3},{3,4},{4,5},{5,6},{6,7},{7,15},{15,14},{... | collective-permute-start | bytes 589832 | tf_op jit(solution)/shard_map/ppermute | solution.py:529
  49.2 0.0 collective-permute-start.4
  49.2 3.2 %collective-permute-done.3.low_ref = bf16[768,128]{1,0:T(8,128)(2,1)S(1)} collective-permute-done((bf16[768,128]{1,0:T(8,128)(2,1)S(1)}, bf16[768,128]{1,0:T(8,128)(2,1)S(1)}, u32[]{:S(2)}, u32[]{:S(2)}) %collective-permute-start.3) | collective-permute-done | bytes 196640 | tf_op jit(solution)/shard_map/ppermute | solution.py:529
  52.4 2.5 %collective-permute-done.4.high_ref = bf16[768,128]{1,0:T(8,128)(2,1)S(1)} collective-permute-done((bf16[768,128]{1,0:T(8,128)(2,1)S(1)}, bf16[768,128]{1,0:T(8,128)(2,1)S(1)}, u32[]{:S(2)}, u32[]{:S(2)}) %collective-permute-start.4) | collective-permute-done | bytes 196640 | tf_op jit(solution)/shard_map/ppermute | solution.py:530
  54.9 3.3 %shard_map.108 = bf16[1280,128]{1,0:T(8,128)(2,1)S(1)} custom-call(s32[16]{0:T(128)S(1)} %broadcast_select_fusion.lm_ref, f32[8,512]{1,0:T(8,128)S(1)} %get-tuple-element.27.coef_ref, bf16[4,64,512]{2,1,0:T(8,128)(2,1)S(1)} %get-tuple-element.28.table_ref, bf16[4,16,192]{2,1,0:T(8,128)(2,1)S(1)} %get-tuple-element.29.coup_ref, ...), custom_call_target="tpu_custom_call" | custom-call | tf_op jit(solution)/shard_map/pallas_call | solution.py:472
  58.2 0.0 copy-start
  58.2 0.0 copy-start.3
  58.2 19.9 %all_to_all.11.got_ref = bf16[160,8,128]{2,1,0:T(8,128)(2,1)S(1)} all-to-all(bf16[160,8,128]{2,1,0:T(8,128)(2,1)S(1)} %bitcast.10), channel_id=1, replica_groups=mesh['gx'=8,'gy'=16,'gz'=2] {'gy','gz'}, dimensions={0} | all-to-all | bytes 655360 | tf_op jit(solution)/shard_map/all_to_all | solution.py:538
  78.1 0.0 copy-done
  78.1 0.0 copy-done.3
  78.1 1.1 %shard_map.109 = (f32[1024,128]{1,0:T(8,128)}, f32[256,128]{1,0:T(8,128)}) custom-call(bf16[160,8,128]{2,1,0:T(8,128)(2,1)S(1)} %all_to_all.11.got_ref, f32[1024,128]{1,0:T(8,128)S(1)} %bitcast.9, s32[16,128]{1,0:T(8,128)S(1)} %bitcast.12), custom_call_target="tpu_custom_call" | custom-call | tf_op jit(solution)/shard_map/pallas_call | solution.py:472
  (3 shorter events, 0.0 us)
Async XLA Ops:
  0.6 3.8 %collective-permute-start = (s32[8]{0:T(128)}, s32[8]{0:T(128)S(1)}, u32[]{:S(2)}, u32[]{:S(2)}) collective-permute-start(s32[8]{0:T(128)} %param.12), channel_id=1, source_target_pairs={{0,1},{1,0},{2,3},{3,2},{4,5},{5,4},{6,7},{7,6},{8,9},{9,8},{10,11... | collective-permute-start | bytes 104 | tf_op jit(solution)/shard_map/ppermute | solution.py:484
  4.2 34.4 %copy-start.1 = (f32[8,16,16,16]{3,2,1,0:T(8,128)S(1)}, f32[8,16,16,16]{3,2,1,0:T(8,128)}, u32[]{:S(2)}) copy-start(f32[8,16,16,16]{3,2,1,0:T(8,128)} %sinv_ref.1) | copy-start | bytes 393220
  4.4 30.3 %copy-start.5 = (f32[2]{0:T(128)S(1)}, f32[2]{0:T(128)}, u32[]{:S(2)}) copy-start(f32[2]{0:T(128)} %spec_ref.2) | copy-start | bytes 28
  34.8 3.8 %copy-start.2 = (bf16[4,7,64,64]{3,2,1,0:T(8,128)(2,1)S(1)}, bf16[4,7,64,64]{3,2,1,0:T(8,128)(2,1)}, u32[]{:S(2)}) copy-start(bf16[4,7,64,64]{3,2,1,0:T(8,128)(2,1)} %kb_ref.1) | copy-start | bytes 688132
  34.8 3.8 %copy-start.4 = (f32[4,16,64]{2,1,0:T(8,128)S(1)}, f32[4,16,64]{2,1,0:T(8,128)}, u32[]{:S(2)}) copy-start(f32[4,16,64]{2,1,0:T(8,128)} %coup_ref.1) | copy-start | bytes 49156
  35.8 6.5 %collective-permute-start.2 = (bf16[1040,128]{1,0:T(8,128)(2,1)S(1)}, bf16[1040,128]{1,0:T(8,128)(2,1)S(1)}, u32[]{:S(2)}, u32[]{:S(2)}) collective-permute-start(bf16[1040,128]{1,0:T(8,128)(2,1)S(1)} %get-tuple-element.34.own_ref), channel_id=1, source_target_pairs={{0,224},{1,0},{2,1},{3,2},{4,3},{5,4},{6,5},{7,6},{15,7},{14,15},{... | collective-permute-start | bytes 798728 | tf_op jit(solution)/shard_map/ppermute | solution.py:518
  35.8 6.4 %collective-permute-start.1 = (bf16[1040,128]{1,0:T(8,128)(2,1)S(1)}, bf16[1040,128]{1,0:T(8,128)(2,1)S(1)}, u32[]{:S(2)}, u32[]{:S(2)}) collective-permute-start(bf16[1040,128]{1,0:T(8,128)(2,1)S(1)} %get-tuple-element.34.own_ref), channel_id=1, source_target_pairs={{224,0},{0,1},{1,2},{2,3},{3,4},{4,5},{5,6},{6,7},{7,15},{15,14},{... | collective-permute-start | bytes 798728 | tf_op jit(solution)/shard_map/ppermute | solution.py:517
  37.9 0.7 copy-start.7
  38.5 0.7 copy-start.6
  47.1 5.3 %collective-permute-start.3 = (bf16[768,128]{1,0:T(8,128)(2,1)S(1)}, bf16[768,128]{1,0:T(8,128)(2,1)S(1)}, u32[]{:S(2)}, u32[]{:S(2)}) collective-permute-start(bf16[768,128]{1,0:T(8,128)(2,1)S(1)} %get-tuple-element.40), channel_id=1, source_target_pairs={{224,0},{0,1},{1,2},{2,3},{3,4},{4,5},{5,6},{6,7},{7,15},{15,14},{... | collective-permute-start | bytes 589832 | tf_op jit(solution)/shard_map/ppermute | solution.py:529
  49.2 5.7 %collective-permute-start.4 = (bf16[768,128]{1,0:T(8,128)(2,1)S(1)}, bf16[768,128]{1,0:T(8,128)(2,1)S(1)}, u32[]{:S(2)}, u32[]{:S(2)}) collective-permute-start(bf16[768,128]{1,0:T(8,128)(2,1)S(1)} %get-tuple-element.41), channel_id=1, source_target_pairs={{0,224},{1,0},{2,1},{3,2},{4,3},{5,4},{6,5},{7,6},{15,7},{14,15},{... | collective-permute-start | bytes 589832 | tf_op jit(solution)/shard_map/ppermute | solution.py:530
  58.2 19.9 %copy-start = (f32[8,64,2,128]{3,2,1,0:T(2,128)S(1)}, f32[8,64,2,128]{3,2,1,0:T(2,128)}, u32[]{:S(2)}) copy-start(f32[8,64,2,128]{3,2,1,0:T(2,128)} %param.9) | copy-start | bytes 1572868
  58.2 19.9 %copy-start.3 = (s32[8,2,128]{2,1,0:T(2,128)S(1)}, s32[8,2,128]{2,1,0:T(2,128)}, u32[]{:S(2)}) copy-start(s32[8,2,128]{2,1,0:T(2,128)} %param.11) | copy-start | bytes 24580

commit v7 on v6

--- a/solution.py
+++ b/solution.py
@@ -93,7 +93,8 @@
 
 
 def spread_kernel(spec_ref, got_ref, fu_ref, fp_ref, mask_ref, send_ref, rows_ref):
-    theta_inv = 1.0 / (jnp.full((1, LANES), spec_ref[1] + spec_ref[0], f32) / 2.0)
+    theta = (spec_ref[:, 1:2] + spec_ref[:, 0:1]) / 2.0
+    theta_inv = 1.0 / jnp.broadcast_to(theta, (1, LANES))
     for half in range(2):
         for b in range(BLOCKS):
             for x in range(XL):
@@ -179,7 +180,7 @@
 
 def sweep(k, mode, begin, last, refs, old, new):
     unroll = UNROLL[mode]
-    coef_ref, lm_ref, table_ref, mask_ref, state = refs
+    coef_ref, table_ref, mask_ref, state = refs
     count = {"wide": 3, "own": 1}.get(mode, 2)
     lanes = block(LOW if mode == "wide" else OWN, count)
     inner = block(0, min(count, 2))
@@ -189,7 +190,7 @@
     def group(g, carry):
         for z in layers_of(g, unroll):
             z64 = pl.multiple_of(z * BU, BU)
-            table = table_ref[lm_ref[z]]
+            table = table_ref[z]
             stack = jnp.concatenate(stack_of(z64, old, mode), axis=0)
             product = jnp.dot(table[:, : 7 * BU], stack, preferred_element_type=f32)
             rows = pl.ds(z64, BU)
@@ -302,12 +303,12 @@
     return high, (v - high.astype(f32)).astype(bf16)
 
 
-def couple(get, lm_ref, coup_ref, mask_ref, rest_ref, sign, q_ref):
+def couple(get, coup_ref, mask_ref, rest_ref, sign, q_ref):
     def group(g, carry):
         for z in layers_of(g, NZ):
             here = pl.ds(pl.multiple_of(z * PB, PB), PB)
             du = get(pl.multiple_of(z * BU, BU))
-            q = jnp.dot(coup_ref[lm_ref[z]], jnp.concatenate(thirds(du), axis=0),
+            q = jnp.dot(coup_ref[z], jnp.concatenate(thirds(du), axis=0),
                         preferred_element_type=f32)
             q_ref[here, :] = q * mask_ref[z, pl.ds(0, 1), block(OWN)] + sign * rest_ref[here, :]
         return carry
@@ -320,8 +321,8 @@
                    preferred_element_type=f32)
 
 
-def prep_kernel(spec_ref, off_ref, kb_ref, coup_ref, sinv_ref,
-                coef_ref, table_ref, pair_ref, band_ref):
+def prep_kernel(spec_ref, off_ref, lm_ref, kb_ref, coup_ref, sinv_ref,
+                coef_ref, table_ref, pair_ref, band_ref, kinds_ref, pairs_ref):
     lower = jnp.full((1, WIDTH), spec_ref[0], f32)
     upper = jnp.full((1, WIDTH), spec_ref[1], f32)
     theta = (upper + lower) / 2.0
@@ -337,11 +338,14 @@
         rho = rho_next
     for m in range(4):
         high, low = halves(coup_ref[m])
-        pair_ref[m] = jnp.concatenate([high, high, low], axis=1)
+        pairs_ref[m] = jnp.concatenate([high, high, low], axis=1)
         high, low = halves(coup_ref[m].T)
         blocks = [kb_ref[m, d] for d in (3, 4, 5, 6, 1, 0, 2)]
         pad = jnp.zeros((BU, PB), bf16)
-        table_ref[m] = jnp.concatenate(blocks + [high, high, low, pad], axis=1)
+        kinds_ref[m] = jnp.concatenate(blocks + [high, high, low, pad], axis=1)
+    for z in range(NZ):
+        table_ref[z] = kinds_ref[lm_ref[z]]
+        pair_ref[z] = pairs_ref[lm_ref[z]]
     row = lax.broadcasted_iota(jnp.int32, (PB, RP), 0)
     col = lax.broadcasted_iota(jnp.int32, (PB, RP), 1)
     spread = (col % PB == row).astype(f32).astype(bf16)
@@ -357,13 +361,13 @@
     band_ref[...] = jnp.concatenate([high, high, low], axis=1)
 
 
-def first_kernel(lm_ref, coef_ref, table_ref, coup_ref, schur_ref,
+def first_kernel(coef_ref, table_ref, coup_ref, schur_ref,
                  fu_ref, fp_ref, mask_ref, own_ref, low_ref, high_ref,
                  ru_ref, du_ref, dp_ref, q_ref, send_ref, up_ref, down_ref,
                  wide_ref, d_ref, r_ref, s_ref, wa_ref, wb_ref):
     widen(wide_ref, mask_ref, low_ref, high_ref)
     pad_in((wa_ref, wb_ref), low_ref, high_ref, own_ref, False)
-    refs = (coef_ref, lm_ref, table_ref, wide_ref, (r_ref, d_ref, s_ref))
+    refs = (coef_ref, table_ref, wide_ref, (r_ref, d_ref, s_ref))
     begin = starter(coef_ref, fu_ref, wa_ref, True)
 
     def last(z64, s):
@@ -373,7 +377,7 @@
     sweep(0, "wide", begin, None, refs, wa_ref, wb_ref)
     sweep(1, "shrink", None, None, refs, wb_ref, wa_ref)
     sweep(2, "ring", None, last, refs, wa_ref, wb_ref)
-    couple(lambda z64: du_ref[pl.ds(z64, BU), :], lm_ref, coup_ref, wide_ref, fp_ref, -1.0, q_ref)
+    couple(lambda z64: du_ref[pl.ds(z64, BU), :], coup_ref, wide_ref, fp_ref, -1.0, q_ref)
     dp_ref[...] = bands(schur_ref, q_ref)
     theta_inv = coef_ref[pl.ds(0, 1), block(0)]
 
@@ -385,7 +389,7 @@
             dp = dp_ref[here, :] * weight
             dp_ref[here, :] = dp
             stack = stack_of(z64, wb_ref, "own") + thirds(dp)
-            product = jnp.dot(table_ref[lm_ref[z]][:, : 7 * BU + 3 * PB],
+            product = jnp.dot(table_ref[z][:, : 7 * BU + 3 * PB],
                               jnp.concatenate(stack, axis=0), preferred_element_type=f32)
             rows = pl.ds(z64, BU)
             ru = fu_ref[rows, :] - product * weight
@@ -406,13 +410,13 @@
         )
 
 
-def second_kernel(lm_ref, coef_ref, table_ref, coup_ref, schur_ref,
+def second_kernel(coef_ref, table_ref, coup_ref, schur_ref,
                   fu_ref, mask_ref, ru_ref, du_ref, dp_ref, q_ref, own_ref, low_ref,
                   high_ref, mlow_ref, mhigh_ref, out_ref,
                   wide_ref, d_ref, r_ref, s_ref, wa_ref, wb_ref, p_ref, rows_ref, sort_ref):
     widen(wide_ref, mask_ref, mlow_ref, mhigh_ref)
     pad_in((wa_ref, wb_ref), low_ref, high_ref, own_ref, True)
-    refs = (coef_ref, lm_ref, table_ref, wide_ref, (r_ref, d_ref, s_ref))
+    refs = (coef_ref, table_ref, wide_ref, (r_ref, d_ref, s_ref))
     begin = starter(coef_ref, ru_ref, wa_ref, False)
     own = block(0)
 
@@ -422,7 +426,7 @@
     sweep(0, "shrink", begin, None, refs, wa_ref, wb_ref)
     sweep(1, "ring", None, None, refs, wb_ref, wa_ref)
     sweep(2, "own", None, last, refs, wa_ref, wb_ref)
-    couple(lambda z64: s_ref[pl.ds(z64, BU), own], lm_ref, coup_ref, wide_ref, q_ref, 1.0, p_ref)
+    couple(lambda z64: s_ref[pl.ds(z64, BU), own], coup_ref, wide_ref, q_ref, 1.0, p_ref)
     p_ref[...] = bands(schur_ref, p_ref)
     for half in range(2):
         for b in range(BLOCKS):
@@ -504,15 +508,16 @@
     )
     got = lax.all_to_all(packed, PLANE, 0, 0, tiled=True)
     fu, fp, mask, send = call(
-        spread_kernel, [spectrum], [got.reshape(CH * BLOCKS * 8, LANES)],
+        spread_kernel, [], [spectrum.reshape(1, 2), got.reshape(CH * BLOCKS * 8, LANES)],
         [((RU, LANES), f32), ((RP, LANES), f32), ((NZ, LANES), f32), ((RU + NZ, LANES), bf16)],
         [((BLOCKS, LANES, LANES), f32)],
     )
     send, spectrum = lax.optimization_barrier((send, spectrum))
     coefs, table, pair, matrix = call(
-        prep_kernel, [spectrum, band_offsets], [kblocks, bcoup, sinv],
-        [((8, WIDTH), f32), ((4, BU, 8 * BU), bf16), ((4, PB, 3 * BU), bf16),
-         ((RP, 3 * RP), bf16)], [],
+        prep_kernel, [spectrum, band_offsets, layers], [kblocks, bcoup, sinv],
+        [((8, WIDTH), f32), ((NZ, BU, 8 * BU), bf16), ((NZ, PB, 3 * BU), bf16),
+         ((RP, 3 * RP), bf16)],
+        [((4, BU, 8 * BU), bf16), ((4, PB, 3 * BU), bf16)],
     )
     low = lax.ppermute(send, ALL, up)
     high = lax.ppermute(send, ALL, down)
@@ -520,7 +525,7 @@
         ((RU + 2 * BU, WIDTH), bf16)
     ] * 2
     ru, du, dp, q, send2, up2, down2 = call(
-        first_kernel, [layers],
+        first_kernel, [],
         [coefs, table, pair, matrix, fu, fp, mask, send, low, high],
         [((RU, LANES), f32), ((RU, LANES), f32), ((RP, LANES), f32), ((RP, LANES), f32),
          ((RU, LANES), bf16), ((PACKED * BU, LANES), bf16), ((PACKED * BU, LANES), bf16)],
@@ -529,7 +534,7 @@
     low2 = lax.ppermute(up2, ALL, up)
     high2 = lax.ppermute(down2, ALL, down)
     (back,) = call(
-        second_kernel, [layers],
+        second_kernel, [],
         [coefs, table, pair, matrix, fu, mask, ru, du, dp, q, send2, low2, high2, low, high],
         [((CH * BLOCKS * 8, LANES), bf16)],
         wide + [((RP, LANES), f32), ((BLOCKS, LANES, LANES), f32),

time: 79.9 us -> 78.9 us (0.987)
  Pallas kernels: 13.2 us -> 12.2 us
    pallas_call x5, Pallas kernels: 11.6 us -> 10.6 us  [call(): pl.pallas_call(kernel, out_shape=[jax.ShapeDtypeStruct(*o) for o in outs]...]
where the time goes in v7:
time: 78.9 us; the launch traced here: 78.2 us
  blocking collectives  50.2 us (64%)
  Pallas kernels  12.2 us (15%)
  waiting for transfers between devices  7.57 us (10%)
  starting transfers between devices  6.2 us (8%)
  local copies, waits for them, and re-layouts  1.25 us (2%)
    all_to_all x1, blocking collectives, body(): got = lax.all_to_all(packed, PLANE, 0, 0, tiled=True)  30.3 us
    all_to_all x1, blocking collectives, body(): lax.all_to_all(back.reshape(CH * BLOCKS, 8, LANES), PLANE, 0, 0, tiled=True)  19.9 us
    pallas_call x5, Pallas kernels, call(): pl.pallas_call(kernel, out_shape=[jax.ShapeDtypeStruct(*o) for o in outs]...  10.6 us
    ppermute x1, waiting for transfers between devices, body(): low2 = lax.ppermute(up2, ALL, up)  3.19 us
    ppermute x1, waiting for transfers between devices, body(): high2 = lax.ppermute(down2, ALL, down)  2.48 us
    ppermute x1, starting transfers between devices, body(): low2 = lax.ppermute(up2, ALL, up)  2.1 us
    ppermute x1, starting transfers between devices, body(): low = lax.ppermute(send, ALL, up)  2.01 us
    ppermute x1, starting transfers between devices, body(): other = lax.ppermute(layer_mats, 'gz', [(0, 1), (1, 0)])  2 us
  transfers between devices with their start and end apart: 5, of which 4 were waited for; matrix products, arithmetic and copies ran while one was open for 0% of the time, Pallas kernels for 4%

profile of v7, /device:TPU:16, one launch (start us, length us, event | category | flops | bytes accessed | tf_op | source)
XLA Modules:
  0.0 78.2 jit_solution(15466106909543161630)
XLA Ops:
  0.6 2.0 %collective-permute-start = (s32[8]{0:T(128)}, s32[8]{0:T(128)S(1)}, u32[]{:S(2)}, u32[]{:S(2)}) collective-permute-start(s32[8]{0:T(128)} %param.12), channel_id=1, source_target_pairs={{0,1},{1,0},{2,3},{3,2},{4,5},{5,4},{6,7},{7,6},{8,9},{9,8},{10,11... | collective-permute-start | bytes 104 | tf_op jit(solution)/shard_map/ppermute | solution.py:488
  2.6 1.6 %shard_map.104 = f32[160,8,128]{2,1,0:T(8,128)S(1)} custom-call(f32[1024,128]{1,0:T(8,128)} %bitcast.9, f32[256,128]{1,0:T(8,128)} %bitcast.15, s32[16,128]{1,0:T(8,128)} %bitcast.12), custom_call_target="tpu_custom_call" | custom-call | tf_op jit(solution)/shard_map/pallas_call | solution.py:492
  4.2 0.0 copy-start.1
  4.2 0.2 collective-permute-done
  4.4 0.0 copy-start.5
  4.4 30.3 %all_to_all.10 = f32[160,8,128]{2,1,0:T(8,128)S(1)} all-to-all(f32[160,8,128]{2,1,0:T(8,128)S(1)} %shard_map.104), channel_id=1, replica_groups=mesh['gx'=8,'gy'=16,'gz'=2] {'gy','gz'}, dimensions={0} | all-to-all | bytes 1310720 | tf_op jit(solution)/shard_map/all_to_all | solution.py:509
  34.8 0.0 copy-start.2
  34.8 0.0 copy-done.5
  34.8 0.5 shard_map.105
  35.3 0.1 collective-permute-start.2
  35.4 2.0 %collective-permute-start.1 = (bf16[1040,128]{1,0:T(8,128)(2,1)S(1)}, bf16[1040,128]{1,0:T(8,128)(2,1)S(1)}, u32[]{:S(2)}, u32[]{:S(2)}) collective-permute-start(bf16[1040,128]{1,0:T(8,128)(2,1)S(1)} %get-tuple-element.34.own_ref), channel_id=1, source_target_pairs={{224,0},{0,1},{1,2},{2,3},{3,4},{4,5},{5,6},{6,7},{7,15},{15,14},{... | collective-permute-start | bytes 798728 | tf_op jit(solution)/shard_map/ppermute | solution.py:522
  37.4 0.7 copy-done.7
  38.0 0.1 broadcast_select_fusion.lm_ref
  38.1 0.0 copy-done.1
  38.1 0.0 copy-done.2
  38.1 0.0 copy-done.4
  38.1 0.6 copy-done.6
  38.7 1.3 %shard_map.106 = (f32[8,512]{1,0:T(8,128)S(1)}, bf16[16,64,512]{2,1,0:T(8,128)(2,1)S(1)}, bf16[16,16,192]{2,1,0:T(8,128)(2,1)S(1)}, bf16[256,768]{1,0:T(8,128)(2,1)S(1)}) custom-call(f32[2]{0:T(128)S(1)} %copy-done.5, s32[8]{0:T(128)S(1)} %copy-done.6, s32[16]{0:T(128)S(1)} %broadcast_select_fusion.lm_ref, bf16[4,7,64,64]{3,2,1,0:T(8,128)(2,1)S(1)} %copy-done.2, ...), custom_call_target="tpu_custom_call" | custom-call | tf_op jit(solution)/shard_map/pallas_call | solution.py:476
  40.0 1.7 %collective-permute-done.2.high_ref.mhigh_ref = bf16[1040,128]{1,0:T(8,128)(2,1)S(1)} collective-permute-done((bf16[1040,128]{1,0:T(8,128)(2,1)S(1)}, bf16[1040,128]{1,0:T(8,128)(2,1)S(1)}, u32[]{:S(2)}, u32[]{:S(2)}) %collective-permute-start.2) | collective-permute-done | bytes 266272 | tf_op jit(solution)/shard_map/ppermute | solution.py:523
  41.8 0.0 collective-permute-done.1.low_ref.mlow_ref
  41.8 4.4 %shard_map.107 = (f32[1024,128]{1,0:T(8,128)S(1)}, f32[1024,128]{1,0:T(8,128)S(1)}, f32[256,128]{1,0:T(8,128)S(1)}, f32[256,128]{1,0:T(8,128)S(1)}, bf16[1024,12...) custom-call(f32[8,512]{1,0:T(8,128)S(1)} %get-tuple-element.27.coef_ref, ...), custom_call_target="tpu_custom_call" | custom-call | tf_op jit(solution)/shard_map/pallas_call | solution.py:476
  46.2 2.1 %collective-permute-start.3 = (bf16[768,128]{1,0:T(8,128)(2,1)S(1)}, bf16[768,128]{1,0:T(8,128)(2,1)S(1)}, u32[]{:S(2)}, u32[]{:S(2)}) collective-permute-start(bf16[768,128]{1,0:T(8,128)(2,1)S(1)} %get-tuple-element.40), channel_id=1, source_target_pairs={{224,0},{0,1},{1,2},{2,3},{3,4},{4,5},{5,6},{6,7},{7,15},{15,14},{... | collective-permute-start | bytes 589832 | tf_op jit(solution)/shard_map/ppermute | solution.py:534
  48.3 0.0 collective-permute-start.4
  48.3 3.2 %collective-permute-done.3.low_ref = bf16[768,128]{1,0:T(8,128)(2,1)S(1)} collective-permute-done((bf16[768,128]{1,0:T(8,128)(2,1)S(1)}, bf16[768,128]{1,0:T(8,128)(2,1)S(1)}, u32[]{:S(2)}, u32[]{:S(2)}) %collective-permute-start.3) | collective-permute-done | bytes 196640 | tf_op jit(solution)/shard_map/ppermute | solution.py:534
  51.5 2.5 %collective-permute-done.4.high_ref = bf16[768,128]{1,0:T(8,128)(2,1)S(1)} collective-permute-done((bf16[768,128]{1,0:T(8,128)(2,1)S(1)}, bf16[768,128]{1,0:T(8,128)(2,1)S(1)}, u32[]{:S(2)}, u32[]{:S(2)}) %collective-permute-start.4) | collective-permute-done | bytes 196640 | tf_op jit(solution)/shard_map/ppermute | solution.py:535
  54.0 3.2 %shard_map.108 = bf16[1280,128]{1,0:T(8,128)(2,1)S(1)} custom-call(f32[8,512]{1,0:T(8,128)S(1)} %get-tuple-element.27.coef_ref, bf16[16,64,512]{2,1,0:T(8,128)(2,1)S(1)} %get-tuple-element.28.table_ref, bf16[16,16,192]{2,1,0:T(8,128)(2,1)S(1)} %get-tuple-element.29.coup_ref, bf16[256,768]{1,0:T(8,128)(2,1)S(1)} %get-tuple-element.30.schur_ref, ...), custom_call_target="tpu_custom_call" | custom-call | tf_op jit(solution)/shard_map/pallas_call | solution.py:476
  57.2 0.0 copy-start
  57.2 0.0 copy-start.3
  57.2 19.9 %all_to_all.11.got_ref = bf16[160,8,128]{2,1,0:T(8,128)(2,1)S(1)} all-to-all(bf16[160,8,128]{2,1,0:T(8,128)(2,1)S(1)} %bitcast.11), channel_id=1, replica_groups=mesh['gx'=8,'gy'=16,'gz'=2] {'gy','gz'}, dimensions={0} | all-to-all | bytes 655360 | tf_op jit(solution)/shard_map/all_to_all | solution.py:543
  77.1 0.0 copy-done
  77.1 0.0 copy-done.3
  77.1 1.1 %shard_map.109 = (f32[1024,128]{1,0:T(8,128)}, f32[256,128]{1,0:T(8,128)}) custom-call(bf16[160,8,128]{2,1,0:T(8,128)(2,1)S(1)} %all_to_all.11.got_ref, f32[1024,128]{1,0:T(8,128)S(1)} %bitcast.10, s32[16,128]{1,0:T(8,128)S(1)} %bitcast.13), custom_call_target="tpu_custom_call" | custom-call | tf_op jit(solution)/shard_map/pallas_call | solution.py:476
  (3 shorter events, 0.0 us)
Async XLA Ops:
  0.6 3.8 %collective-permute-start = (s32[8]{0:T(128)}, s32[8]{0:T(128)S(1)}, u32[]{:S(2)}, u32[]{:S(2)}) collective-permute-start(s32[8]{0:T(128)} %param.12), channel_id=1, source_target_pairs={{0,1},{1,0},{2,3},{3,2},{4,5},{5,4},{6,7},{7,6},{8,9},{9,8},{10,11... | collective-permute-start | bytes 104 | tf_op jit(solution)/shard_map/ppermute | solution.py:488
  4.2 33.9 %copy-start.1 = (f32[8,16,16,16]{3,2,1,0:T(8,128)S(1)}, f32[8,16,16,16]{3,2,1,0:T(8,128)}, u32[]{:S(2)}) copy-start(f32[8,16,16,16]{3,2,1,0:T(8,128)} %sinv_ref.1) | copy-start | bytes 393220
  4.4 30.3 %copy-start.5 = (f32[2]{0:T(128)S(1)}, f32[2]{0:T(128)}, u32[]{:S(2)}) copy-start(f32[2]{0:T(128)} %spec_ref) | copy-start | bytes 28
  34.8 3.4 %copy-start.2 = (bf16[4,7,64,64]{3,2,1,0:T(8,128)(2,1)S(1)}, bf16[4,7,64,64]{3,2,1,0:T(8,128)(2,1)}, u32[]{:S(2)}) copy-start(bf16[4,7,64,64]{3,2,1,0:T(8,128)(2,1)} %kb_ref.1) | copy-start | bytes 688132
  34.8 3.4 %copy-start.4 = (f32[4,16,64]{2,1,0:T(8,128)S(1)}, f32[4,16,64]{2,1,0:T(8,128)}, u32[]{:S(2)}) copy-start(f32[4,16,64]{2,1,0:T(8,128)} %coup_ref.1) | copy-start | bytes 49156
  35.3 6.5 %collective-permute-start.2 = (bf16[1040,128]{1,0:T(8,128)(2,1)S(1)}, bf16[1040,128]{1,0:T(8,128)(2,1)S(1)}, u32[]{:S(2)}, u32[]{:S(2)}) collective-permute-start(bf16[1040,128]{1,0:T(8,128)(2,1)S(1)} %get-tuple-element.34.own_ref), channel_id=1, source_target_pairs={{0,224},{1,0},{2,1},{3,2},{4,3},{5,4},{6,5},{7,6},{15,7},{14,15},{... | collective-permute-start | bytes 798728 | tf_op jit(solution)/shard_map/ppermute | solution.py:523
  35.4 6.4 %collective-permute-start.1 = (bf16[1040,128]{1,0:T(8,128)(2,1)S(1)}, bf16[1040,128]{1,0:T(8,128)(2,1)S(1)}, u32[]{:S(2)}, u32[]{:S(2)}) collective-permute-start(bf16[1040,128]{1,0:T(8,128)(2,1)S(1)} %get-tuple-element.34.own_ref), channel_id=1, source_target_pairs={{224,0},{0,1},{1,2},{2,3},{3,4},{4,5},{5,6},{6,7},{7,15},{15,14},{... | collective-permute-start | bytes 798728 | tf_op jit(solution)/shard_map/ppermute | solution.py:522
  37.4 0.7 copy-start.7
  38.0 0.7 copy-start.6
  46.2 5.3 %collective-permute-start.3 = (bf16[768,128]{1,0:T(8,128)(2,1)S(1)}, bf16[768,128]{1,0:T(8,128)(2,1)S(1)}, u32[]{:S(2)}, u32[]{:S(2)}) collective-permute-start(bf16[768,128]{1,0:T(8,128)(2,1)S(1)} %get-tuple-element.40), channel_id=1, source_target_pairs={{224,0},{0,1},{1,2},{2,3},{3,4},{4,5},{5,6},{6,7},{7,15},{15,14},{... | collective-permute-start | bytes 589832 | tf_op jit(solution)/shard_map/ppermute | solution.py:534
  48.3 5.7 %collective-permute-start.4 = (bf16[768,128]{1,0:T(8,128)(2,1)S(1)}, bf16[768,128]{1,0:T(8,128)(2,1)S(1)}, u32[]{:S(2)}, u32[]{:S(2)}) collective-permute-start(bf16[768,128]{1,0:T(8,128)(2,1)S(1)} %get-tuple-element.41), channel_id=1, source_target_pairs={{0,224},{1,0},{2,1},{3,2},{4,3},{5,4},{6,5},{7,6},{15,7},{14,15},{... | collective-permute-start | bytes 589832 | tf_op jit(solution)/shard_map/ppermute | solution.py:535
  57.2 19.9 %copy-start = (f32[8,64,2,128]{3,2,1,0:T(2,128)S(1)}, f32[8,64,2,128]{3,2,1,0:T(2,128)}, u32[]{:S(2)}) copy-start(f32[8,64,2,128]{3,2,1,0:T(2,128)} %param.9) | copy-start | bytes 1572868
  57.2 19.9 %copy-start.3 = (s32[8,2,128]{2,1,0:T(2,128)S(1)}, s32[8,2,128]{2,1,0:T(2,128)}, u32[]{:S(2)}) copy-start(s32[8,2,128]{2,1,0:T(2,128)} %param.11) | copy-start | bytes 24580

commit v8 on v7

--- a/solution.py
+++ b/solution.py
@@ -363,8 +363,8 @@
 
 def first_kernel(coef_ref, table_ref, coup_ref, schur_ref,
                  fu_ref, fp_ref, mask_ref, own_ref, low_ref, high_ref,
-                 ru_ref, du_ref, dp_ref, q_ref, send_ref, up_ref, down_ref,
-                 wide_ref, d_ref, r_ref, s_ref, wa_ref, wb_ref):
+                 ru_ref, du_ref, dp_ref, q_ref, send_ref, up_ref, down_ref, wide_ref,
+                 d_ref, r_ref, s_ref, wa_ref, wb_ref):
     widen(wide_ref, mask_ref, low_ref, high_ref)
     pad_in((wa_ref, wb_ref), low_ref, high_ref, own_ref, False)
     refs = (coef_ref, table_ref, wide_ref, (r_ref, d_ref, s_ref))
@@ -411,10 +411,9 @@
 
 
 def second_kernel(coef_ref, table_ref, coup_ref, schur_ref,
-                  fu_ref, mask_ref, ru_ref, du_ref, dp_ref, q_ref, own_ref, low_ref,
-                  high_ref, mlow_ref, mhigh_ref, out_ref,
-                  wide_ref, d_ref, r_ref, s_ref, wa_ref, wb_ref, p_ref, rows_ref, sort_ref):
-    widen(wide_ref, mask_ref, mlow_ref, mhigh_ref)
+                  fu_ref, wide_ref, ru_ref, du_ref, dp_ref, q_ref, own_ref, low_ref,
+                  high_ref, out_ref,
+                  d_ref, r_ref, s_ref, wa_ref, wb_ref, p_ref, rows_ref, sort_ref):
     pad_in((wa_ref, wb_ref), low_ref, high_ref, own_ref, True)
     refs = (coef_ref, table_ref, wide_ref, (r_ref, d_ref, s_ref))
     begin = starter(coef_ref, ru_ref, wa_ref, False)
@@ -437,7 +436,7 @@
                 pressure = []
                 for z in range(half * ZL, half * ZL + ZL):
                     here = pl.ds(z * PB, PB)
-                    dp = p_ref[here, :] * mask_ref[pl.ds(z, 1), :]
+                    dp = p_ref[here, :] * wide_ref[z, pl.ds(0, 1), block(OWN)]
                     pressure.append(dp + dp_ref[here, :])
                 flat = jnp.concatenate(pressure, axis=0)
             rows_ref[b] = flat.T
@@ -521,21 +520,22 @@
     )
     low = lax.ppermute(send, ALL, up)
     high = lax.ppermute(send, ALL, down)
-    wide = [((NZ, 8, WIDTH), f32)] + [((RU, 2 * LANES), f32)] * 3 + [
+    wide = [((RU, 2 * LANES), f32)] * 3 + [
         ((RU + 2 * BU, WIDTH), bf16)
     ] * 2
-    ru, du, dp, q, send2, up2, down2 = call(
+    ru, du, dp, q, send2, up2, down2, live = call(
         first_kernel, [],
         [coefs, table, pair, matrix, fu, fp, mask, send, low, high],
         [((RU, LANES), f32), ((RU, LANES), f32), ((RP, LANES), f32), ((RP, LANES), f32),
-         ((RU, LANES), bf16), ((PACKED * BU, LANES), bf16), ((PACKED * BU, LANES), bf16)],
+         ((RU, LANES), bf16), ((PACKED * BU, LANES), bf16), ((PACKED * BU, LANES), bf16),
+         ((NZ, 8, WIDTH), f32)],
         wide,
     )
     low2 = lax.ppermute(up2, ALL, up)
     high2 = lax.ppermute(down2, ALL, down)
     (back,) = call(
         second_kernel, [],
-        [coefs, table, pair, matrix, fu, mask, ru, du, dp, q, send2, low2, high2, low, high],
+        [coefs, table, pair, matrix, fu, live, ru, du, dp, q, send2, low2, high2],
         [((CH * BLOCKS * 8, LANES), bf16)],
         wide + [((RP, LANES), f32), ((BLOCKS, LANES, LANES), f32),
                 ((CH * BLOCKS * 8, LANES), f32)],

time: 78.9 us -> 78.6 us (level)
  no operation moved by 1% of the time
where the time goes in v8:
time: 78.6 us; the launch traced here: 77.9 us
  blocking collectives  50.2 us (64%)
  Pallas kernels  11.8 us (15%)
  waiting for transfers between devices  7.61 us (10%)
  starting transfers between devices  6.21 us (8%)
  local copies, waits for them, and re-layouts  1.25 us (2%)
    all_to_all x1, blocking collectives, body(): got = lax.all_to_all(packed, PLANE, 0, 0, tiled=True)  30.3 us
    all_to_all x1, blocking collectives, body(): lax.all_to_all(back.reshape(CH * BLOCKS, 8, LANES), PLANE, 0, 0, tiled=True)  19.9 us
    pallas_call x5, Pallas kernels, call(): pl.pallas_call(kernel, out_shape=[jax.ShapeDtypeStruct(*o) for o in outs]...  10.2 us
    ppermute x1, waiting for transfers between devices, body(): low2 = lax.ppermute(up2, ALL, up)  3.19 us
    ppermute x1, waiting for transfers between devices, body(): high2 = lax.ppermute(down2, ALL, down)  2.48 us
    ppermute x1, starting transfers between devices, body(): low2 = lax.ppermute(up2, ALL, up)  2.1 us
    ppermute x1, starting transfers between devices, body(): low = lax.ppermute(send, ALL, up)  2.01 us
    ppermute x1, starting transfers between devices, body(): other = lax.ppermute(layer_mats, 'gz', [(0, 1), (1, 0)])  2 us
  transfers between devices with their start and end apart: 5, of which 4 were waited for; matrix products, arithmetic and copies ran while one was open for 0% of the time, Pallas kernels for 4%

profile of v8, /device:TPU:16, one launch (start us, length us, event | category | flops | bytes accessed | tf_op | source)
XLA Modules:
  0.0 77.9 jit_solution(12677338772061823006)
XLA Ops:
  0.6 2.0 %collective-permute-start = (s32[8]{0:T(128)}, s32[8]{0:T(128)S(1)}, u32[]{:S(2)}, u32[]{:S(2)}) collective-permute-start(s32[8]{0:T(128)} %param.12), channel_id=1, source_target_pairs={{0,1},{1,0},{2,3},{3,2},{4,5},{5,4},{6,7},{7,6},{8,9},{9,8},{10,11... | collective-permute-start | bytes 104 | tf_op jit(solution)/shard_map/ppermute | solution.py:487
  2.6 1.6 %shard_map.104 = f32[160,8,128]{2,1,0:T(8,128)S(1)} custom-call(f32[1024,128]{1,0:T(8,128)} %bitcast.9, f32[256,128]{1,0:T(8,128)} %bitcast.15, s32[16,128]{1,0:T(8,128)} %bitcast.12), custom_call_target="tpu_custom_call" | custom-call | tf_op jit(solution)/shard_map/pallas_call | solution.py:491
  4.2 0.0 copy-start.1
  4.2 0.2 collective-permute-done
  4.4 0.0 copy-start.5
  4.4 30.3 %all_to_all.10 = f32[160,8,128]{2,1,0:T(8,128)S(1)} all-to-all(f32[160,8,128]{2,1,0:T(8,128)S(1)} %shard_map.104), channel_id=1, replica_groups=mesh['gx'=8,'gy'=16,'gz'=2] {'gy','gz'}, dimensions={0} | all-to-all | bytes 1310720 | tf_op jit(solution)/shard_map/all_to_all | solution.py:508
  34.8 0.0 copy-start.2
  34.8 0.0 copy-done.5
  34.8 0.5 shard_map.105
  35.3 0.1 collective-permute-start.2
  35.4 2.0 %collective-permute-start.1 = (bf16[1040,128]{1,0:T(8,128)(2,1)S(1)}, bf16[1040,128]{1,0:T(8,128)(2,1)S(1)}, u32[]{:S(2)}, u32[]{:S(2)}) collective-permute-start(bf16[1040,128]{1,0:T(8,128)(2,1)S(1)} %get-tuple-element.35.own_ref), channel_id=1, source_target_pairs={{224,0},{0,1},{1,2},{2,3},{3,4},{4,5},{5,6},{6,7},{7,15},{15,14},{... | collective-permute-start | bytes 798728 | tf_op jit(solution)/shard_map/ppermute | solution.py:521
  37.4 0.7 copy-done.7
  38.0 0.1 broadcast_select_fusion.lm_ref
  38.1 0.0 copy-done.1
  38.1 0.0 copy-done.2
  38.1 0.0 copy-done.4
  38.1 0.6 copy-done.6
  38.7 1.3 %shard_map.106 = (f32[8,512]{1,0:T(8,128)S(1)}, bf16[16,64,512]{2,1,0:T(8,128)(2,1)S(1)}, bf16[16,16,192]{2,1,0:T(8,128)(2,1)S(1)}, bf16[256,768]{1,0:T(8,128)(2,1)S(1)}) custom-call(f32[2]{0:T(128)S(1)} %copy-done.5, s32[8]{0:T(128)S(1)} %copy-done.6, s32[16]{0:T(128)S(1)} %broadcast_select_fusion.lm_ref, bf16[4,7,64,64]{3,2,1,0:T(8,128)(2,1)S(1)} %copy-done.2, ...), custom_call_target="tpu_custom_call" | custom-call | tf_op jit(solution)/shard_map/pallas_call | solution.py:475
  40.0 1.8 %collective-permute-done.2.high_ref = bf16[1040,128]{1,0:T(8,128)(2,1)S(1)} collective-permute-done((bf16[1040,128]{1,0:T(8,128)(2,1)S(1)}, bf16[1040,128]{1,0:T(8,128)(2,1)S(1)}, u32[]{:S(2)}, u32[]{:S(2)}) %collective-permute-start.2) | collective-permute-done | bytes 266272 | tf_op jit(solution)/shard_map/ppermute | solution.py:522
  41.8 0.0 collective-permute-done.1.low_ref
  41.8 4.4 %shard_map.107 = (f32[1024,128]{1,0:T(8,128)S(1)}, f32[1024,128]{1,0:T(8,128)S(1)}, f32[256,128]{1,0:T(8,128)S(1)}, f32[256,128]{1,0:T(8,128)S(1)}, bf16[1024,12...) custom-call(f32[8,512]{1,0:T(8,128)S(1)} %get-tuple-element.28.coef_, ...), custom_call_target="tpu_custom_call" | custom-call | tf_op jit(solution)/shard_map/pallas_call | solution.py:475
  46.2 2.1 %collective-permute-start.3 = (bf16[768,128]{1,0:T(8,128)(2,1)S(1)}, bf16[768,128]{1,0:T(8,128)(2,1)S(1)}, u32[]{:S(2)}, u32[]{:S(2)}) collective-permute-start(bf16[768,128]{1,0:T(8,128)(2,1)S(1)} %get-tuple-element.42), channel_id=1, source_target_pairs={{224,0},{0,1},{1,2},{2,3},{3,4},{4,5},{5,6},{6,7},{7,15},{15,14},{... | collective-permute-start | bytes 589832 | tf_op jit(solution)/shard_map/ppermute | solution.py:534
  48.3 0.0 collective-permute-start.4
  48.3 3.2 %collective-permute-done.3.low_ref = bf16[768,128]{1,0:T(8,128)(2,1)S(1)} collective-permute-done((bf16[768,128]{1,0:T(8,128)(2,1)S(1)}, bf16[768,128]{1,0:T(8,128)(2,1)S(1)}, u32[]{:S(2)}, u32[]{:S(2)}) %collective-permute-start.3) | collective-permute-done | bytes 196640 | tf_op jit(solution)/shard_map/ppermute | solution.py:534
  51.5 2.5 %collective-permute-done.4.high_ref = bf16[768,128]{1,0:T(8,128)(2,1)S(1)} collective-permute-done((bf16[768,128]{1,0:T(8,128)(2,1)S(1)}, bf16[768,128]{1,0:T(8,128)(2,1)S(1)}, u32[]{:S(2)}, u32[]{:S(2)}) %collective-permute-start.4) | collective-permute-done | bytes 196640 | tf_op jit(solution)/shard_map/ppermute | solution.py:535
  54.0 2.9 %shard_map.108 = bf16[1280,128]{1,0:T(8,128)(2,1)S(1)} custom-call(f32[8,512]{1,0:T(8,128)S(1)} %get-tuple-element.28.coef_ref, bf16[16,64,512]{2,1,0:T(8,128)(2,1)S(1)} %get-tuple-element.29.table_ref, bf16[16,16,192]{2,1,0:T(8,128)(2,1)S(1)} %get-tuple-element.30.coup_ref, bf16[256,768]{1,0:T(8,128)(2,1)S(1)} %get-tuple-element.31.schur_ref, ...), custom_call_target="tpu_custom_call" | custom-call | tf_op jit(solution)/shard_map/pallas_call | solution.py:475
  56.9 0.0 copy-start
  56.9 0.0 copy-start.3
  56.9 19.9 %all_to_all.11.got_ref = bf16[160,8,128]{2,1,0:T(8,128)(2,1)S(1)} all-to-all(bf16[160,8,128]{2,1,0:T(8,128)(2,1)S(1)} %bitcast.11), channel_id=1, replica_groups=mesh['gx'=8,'gy'=16,'gz'=2] {'gy','gz'}, dimensions={0} | all-to-all | bytes 655360 | tf_op jit(solution)/shard_map/all_to_all | solution.py:543
  76.8 0.0 copy-done
  76.8 0.0 copy-done.3
  76.8 1.1 %shard_map.109 = (f32[1024,128]{1,0:T(8,128)}, f32[256,128]{1,0:T(8,128)}) custom-call(bf16[160,8,128]{2,1,0:T(8,128)(2,1)S(1)} %all_to_all.11.got_ref, f32[1024,128]{1,0:T(8,128)S(1)} %bitcast.10, s32[16,128]{1,0:T(8,128)S(1)} %bitcast.13), custom_call_target="tpu_custom_call" | custom-call | tf_op jit(solution)/shard_map/pallas_call | solution.py:475
  (3 shorter events, 0.0 us)
Async XLA Ops:
  0.6 3.8 %collective-permute-start = (s32[8]{0:T(128)}, s32[8]{0:T(128)S(1)}, u32[]{:S(2)}, u32[]{:S(2)}) collective-permute-start(s32[8]{0:T(128)} %param.12), channel_id=1, source_target_pairs={{0,1},{1,0},{2,3},{3,2},{4,5},{5,4},{6,7},{7,6},{8,9},{9,8},{10,11... | collective-permute-start | bytes 104 | tf_op jit(solution)/shard_map/ppermute | solution.py:487
  4.2 33.9 %copy-start.1 = (f32[8,16,16,16]{3,2,1,0:T(8,128)S(1)}, f32[8,16,16,16]{3,2,1,0:T(8,128)}, u32[]{:S(2)}) copy-start(f32[8,16,16,16]{3,2,1,0:T(8,128)} %sinv_ref.1) | copy-start | bytes 393220
  4.4 30.3 %copy-start.5 = (f32[2]{0:T(128)S(1)}, f32[2]{0:T(128)}, u32[]{:S(2)}) copy-start(f32[2]{0:T(128)} %spec_ref) | copy-start | bytes 28
  34.8 3.4 %copy-start.2 = (bf16[4,7,64,64]{3,2,1,0:T(8,128)(2,1)S(1)}, bf16[4,7,64,64]{3,2,1,0:T(8,128)(2,1)}, u32[]{:S(2)}) copy-start(bf16[4,7,64,64]{3,2,1,0:T(8,128)(2,1)} %kb_ref.1) | copy-start | bytes 688132
  34.8 3.4 %copy-start.4 = (f32[4,16,64]{2,1,0:T(8,128)S(1)}, f32[4,16,64]{2,1,0:T(8,128)}, u32[]{:S(2)}) copy-start(f32[4,16,64]{2,1,0:T(8,128)} %coup_ref.1) | copy-start | bytes 49156
  35.3 6.5 %collective-permute-start.2 = (bf16[1040,128]{1,0:T(8,128)(2,1)S(1)}, bf16[1040,128]{1,0:T(8,128)(2,1)S(1)}, u32[]{:S(2)}, u32[]{:S(2)}) collective-permute-start(bf16[1040,128]{1,0:T(8,128)(2,1)S(1)} %get-tuple-element.35.own_ref), channel_id=1, source_target_pairs={{0,224},{1,0},{2,1},{3,2},{4,3},{5,4},{6,5},{7,6},{15,7},{14,15},{... | collective-permute-start | bytes 798728 | tf_op jit(solution)/shard_map/ppermute | solution.py:522
  35.4 6.4 %collective-permute-start.1 = (bf16[1040,128]{1,0:T(8,128)(2,1)S(1)}, bf16[1040,128]{1,0:T(8,128)(2,1)S(1)}, u32[]{:S(2)}, u32[]{:S(2)}) collective-permute-start(bf16[1040,128]{1,0:T(8,128)(2,1)S(1)} %get-tuple-element.35.own_ref), channel_id=1, source_target_pairs={{224,0},{0,1},{1,2},{2,3},{3,4},{4,5},{5,6},{6,7},{7,15},{15,14},{... | collective-permute-start | bytes 798728 | tf_op jit(solution)/shard_map/ppermute | solution.py:521
  37.4 0.7 copy-start.7
  38.0 0.7 copy-start.6
  46.2 5.3 %collective-permute-start.3 = (bf16[768,128]{1,0:T(8,128)(2,1)S(1)}, bf16[768,128]{1,0:T(8,128)(2,1)S(1)}, u32[]{:S(2)}, u32[]{:S(2)}) collective-permute-start(bf16[768,128]{1,0:T(8,128)(2,1)S(1)} %get-tuple-element.42), channel_id=1, source_target_pairs={{224,0},{0,1},{1,2},{2,3},{3,4},{4,5},{5,6},{6,7},{7,15},{15,14},{... | collective-permute-start | bytes 589832 | tf_op jit(solution)/shard_map/ppermute | solution.py:534
  48.3 5.7 %collective-permute-start.4 = (bf16[768,128]{1,0:T(8,128)(2,1)S(1)}, bf16[768,128]{1,0:T(8,128)(2,1)S(1)}, u32[]{:S(2)}, u32[]{:S(2)}) collective-permute-start(bf16[768,128]{1,0:T(8,128)(2,1)S(1)} %get-tuple-element.43), channel_id=1, source_target_pairs={{0,224},{1,0},{2,1},{3,2},{4,3},{5,4},{6,5},{7,6},{15,7},{14,15},{... | collective-permute-start | bytes 589832 | tf_op jit(solution)/shard_map/ppermute | solution.py:535
  56.9 19.9 %copy-start = (f32[8,64,2,128]{3,2,1,0:T(2,128)S(1)}, f32[8,64,2,128]{3,2,1,0:T(2,128)}, u32[]{:S(2)}) copy-start(f32[8,64,2,128]{3,2,1,0:T(2,128)} %param.9) | copy-start | bytes 1572868
  56.9 19.9 %copy-start.3 = (s32[8,2,128]{2,1,0:T(2,128)S(1)}, s32[8,2,128]{2,1,0:T(2,128)}, u32[]{:S(2)}) copy-start(s32[8,2,128]{2,1,0:T(2,128)} %param.11) | copy-start | bytes 24580
